TPU v7x, 32 devices: a whole 2x2x4 slice. The times are simulated.
32 devices in a mesh: ctx: 4 (over z), fsdp: 8 (over y, x, core).
Axes of the slice: x: 2, y: 2, z: 4, core: 2. Of those that a mesh axis runs over, the one named last changes fastest.
Arguments:
- tokens: bfloat16 [8, 1024, 2048], P('fsdp', 'ctx'), may hold values from -6 to 6
- attn_gain: bfloat16 [2048], P('fsdp'), may hold values from 0.25 to 1.75
- w_query: bfloat16 [2048, 2048], P('fsdp'), may hold values from -1.2374369 to 1.2374369
- w_key: bfloat16 [2048, 256], P('fsdp'), may hold values from -0.13258252 to 0.13258252
- w_value: bfloat16 [2048, 256], P('fsdp'), may hold values from -0.125 to 0.125
- w_out: bfloat16 [2048, 2048], P('fsdp'), may hold values from -1.5 to 1.5
- ffn_gain: bfloat16 [2048], P('fsdp'), may hold values from 0.25 to 1.75
- w_gate: bfloat16 [2048, 5632], P('fsdp'), may hold values from -0.125 to 0.125
- w_up: bfloat16 [2048, 5632], P('fsdp'), may hold values from -0.125 to 0.125
- w_down: bfloat16 [5632, 2048], P('fsdp'), may hold values from -0.078125 to 0.078125
- block_table: int32 [4, 2], replicated, may hold values from 0 to 7, as said below
- positions: int32 [8, 1024], P('fsdp', 'ctx'), may hold values from 0 to 5118, as said below
- out_grad: bfloat16 [8, 1024, 2048], P('fsdp', 'ctx'), may hold values from -6 to 6
Outputs:
- layer_out: bfloat16 [8, 1024, 2048], P('fsdp', 'ctx')
- tokens_grad: float32 [8, 1024, 2048], P('fsdp', 'ctx')
- attn_gain_grad: float32 [2048], P('fsdp')
- w_query_grad: float32 [2048, 2048], P('fsdp')
- w_key_grad: float32 [2048, 256], P('fsdp')
- w_value_grad: float32 [2048, 256], P('fsdp')
- w_out_grad: float32 [2048, 2048], P('fsdp')
- ffn_gain_grad: float32 [2048], P('fsdp')
- w_gate_grad: float32 [2048, 5632], P('fsdp')
- w_up_grad: float32 [2048, 5632], P('fsdp')
- w_down_grad: float32 [5632, 2048], P('fsdp')
Inputs may be any that keep to these rules, and one draw needn't show every extreme that they name: `block_table`: row c holds a block p and its mirror 8 - 1 - p; every block of 0 to 7 stands once in the table. positions[s, r] is an offset of sequence s plus idx of stored row r, so positions rise by one along a sequence.
All inputs are finite; a program needn't handle non-finite values.
Results may differ from a plain program's by a relative error of at most 0.014.
Values may be sent and summed in bfloat16 or wider, within the bound.
A program may use at most 512 MiB of HBM per device.

v0:
```python
import jax
import jax.numpy as jnp
from jax import lax
from jax.sharding import PartitionSpec as P

HEADS = 32
KV_HEADS = 4
HEAD_DIM = 64


EPS = 1e-05
THETA = 10000.0


def rope_tables(positions):
    half_dim = HEAD_DIM // 2
    frequency = THETA ** (-jnp.arange(half_dim, dtype=jnp.float32) * (2.0 / HEAD_DIM))
    angle = positions.astype(jnp.float32)[:, None] * frequency[None, :]
    return (jnp.cos(angle)[:, None, :], jnp.sin(angle)[:, None, :])


def rotate(values, cosine, sine):
    half_dim = HEAD_DIM // 2
    first = values[..., :half_dim]
    second = values[..., half_dim:]
    return jnp.concatenate(
        [first * cosine - second * sine, second * cosine + first * sine], axis=-1
    )


def unrotate(grads, cosine, sine):
    half_dim = HEAD_DIM // 2
    first = grads[..., :half_dim]
    second = grads[..., half_dim:]
    return jnp.concatenate(
        [first * cosine + second * sine, second * cosine - first * sine], axis=-1
    )


def contract_rows(left, right):
    return lax.dot_general(
        left, right, (((0,), (0,)), ((), ())), preferred_element_type=jnp.float32
    )


def times_transpose(left, right):
    return lax.dot_general(
        left, right, (((1,), (1,)), ((), ())), preferred_element_type=jnp.float32
    )


def shards(
    tokens,
    attn_gain,
    w_query,
    w_key,
    w_value,
    w_out,
    ffn_gain,
    w_gate,
    w_up,
    w_down,
    block_table,
    positions,
    out_grad,
):
    inputs = tokens[0].astype(jnp.float32)
    cotangent = out_grad[0].astype(jnp.float32)
    local_rows = inputs.shape[0]
    model_width = inputs.shape[1]
    hidden_width = w_gate.shape[1]
    group_size = HEADS // KV_HEADS
    query_width = HEADS * HEAD_DIM
    key_width = KV_HEADS * HEAD_DIM
    score_scale = HEAD_DIM ** (-0.5)
    cosine, sine = rope_tables(positions[0])
    block_rows = local_rows // 2
    seq_index = (
        block_table[:, :, None] * block_rows
        + jnp.arange(block_rows, dtype=jnp.int32)[None, None, :]
    ).reshape(-1)
    own_index = lax.dynamic_slice_in_dim(seq_index, lax.axis_index("ctx") * local_rows, local_rows)
    allowed = seq_index[None, :] <= own_index[:, None]
    inverse_one = lax.rsqrt(jnp.mean(inputs * inputs, axis=1, keepdims=True) + EPS)
    unit_one = inputs * inverse_one
    gain_piece = lax.all_gather(attn_gain, "fsdp", axis=0, tiled=True)
    query_piece = lax.all_gather(w_query, "fsdp", axis=0, tiled=True)
    key_piece = lax.all_gather(w_key, "fsdp", axis=0, tiled=True)
    value_piece = lax.all_gather(w_value, "fsdp", axis=0, tiled=True)
    out_piece = lax.all_gather(w_out, "fsdp", axis=0, tiled=True)
    columns = (unit_one * gain_piece.astype(jnp.float32)[None, :]).astype(jnp.bfloat16)
    query_sum = jnp.dot(columns, query_piece, preferred_element_type=jnp.float32)
    key_sum = jnp.dot(columns, key_piece, preferred_element_type=jnp.float32)
    value_sum = jnp.dot(columns, value_piece, preferred_element_type=jnp.float32)
    normed = columns
    out_full = out_piece
    query_sum, key_sum, value_sum, normed_one, out_full = (
        query_sum,
        key_sum,
        value_sum,
        normed,
        out_full,
    )
    queries_low = rotate(query_sum.reshape(local_rows, HEADS, HEAD_DIM), cosine, sine).astype(
        jnp.bfloat16
    )
    keys_low = (
        rotate(key_sum.reshape(local_rows, KV_HEADS, HEAD_DIM), cosine, sine)
        .reshape(local_rows, key_width)
        .astype(jnp.bfloat16)
    )
    values_low = value_sum.astype(jnp.bfloat16)
    keys_all, values_all = (
        lax.all_gather(keys_low, "ctx", axis=0, tiled=True),
        lax.all_gather(values_low, "ctx", axis=0, tiled=True),
    )
    seq_length = keys_all.shape[0]
    query_heads = queries_low.reshape(local_rows, KV_HEADS, group_size, HEAD_DIM).transpose(
        1, 2, 0, 3
    )
    key_heads = keys_all.reshape(seq_length, KV_HEADS, HEAD_DIM).transpose(1, 0, 2)
    value_heads = values_all.reshape(seq_length, KV_HEADS, HEAD_DIM).transpose(1, 0, 2)

    def scores_of(query_one, key_block):
        raw = times_transpose(query_one, key_block) * score_scale
        return jnp.where(allowed, raw, -1e30)

    def head_forward(operands):
        query_block, key_block, value_block = operands

        def single(query_one):
            scores = scores_of(query_one, key_block)
            highest = jnp.max(scores, axis=-1, keepdims=True)
            weights = jnp.exp(scores - highest)
            totals = jnp.sum(weights, axis=-1, keepdims=True)
            softmaxed = (weights / totals).astype(jnp.bfloat16)
            mixed = jnp.dot(softmaxed, value_block, preferred_element_type=jnp.float32)
            return (mixed, highest[:, 0] + jnp.log(totals[:, 0]))

        return lax.map(single, query_block)

    mixed_heads, log_totals = lax.map(head_forward, (query_heads, key_heads, value_heads))
    attended = (
        mixed_heads.transpose(2, 0, 1, 3).reshape(local_rows, query_width).astype(jnp.bfloat16)
    )
    hidden_one = inputs + jnp.dot(attended, out_full, preferred_element_type=jnp.float32)
    inverse_two = lax.rsqrt(jnp.mean(hidden_one * hidden_one, axis=1, keepdims=True) + EPS)
    unit_two = hidden_one * inverse_two
    gain_piece = lax.all_gather(ffn_gain, "fsdp", axis=0, tiled=True)
    gate_piece = lax.all_gather(w_gate, "fsdp", axis=0, tiled=True)
    up_piece = lax.all_gather(w_up, "fsdp", axis=0, tiled=True)
    columns = (unit_two * gain_piece.astype(jnp.float32)[None, :]).astype(jnp.bfloat16)
    gate_sum = jnp.dot(columns, gate_piece, preferred_element_type=jnp.float32)
    up_sum = jnp.dot(columns, up_piece, preferred_element_type=jnp.float32)
    sigmoid_gate = jax.nn.sigmoid(gate_sum)
    silu_gate = gate_sum * sigmoid_gate
    activated = (silu_gate * up_sum).astype(jnp.bfloat16)
    branch_out = jnp.dot(
        activated,
        lax.all_gather(w_down, "fsdp", axis=0, tiled=True),
        preferred_element_type=jnp.float32,
    )
    layer_out = (hidden_one + branch_out).astype(jnp.bfloat16)
    grad_branch = cotangent.astype(jnp.bfloat16)
    grad_activated = times_transpose(
        grad_branch, lax.all_gather(w_down, "fsdp", axis=0, tiled=True)
    )
    grad_gate = (
        grad_activated * up_sum * sigmoid_gate * (1.0 + gate_sum * (1.0 - sigmoid_gate))
    ).astype(jnp.bfloat16)
    grad_up = (grad_activated * silu_gate).astype(jnp.bfloat16)
    gain_piece = lax.all_gather(ffn_gain, "fsdp", axis=0, tiled=True)
    gate_piece = lax.all_gather(w_gate, "fsdp", axis=0, tiled=True)
    up_piece = lax.all_gather(w_up, "fsdp", axis=0, tiled=True)
    grad_cols = times_transpose(grad_gate, gate_piece) + times_transpose(grad_up, up_piece)
    gain_grad = jnp.sum(grad_cols * unit_two, axis=0)
    grad_unit = grad_cols * gain_piece.astype(jnp.float32)[None, :]
    grad_unit_two = grad_unit
    gain_grad_two = gain_grad
    grad_gate_up = jnp.concatenate([grad_gate, grad_up], axis=1)
    down_shard = lax.psum_scatter(
        contract_rows(activated, grad_branch), "fsdp", scatter_dimension=0, tiled=True
    )
    gate_up_shard = lax.psum_scatter(
        contract_rows(columns, grad_gate_up), "fsdp", scatter_dimension=0, tiled=True
    )
    grad_hidden = cotangent + inverse_two * (
        grad_unit_two - unit_two * jnp.mean(grad_unit_two * unit_two, axis=1, keepdims=True)
    )
    grad_attn_low = grad_hidden.astype(jnp.bfloat16)
    grad_attended = times_transpose(
        grad_attn_low, lax.all_gather(w_out, "fsdp", axis=0, tiled=True)
    ).astype(jnp.bfloat16)
    out_term = contract_rows(attended, grad_attn_low)
    grad_heads = grad_attended.reshape(local_rows, KV_HEADS, group_size, HEAD_DIM).transpose(
        1, 2, 0, 3
    )

    def head_backward(operands):
        query_block, key_block, value_block, grad_block, log_block = operands

        def single(carry, items):
            key_total, value_total = carry
            query_one, grad_one, log_one = items
            scores = scores_of(query_one, key_block)
            softmaxed = jnp.exp(scores - log_one[:, None])
            grad_probs = times_transpose(grad_one, value_block)
            inner = jnp.sum(softmaxed * grad_probs, axis=-1, keepdims=True)
            grad_scores = (softmaxed * (grad_probs - inner)).astype(jnp.bfloat16)
            grad_query = (
                jnp.dot(grad_scores, key_block, preferred_element_type=jnp.float32) * score_scale
            )
            key_total = key_total + contract_rows(grad_scores, query_one) * score_scale
            value_total = value_total + contract_rows(softmaxed.astype(jnp.bfloat16), grad_one)
            return ((key_total, value_total), grad_query)

        start_totals = (
            jnp.zeros((seq_length, HEAD_DIM), jnp.float32),
            jnp.zeros((seq_length, HEAD_DIM), jnp.float32),
        )
        (key_total, value_total), grad_query = lax.scan(
            single, start_totals, (query_block, grad_block, log_block)
        )
        return (grad_query, key_total, value_total)

    grad_query_heads, grad_key_heads, grad_value_heads = lax.map(
        head_backward, (query_heads, key_heads, value_heads, grad_heads, log_totals)
    )
    grad_keys_all = grad_key_heads.transpose(1, 0, 2).reshape(seq_length, key_width)
    grad_values_all = grad_value_heads.transpose(1, 0, 2).reshape(seq_length, key_width)
    own_key_grad, own_value_grad = (
        lax.psum_scatter(grad_keys_all, "ctx", scatter_dimension=0, tiled=True),
        lax.psum_scatter(grad_values_all, "ctx", scatter_dimension=0, tiled=True),
    )
    grad_key_low = (
        unrotate(own_key_grad.reshape(local_rows, KV_HEADS, HEAD_DIM), cosine, sine)
        .reshape(local_rows, key_width)
        .astype(jnp.bfloat16)
    )
    grad_value_low = own_value_grad.astype(jnp.bfloat16)
    grad_query_rows = grad_query_heads.transpose(2, 0, 1, 3).reshape(local_rows, HEADS, HEAD_DIM)
    grad_query_low = (
        unrotate(grad_query_rows, cosine, sine)
        .reshape(local_rows, query_width)
        .astype(jnp.bfloat16)
    )
    gain_piece = lax.all_gather(attn_gain, "fsdp", axis=0, tiled=True)
    query_piece = lax.all_gather(w_query, "fsdp", axis=0, tiled=True)
    key_piece = lax.all_gather(w_key, "fsdp", axis=0, tiled=True)
    value_piece = lax.all_gather(w_value, "fsdp", axis=0, tiled=True)
    grad_cols = (
        times_transpose(grad_query_low, query_piece)
        + times_transpose(grad_key_low, key_piece)
        + times_transpose(grad_value_low, value_piece)
    )
    gain_grad = jnp.sum(grad_cols * unit_one, axis=0)
    grad_unit = grad_cols * gain_piece.astype(jnp.float32)[None, :]
    tokens_grad = grad_hidden + inverse_one * (
        grad_unit - unit_one * jnp.mean(grad_unit * unit_one, axis=1, keepdims=True)
    )
    query_term = contract_rows(normed_one, grad_query_low)
    key_term = contract_rows(normed_one, grad_key_low)
    value_term = contract_rows(normed_one, grad_value_low)
    gain_one_shard, gain_two_shard, query_shard, key_shard, value_shard, out_shard = (
        lax.psum_scatter(gain_grad, "fsdp", scatter_dimension=0, tiled=True),
        lax.psum_scatter(gain_grad_two, "fsdp", scatter_dimension=0, tiled=True),
        lax.psum_scatter(query_term, "fsdp", scatter_dimension=0, tiled=True),
        lax.psum_scatter(key_term, "fsdp", scatter_dimension=0, tiled=True),
        lax.psum_scatter(value_term, "fsdp", scatter_dimension=0, tiled=True),
        lax.psum_scatter(out_term, "fsdp", scatter_dimension=0, tiled=True),
    )
    gate_shard = gate_up_shard[:, :hidden_width]
    up_shard = gate_up_shard[:, hidden_width:]
    summed = lax.psum(
        (
            gain_one_shard,
            query_shard,
            key_shard,
            value_shard,
            out_shard,
            gain_two_shard,
            gate_shard,
            up_shard,
            down_shard,
        ),
        "ctx",
    )
    return (
        layer_out.reshape(1, local_rows, model_width),
        tokens_grad.reshape(1, local_rows, model_width),
        summed[0],
        summed[1],
        summed[2],
        summed[3],
        summed[4],
        summed[5],
        summed[6],
        summed[7],
        summed[8],
    )


def solution(mesh):
    return jax.shard_map(
        shards,
        mesh=mesh,
        in_specs=(
            P("fsdp", "ctx", None),
            P("fsdp"),
            P("fsdp", None),
            P("fsdp", None),
            P("fsdp", None),
            P("fsdp", None),
            P("fsdp"),
            P("fsdp", None),
            P("fsdp", None),
            P("fsdp", None),
            P(),
            P("fsdp", "ctx"),
            P("fsdp", "ctx", None),
        ),
        out_specs=(
            P("fsdp", "ctx", None),
            P("fsdp", "ctx", None),
            P("fsdp"),
            P("fsdp", None),
            P("fsdp", None),
            P("fsdp", None),
            P("fsdp", None),
            P("fsdp"),
            P("fsdp", None),
            P("fsdp", None),
            P("fsdp", None),
        ),
        check_vma=False,
    )
```

profile of v0, /device:TPU:0, one launch (start us, length us, event | category | flops | bytes accessed | tf_op | source)
XLA Modules:
  0.0 3205.1 jit_solution(12606878503554546676)
XLA Ops:
  13.1 10.4 all-gather
  24.0 8.9 all-gather.1
  38.3 16.1 all_gather.45
  54.8 6.8 all-gather.14.cloned.1.call-done
  63.3 16.4 all_gather.47
  81.2 36.7 %all-gather.10.cloned.1.call-done = bf16[2048,2048]{1,0:T(8,128)(2,1)} async-done(((bf16[256,2048]{1,0:T(8,128)(2,1)}), bf16[2048,2048]{1,0:T(8,128)(2,1)}) %all-gather.10.cloned.1.call-update) | async-done | bytes 8388624 | tf_op jit(solution)/shard_map/all_gather | solution.py:87
  117.9 12.3 copy.43
  130.3 5.8 fusion.60
  139.9 4.7 maximum_bitcast_fusion
  144.6 60.9 %while.64 = (s32[]{:T(128)}, bf16[4,8,256,64]{2,3,1,0:T(8,128)(2,1)}, f32[4,8,256]{2,1,0:T(8,128)S(1)}, bf16[4,8,256,64]{3,2,1,0:T(8,128)(2,1)}, bf16[4,1024,64]...) while((s32[]{:T(128)}, ...), condition=%wide.region_6.7_spmd.clone.clone, body=%wide.region_1.6_spmd.clone.sunk.clone | while | flops 69467904 | bytes 6454618 | solution.py:142
  147.6 11.5 while.63
  162.8 11.5 while.63
  178.0 11.6 while.63
  193.4 11.4 while.63
  206.5 6.2 multiply_reduce_fusion.3
  212.9 79.4 %all-gather.18.cloned.1.call-done = bf16[2048,5632]{1,0:T(8,128)(2,1)} async-done(((bf16[256,5632]{1,0:T(8,128)(2,1)}), bf16[2048,5632]{1,0:T(8,128)(2,1)}) %all-gather.18.cloned.1.call-update) | async-done | bytes 23068688 | tf_op jit(solution)/shard_map/all_gather | solution.py:150
  292.4 13.5 fusion.81
  305.8 104.8 %all-gather.20.cloned.1.call-done = bf16[2048,5632]{1,0:T(8,128)(2,1)} async-done(((bf16[256,5632]{1,0:T(8,128)(2,1)}), bf16[2048,5632]{1,0:T(8,128)(2,1)}) %all-gather.20.cloned.1.call-update) | async-done | bytes 23068688 | tf_op jit(solution)/shard_map/all_gather | solution.py:151
  410.6 14.1 fusion.82
  424.7 104.3 %all-gather.22.cloned.1.call-done = bf16[5632,2048]{1,0:T(8,128)(2,1)} async-done(((bf16[704,2048]{1,0:T(8,128)(2,1)}), bf16[5632,2048]{1,0:T(8,128)(2,1)}) %all-gather.22.cloned.1.call-update) | async-done | bytes 23068688 | tf_op jit(solution)/shard_map/all_gather | solution.py:160
  529.0 18.5 multiply_convert_fusion.1
  547.5 12.5 fusion.83
  560.0 14.0 multiply_reduce_fusion.1
  577.5 5.8 convolution_convert_fusion
  583.8 168.1 %while.66 = (s32[]{:T(128)}, f32[4,8,256,64]{2,3,1,0:T(8,128)}, f32[4,1024,64]{1,2,0:T(8,128)}, f32[4,1024,64]{1,2,0:T(8,128)}, bf16[4,8,256,64]{3,2,1,0:T(8,128...) while((s32[]{:T(128)}, f32[4,8,256,64]{2,3,1,0:T(8,128)}, ...), condition=%wide.region_13.14_spmd.clone.clone, body=%wide.region_9.13_spmd.clone.sunk.clone | while | flops 170737408 | bytes 22899168 | solution.py:226
  588.6 34.4 %while.65 = (s32[]{:T(128)}, f32[1024,64]{0,1:T(8,128)S(1)}, f32[1024,64]{0,1:T(8,128)S(1)}, f32[8,256,64]{1,2,0:T(8,128)}, bf16[8,256,64]{2,1,0:T(8,128)(2,1)},...) while((s32[]{:T(128)}, f32[1024,64]{0,1:T(8,128)S(1)}, ...), condition=%wide.region_12.12_spmd.clone, body=%wide.region_10.11_spmd.clone.sunk | while | flops 170475264 | bytes 10032288 | solution.py:221
  630.6 34.4 %while.65 = (s32[]{:T(128)}, f32[1024,64]{0,1:T(8,128)S(1)}, f32[1024,64]{0,1:T(8,128)S(1)}, f32[8,256,64]{1,2,0:T(8,128)}, bf16[8,256,64]{2,1,0:T(8,128)(2,1)},...) while((s32[]{:T(128)}, f32[1024,64]{0,1:T(8,128)S(1)}, ...), condition=%wide.region_12.12_spmd.clone, body=%wide.region_10.11_spmd.clone.sunk | while | flops 170475264 | bytes 10032288 | solution.py:221
  672.6 34.4 %while.65 = (s32[]{:T(128)}, f32[1024,64]{0,1:T(8,128)S(1)}, f32[1024,64]{0,1:T(8,128)S(1)}, f32[8,256,64]{1,2,0:T(8,128)}, bf16[8,256,64]{2,1,0:T(8,128)(2,1)},...) while((s32[]{:T(128)}, f32[1024,64]{0,1:T(8,128)S(1)}, ...), condition=%wide.region_12.12_spmd.clone, body=%wide.region_10.11_spmd.clone.sunk | while | flops 170475264 | bytes 10032288 | solution.py:221
  714.6 34.4 %while.65 = (s32[]{:T(128)}, f32[1024,64]{0,1:T(8,128)S(1)}, f32[1024,64]{0,1:T(8,128)S(1)}, f32[8,256,64]{1,2,0:T(8,128)}, bf16[8,256,64]{2,1,0:T(8,128)(2,1)},...) while((s32[]{:T(128)}, f32[1024,64]{0,1:T(8,128)S(1)}, ...), condition=%wide.region_12.12_spmd.clone, body=%wide.region_10.11_spmd.clone.sunk | while | flops 170475264 | bytes 10032288 | solution.py:221
  753.0 34.9 %fusion.30 = f32[2048,11264]{1,0:T(8,128)} fusion(bf16[256,2048]{1,0:T(8,128)(2,1)S(1)} %copy-done.14, bf16[256,5632]{1,0:T(8,128)(2,1)} %get-tuple-element.429, bf16[256,5632]{1,0:T(8,128)(2,1)} %get-tuple-element.430), kind=kOutput, calls=%fused_computation.55 | convolution fusion | flops 11822694400 | bytes 99090432 | tf_op jit(solution)/shard_map/dot_general | solution.py:41
  791.8 15.6 reduce-scatter.10.cloned.1.call-done
  812.0 9.2 fusion.64
  822.9 9.6 fusion.66
  832.5 21.7 fusion.54
  856.1 983.4 %all-reduce.9.cloned.1.call-done = f32[2048,11264]{1,0:T(8,128)} async-done(((f32[2048,11264]{1,0:T(8,128)}), f32[2048,11264]{1,0:T(8,128)}) %all-reduce.9.cloned.1.call-update) | async-done | bytes 92274704
  1839.5 10.4 fusion.80
  1850.0 35.5 %reduce-scatter.14.cloned.1.call-done = f32[256,256]{1,0:T(8,128)} async-done(((f32[2048,256]{1,0:T(8,128)}), f32[256,256]{1,0:T(8,128)}) %reduce-scatter.14.cloned.1.call-update) | async-done | bytes 262160 | tf_op jit(solution)/shard_map/reduce_scatter | solution.py:268
  1885.4 45.0 %reduce-scatter.16.cloned.1.call-done = f32[256,256]{1,0:T(8,128)} async-done(((f32[2048,256]{1,0:T(8,128)}), f32[256,256]{1,0:T(8,128)}) %reduce-scatter.16.cloned.1.call-update) | async-done | bytes 262160 | tf_op jit(solution)/shard_map/reduce_scatter | solution.py:269
  1930.4 119.9 %reduce-scatter.12.cloned.1.call-done = f32[256,2048]{1,0:T(8,128)} async-done(((f32[2048,2048]{1,0:T(8,128)}), f32[256,2048]{1,0:T(8,128)}) %reduce-scatter.12.cloned.1.call-update) | async-done | bytes 2097168 | tf_op jit(solution)/shard_map/reduce_scatter | solution.py:267
  2050.3 119.8 %reduce-scatter.18.cloned.1.call-done = f32[256,2048]{1,0:T(8,128)} async-done(((f32[2048,2048]{1,0:T(8,128)}), f32[256,2048]{1,0:T(8,128)}) %reduce-scatter.18.cloned.1.call-update) | async-done | bytes 2097168 | tf_op jit(solution)/shard_map/reduce_scatter | solution.py:270
  2170.1 268.2 %reduce-scatter.20.cloned.1.call-done = f32[704,2048]{1,0:T(8,128)} async-done(((f32[5632,2048]{1,0:T(8,128)}), f32[704,2048]{1,0:T(8,128)}) %reduce-scatter.20.cloned.1.call-update) | async-done | bytes 5767184 | tf_op jit(solution)/shard_map/reduce_scatter | solution.py:181
  2438.4 6.2 fusion.84
  2444.7 13.5 fusion.43
  2461.8 24.6 all-reduce.3
  2486.6 13.0 all-reduce.4
  2499.6 3.5 fusion.49
  2503.0 676.1 %all-reduce.11.cloned.1.call-done = (f32[256,2048]{1,0:T(8,128)}, f32[256,256]{1,0:T(8,128)}, f32[256,256]{1,0:T(8,128)}, f32[256,2048]{1,0:T(8,128)}, f32[256,5...) async-done(((f32[256,2048]{1,0:T(8,128)}, f32[256,256]{1,0:T(8,128)}, f32[256,256]{1,0:T(8,128)}, f32[256,2048]{1,0:T(8,128)}, f32[256,5632]{1,0:T(8,128)}, ...) | async-done | bytes 22020112 | tf_op jit(solution)/shard_map/psum | solution.py:274
  3179.2 3.3 copy.125
  (698 shorter events, 282.3 us)
Async XLA Ops:
  7.2 29.0 all-gather.12.cloned.1.call-start
  7.9 53.7 %all-gather.14.cloned.1.call-start = ((), (), s32[]{:S(2)}) async-start(), calls=%async_computation.9 | async-start | bytes 1179648 | tf_op jit(solution)/shard_map/all_gather | solution.py:89
  8.7 109.2 %all-gather.10.cloned.1.call-start = ((), (), s32[]{:S(2)}) async-start(), calls=%async_computation.7 | async-start | bytes 9437184 | tf_op jit(solution)/shard_map/all_gather | solution.py:87
  9.4 196.1 %all-gather.16.cloned.1.call-start = ((), (), s32[]{:S(2)}) async-start(), calls=%async_computation.10 | async-start | bytes 9437184 | tf_op jit(solution)/shard_map/all_gather | solution.py:90
  10.0 282.4 %all-gather.18.cloned.1.call-start = ((), (), s32[]{:S(2)}) async-start(), calls=%async_computation.11 | async-start | bytes 25952256 | tf_op jit(solution)/shard_map/all_gather | solution.py:150
  10.6 400.0 %all-gather.20.cloned.1.call-start = ((), (), s32[]{:S(2)}) async-start(), calls=%async_computation.12 | async-start | bytes 25952256 | tf_op jit(solution)/shard_map/all_gather | solution.py:151
  11.1 2.0 copy-start.33
  11.1 12.3 copy-start
  11.2 12.7 copy-start.31
  11.2 12.7 copy-start.32
  11.2 12.9 copy-start.34
  11.2 517.8 %all-gather.22.cloned.1.call-start = ((), (), s32[]{:S(2)}) async-start(), calls=%async_computation.13 | async-start | bytes 25952256 | tf_op jit(solution)/shard_map/all_gather | solution.py:160
  11.9 776.1 %reduce-scatter.8.cloned.1.call-start = ((), (), s32[]{:S(2)}) async-start(), calls=%async_computation.14 | async-start | bytes 1310720 | tf_op jit(solution)/shard_map/reduce_scatter | solution.py:232
  23.5 106.8 %copy-start.26 = (f32[8,1,256]{2,1,0:T(1,128)}, f32[8,1,256]{2,1,0:T(1,128)S(1)}, u32[]{:S(2)}) copy-start(f32[8,1,256]{2,1,0:T(1,128)S(1)} %convert_element_type.151) | copy-start | bytes 24580
  23.8 106.4 %copy-start.28 = (f32[256]{0:T(256)}, f32[256]{0:T(256)S(1)}, u32[]{:S(2)}) copy-start(f32[256]{0:T(256)S(1)} %add_rsqrt_fusion.1) | copy-start | bytes 3076
  33.1 103.0 %copy-start.22 = (f32[256,32]{0,1:T(8,128)}, f32[256,32]{0,1:T(8,128)S(1)}, u32[]{:S(2)}) copy-start(f32[256,32]{0,1:T(8,128)S(1)} %get-tuple-element.440) | copy-start | bytes 98308
  33.1 103.0 %copy-start.24 = (f32[256,32]{0,1:T(8,128)}, f32[256,32]{0,1:T(8,128)S(1)}, u32[]{:S(2)}) copy-start(f32[256,32]{0,1:T(8,128)S(1)} %get-tuple-element.441) | copy-start | bytes 98308
  212.6 361.3 %copy-start.4 = (f32[256,2048]{1,0:T(8,128)}, f32[256,2048]{1,0:T(8,128)S(1)}, u32[]{:S(2)}) copy-start(f32[256,2048]{1,0:T(8,128)S(1)} %get-tuple-element.443) | copy-start | bytes 6291460
  212.9 197.7 %copy-start.13 = (bf16[256,2048]{1,0:T(8,128)(2,1)}, bf16[256,2048]{1,0:T(8,128)(2,1)S(1)}, u32[]{:S(2)}) copy-start(bf16[256,2048]{1,0:T(8,128)(2,1)S(1)} %multiply_convert_fusion.4) | copy-start | bytes 3145732
  560.0 14.0 copy-start.17
  583.8 4.8 copy-start.10
  623.0 2.8 copy-start.11
  625.8 4.8 copy-start.10
  665.0 2.8 copy-start.11
  667.8 4.8 copy-start.10
  707.0 2.8 copy-start.11
  709.8 4.8 copy-start.10
  749.0 2.8 copy-start.11
  751.8 55.5 %reduce-scatter.10.cloned.1.call-start = ((), (), s32[]{:S(2)}) async-start(), calls=%async_computation.15 | async-start | bytes 1310720 | tf_op jit(solution)/shard_map/reduce_scatter | solution.py:233
  752.6 1087.0 %all-reduce.9.cloned.1.call-start = ((), (), s32[]{:S(2)}) async-start(), calls=%async_computation.21 | async-start | bytes 184549376
  788.0 1.8 copy-start.27
  788.0 1.8 copy-start.29
  788.0 1097.4 %reduce-scatter.14.cloned.1.call-start = ((), (), s32[]{:S(2)}) async-start(), calls=%async_computation.17 | async-start | bytes 2359296 | tf_op jit(solution)/shard_map/reduce_scatter | solution.py:268
  791.7 18.8 copy-start.18
  791.8 1138.6 %reduce-scatter.16.cloned.1.call-start = ((), (), s32[]{:S(2)}) async-start(), calls=%async_computation.18 | async-start | bytes 2359296 | tf_op jit(solution)/shard_map/reduce_scatter | solution.py:269
  810.3 1240.1 %reduce-scatter.12.cloned.1.call-start = ((), (), s32[]{:S(2)}) async-start(), calls=%async_computation.16 | async-start | bytes 18874368 | tf_op jit(solution)/shard_map/reduce_scatter | solution.py:267
  821.2 1349.0 %reduce-scatter.18.cloned.1.call-start = ((), (), s32[]{:S(2)}) async-start(), calls=%async_computation.19 | async-start | bytes 18874368 | tf_op jit(solution)/shard_map/reduce_scatter | solution.py:270
  832.4 1605.9 %reduce-scatter.20.cloned.1.call-start = ((), (), s32[]{:S(2)}) async-start(), calls=%async_computation.20 | async-start | bytes 51904512 | tf_op jit(solution)/shard_map/reduce_scatter | solution.py:181
  854.2 2324.9 %all-reduce.11.cloned.1.call-start = ((), (), s32[]{:S(2)}) async-start(), calls=%async_computation.22 | async-start | bytes 44040192 | tf_op jit(solution)/shard_map/psum | solution.py:274
  2438.4 6.3 copy-start.5
  2438.4 6.3 copy-start.12
  2444.7 13.5 copy-start.16
  2459.5 2.3 copy-start.30
  3179.2 7.0 copy-start.19
  3179.2 8.3 copy-start.9
  3187.5 4.7 copy-start.8
  3187.5 7.5 slice-start
  3192.2 3.6 slice-start.1
  (43 other events, 43.4 us)
Sparse Core Ops, SparseCore 0:
  9.9 26.2 all-gather.11
  38.1 23.4 all-gather.13
  63.5 54.3 all-gather.9
  119.6 54.3 all-gather.15
  175.8 116.4 all-gather.17
  294.1 116.4 all-gather.19
  412.5 116.4 all-gather.21
  752.0 27.1 reduce-scatter.7
  781.5 25.7 reduce-scatter.9
  811.0 1028.4 all-reduce.8
  1843.8 41.6 reduce-scatter.13
  1889.1 41.1 reduce-scatter.15
  1934.4 115.9 reduce-scatter.11
  2054.2 115.9 reduce-scatter.17
  2174.0 264.2 reduce-scatter.19
  2442.2 736.8 all-reduce.10
where the time goes:
time: 3210 us
  waiting for transfers between devices  2600 us (81%)
  matrix products  350 us (11%)
  local copies, waits for them, and re-layouts  110 us (3%)
  blocking collectives  89.2 us (3%)
  other arithmetic  33.1 us (1%)
    unnamed x17, waiting for transfers between devices  989 us
    psum x1, waiting for transfers between devices, shards(): lax.psum((gain_one_shard, query_shard, key_shard, value_shard, out_shard,...  676 us
    reduce_scatter x1, waiting for transfers between devices, shards(): lax.psum_scatter(contract_rows(activated, grad_branch), 'fsdp', scatter_d...  268 us
    dot_general x103, matrix products, times_transpose(): lax.dot_general(left, right, (((1,), (1,)), ((), ())), preferred_element_...  128 us
    dot_general x70, matrix products, contract_rows(): lax.dot_general(left, right, (((0,), (0,)), ((), ())), preferred_element_...  124 us
    reduce_scatter x1, waiting for transfers between devices, shards(): lax.psum_scatter(query_term, 'fsdp', scatter_dimension=0, tiled=True)  120 us
    reduce_scatter x1, waiting for transfers between devices, shards(): lax.psum_scatter(out_term, 'fsdp', scatter_dimension=0, tiled=True)  120 us
    all_gather x1, waiting for transfers between devices, shards(): up_piece = lax.all_gather(w_up, 'fsdp', axis=0, tiled=True)  105 us
  transfers between devices with their start and end apart: 16, of which 14 were waited for; matrix products, arithmetic and copies ran while one was open for 7% of the time, Pallas kernels for 0%

commit v1 on v0

v1 whole, which is shorter than its diff:
```python
import functools

import jax
import jax.numpy as jnp
from jax import lax
from jax.experimental import pallas as pl
from jax.experimental.pallas import tpu as pltpu
from jax.sharding import PartitionSpec as P

HEADS = 32
KV_HEADS = 4
HEAD_DIM = 64
GROUP = HEADS // KV_HEADS
PAIRS = GROUP // 2
LANES = 2 * HEAD_DIM
STACK = PAIRS * LANES

EPS = 1e-05
THETA = 10000.0
NEG = -1e30
FLIGHT = 2
BF = jnp.bfloat16
F32 = jnp.float32


def dot(left, right, contract, out=F32):
    return lax.dot_general(
        left, right, ((contract[:1], contract[1:]), ((), ())), preferred_element_type=out
    )


def swap_halves(z):
    lane = lax.broadcasted_iota(jnp.int32, z.shape, 1)
    first = (lane % HEAD_DIM) < (HEAD_DIM // 2)
    return jnp.where(
        first,
        pltpu.roll(z, LANES - HEAD_DIM // 2, 1),
        pltpu.roll(z, HEAD_DIM // 2, 1),
    )


def split_heads(rows):
    lane = lax.broadcasted_iota(jnp.int32, rows.shape, 1)
    zero = jnp.zeros_like(rows)
    return jnp.concatenate(
        [jnp.where(lane < HEAD_DIM, rows, zero), jnp.where(lane >= HEAD_DIM, rows, zero)], axis=0
    )


def join_heads(columns):
    half = columns.shape[1] // 2
    sub = lax.broadcasted_iota(jnp.int32, (LANES, half), 0)
    return jnp.where(sub < HEAD_DIM, columns[:, :half], columns[:, half:]).T


def stack_pairs(ref, rows):
    return jnp.concatenate([ref[rows, p * LANES : (p + 1) * LANES] for p in range(PAIRS)], axis=0)


def two_blocks(ref, table, j, block):
    parts = [
        ref[pl.ds(pl.multiple_of(table[2 + 2 * j + i] * block, block), block), :] for i in range(2)
    ]
    return jnp.concatenate(parts, axis=0)


def causal(scores, j, own, block):
    key = lax.broadcasted_iota(jnp.int32, scores.shape, 0) + j * (2 * block)
    query = lax.broadcasted_iota(jnp.int32, scores.shape, 1) % block + own * block
    return jnp.where(key <= query, scores, NEG)


def head_twice(pair, group):
    wide = pair.astype(F32)
    lane = lax.broadcasted_iota(jnp.int32, wide.shape, 1)
    keep = (lane < HEAD_DIM) == (group % 2 == 0)
    return jnp.where(keep, wide, pltpu.roll(wide, HEAD_DIM, 1)).astype(BF)


def attention_forward_kernel(
    table,
    q_ref,
    cos_ref,
    sin_ref,
    k_pair,
    v_pair,
    qr_ref,
    o_ref,
    ob_ref,
    lse_ref,
    qm,
    m,
    l,
    acc,
    k_ref,
    v_ref,
):
    block = q_ref.shape[0] // 2
    group = pl.program_id(0)
    k_ref[...] = head_twice(k_pair[...], group)
    v_ref[...] = head_twice(v_pair[...], group)
    for h in range(2):
        rows = slice(h * block, (h + 1) * block)
        cosine, sine = cos_ref[rows, :], sin_ref[rows, :]
        for p in range(PAIRS):
            lanes = slice(p * LANES, (p + 1) * LANES)
            z = q_ref[rows, lanes]
            qr_ref[rows, lanes] = (z * cosine + swap_halves(z) * sine).astype(BF)
        scaled = stack_pairs(qr_ref, rows).astype(F32) * (HEAD_DIM**-0.5)
        qm[...] = split_heads(scaled).astype(BF)
        m[...] = jnp.full_like(m, NEG)
        l[...] = jnp.zeros_like(l)
        acc[...] = jnp.zeros_like(acc)
        own = table[h]

        def step(j, masked):
            keys = two_blocks(k_ref, table, j, block)
            values = two_blocks(v_ref, table, j, block)
            s = dot(keys, qm[...], (1, 1))
            if masked:
                s = causal(s, j, own, block)
            before = m[...]
            now = jnp.maximum(before, jnp.max(s, axis=0, keepdims=True))
            p = jnp.exp(s - now)
            decay = jnp.exp(before - now)
            l[...] = l[...] * decay + jnp.sum(p, axis=0, keepdims=True)
            acc[...] = acc[...] * decay + dot(values, p.astype(BF), (0, 0))
            m[...] = now

        last = own // 2

        @pl.loop(0, last)
        def _(j):
            step(j, False)

        step(last, True)
        lse_ref[0, h : h + 1, :] = m[...] + jnp.log(l[...])
        o = join_heads(acc[...] / l[...])
        for p in range(PAIRS):
            lanes = slice(p * LANES, (p + 1) * LANES)
            piece = o[p * block : (p + 1) * block, :]
            o_ref[rows, lanes] = piece
            ob_ref[rows, lanes] = piece.astype(BF)


def attention_forward(table, q, cosine, sine, kv):
    rows, length = q.shape[0], kv.shape[0]
    query_width = HEADS * HEAD_DIM
    columns = pl.BlockSpec((rows, STACK), lambda g, t: (0, g))
    whole = pl.BlockSpec((rows, LANES), lambda g, t: (0, 0))
    key_pair = pl.BlockSpec((length, LANES), lambda g, t: (0, g // 2))
    value_pair = pl.BlockSpec((length, LANES), lambda g, t: (0, KV_HEADS // 2 + g // 2))
    wide = GROUP * (rows // 2)
    return pl.pallas_call(
        attention_forward_kernel,
        grid_spec=pltpu.PrefetchScalarGridSpec(
            num_scalar_prefetch=1,
            grid=(KV_HEADS,),
            in_specs=[columns, whole, whole, key_pair, value_pair],
            out_specs=[
                columns,
                columns,
                columns,
                pl.BlockSpec((1, 2, wide), lambda g, t: (g, 0, 0)),
            ],
            scratch_shapes=[
                pltpu.VMEM((wide, LANES), BF),
                pltpu.VMEM((1, wide), F32),
                pltpu.VMEM((1, wide), F32),
                pltpu.VMEM((LANES, wide), F32),
                pltpu.VMEM((length, LANES), BF),
                pltpu.VMEM((length, LANES), BF),
            ],
        ),
        out_shape=[
            jax.ShapeDtypeStruct((rows, query_width), BF),
            jax.ShapeDtypeStruct((rows, query_width), F32),
            jax.ShapeDtypeStruct((rows, query_width), BF),
            jax.ShapeDtypeStruct((KV_HEADS, 2, wide), F32),
        ],
        compiler_params=pltpu.CompilerParams(vmem_limit_bytes=32 << 20),
        cost_estimate=pl.CostEstimate(
            flops=8 * HEADS * rows * length * HEAD_DIM,
            bytes_accessed=16 * rows * HEADS * HEAD_DIM,
            transcendentals=HEADS * rows * length,
        ),
        name="attention_forward",
    )(table, q, cosine, sine, kv, kv)


def attention_backward_kernel(
    table,
    qr_ref,
    do_ref,
    o_ref,
    lse_ref,
    k_pair,
    v_pair,
    cos_ref,
    sin_ref,
    dq_ref,
    dkv_ref,
    qm,
    dom,
    dqt,
    k_ref,
    v_ref,
    dk_ref,
    dv_ref,
):
    block = qr_ref.shape[0] // 2
    group = pl.program_id(0)
    k_ref[...] = head_twice(k_pair[...], group)
    v_ref[...] = head_twice(v_pair[...], group)
    dk_ref[...] = jnp.zeros_like(dk_ref)
    dv_ref[...] = jnp.zeros_like(dv_ref)
    for h in range(2):
        rows = slice(h * block, (h + 1) * block)
        scaled = stack_pairs(qr_ref, rows).astype(F32) * (HEAD_DIM**-0.5)
        qm[...] = split_heads(scaled).astype(BF)
        grads = stack_pairs(do_ref, rows).astype(F32)
        dom[...] = split_heads(grads).astype(BF)
        product = (grads * stack_pairs(o_ref, rows)).T
        inner = jnp.concatenate(
            [
                jnp.sum(product[:HEAD_DIM], axis=0, keepdims=True),
                jnp.sum(product[HEAD_DIM:], axis=0, keepdims=True),
            ],
            axis=1,
        )
        lse = lse_ref[0, h : h + 1, :]
        dqt[...] = jnp.zeros_like(dqt)
        own = table[h]

        def step(j, masked):
            keys = two_blocks(k_ref, table, j, block)
            values = two_blocks(v_ref, table, j, block)
            s = dot(keys, qm[...], (1, 1))
            if masked:
                s = causal(s, j, own, block)
            p = jnp.exp(s - lse)
            dp = dot(values, dom[...], (1, 1))
            ds = (p * (dp - inner)).astype(BF)
            dv = dot(p.astype(BF), dom[...], (1, 0))
            dk = dot(ds, qm[...], (1, 0))
            dqt[...] += dot(keys, ds, (0, 0))
            for i in range(2):
                at = pl.ds(pl.multiple_of(table[2 + 2 * j + i] * block, block), block)
                dk_ref[at, :] += dk[i * block : (i + 1) * block]
                dv_ref[at, :] += dv[i * block : (i + 1) * block]

        last = own // 2

        @pl.loop(0, last)
        def _(j):
            step(j, False)

        step(last, True)
        cosine, sine = cos_ref[rows, :], sin_ref[rows, :]
        dq = join_heads(dqt[...] * (HEAD_DIM**-0.5))
        for p in range(PAIRS):
            z = dq[p * block : (p + 1) * block, :]
            dq_ref[rows, p * LANES : (p + 1) * LANES] = (
                z * cosine - swap_halves(z) * sine
            ).astype(BF)
    lane = lax.broadcasted_iota(jnp.int32, dk_ref.shape, 1)
    keep = (lane < HEAD_DIM) == (group % 2 == 0)
    for i, ref in enumerate((dk_ref, dv_ref)):
        both = ref[...] + pltpu.roll(ref[...], HEAD_DIM, 1)
        dkv_ref[i] = jnp.where(keep, both, dkv_ref[i].astype(F32)).astype(BF)


def attention_backward(table, qr, grads, o, lse, kv, cosine, sine):
    rows, length = qr.shape[0], kv.shape[0]
    columns = pl.BlockSpec((rows, STACK), lambda g, t: (0, g))
    whole = pl.BlockSpec((rows, LANES), lambda g, t: (0, 0))
    key_pair = pl.BlockSpec((length, LANES), lambda g, t: (0, g // 2))
    value_pair = pl.BlockSpec((length, LANES), lambda g, t: (0, KV_HEADS // 2 + g // 2))
    wide = GROUP * (rows // 2)
    return pl.pallas_call(
        attention_backward_kernel,
        grid_spec=pltpu.PrefetchScalarGridSpec(
            num_scalar_prefetch=1,
            grid=(KV_HEADS,),
            in_specs=[
                columns,
                columns,
                columns,
                pl.BlockSpec((1, 2, wide), lambda g, t: (g, 0, 0)),
                key_pair,
                value_pair,
                whole,
                whole,
            ],
            out_specs=[columns, pl.BlockSpec((2, length, LANES), lambda g, t: (0, 0, g // 2))],
            scratch_shapes=[
                pltpu.VMEM((wide, LANES), BF),
                pltpu.VMEM((wide, LANES), BF),
                pltpu.VMEM((LANES, wide), F32),
                pltpu.VMEM((length, LANES), BF),
                pltpu.VMEM((length, LANES), BF),
                pltpu.VMEM((length, LANES), F32),
                pltpu.VMEM((length, LANES), F32),
            ],
        ),
        out_shape=[
            jax.ShapeDtypeStruct(qr.shape, BF),
            jax.ShapeDtypeStruct((2, length, KV_HEADS * HEAD_DIM), BF),
        ],
        compiler_params=pltpu.CompilerParams(vmem_limit_bytes=32 << 20),
        cost_estimate=pl.CostEstimate(
            flops=20 * HEADS * rows * length * HEAD_DIM,
            bytes_accessed=16 * rows * HEADS * HEAD_DIM,
            transcendentals=HEADS * rows * length,
        ),
        name="attention_backward",
    )(table, qr, grads, o, lse, kv, kv, cosine, sine)


def own_keys_kernel(k_ref, v_ref, cos_ref, sin_ref, kv_ref):
    width = k_ref.shape[1]
    for p in range(width // LANES):
        lanes = slice(p * LANES, (p + 1) * LANES)
        z = k_ref[:, lanes]
        kv_ref[:, lanes] = (z * cos_ref[...] + swap_halves(z) * sin_ref[...]).astype(BF)
    kv_ref[:, width:] = v_ref[...].astype(BF)


def own_keys(qkv, cosine, sine):
    rows, width = qkv.shape[0], KV_HEADS * HEAD_DIM
    at = HEADS * HEAD_DIM // width
    whole = pl.BlockSpec((rows, LANES), lambda i: (0, 0))
    return pl.pallas_call(
        own_keys_kernel,
        grid=(1,),
        in_specs=[
            pl.BlockSpec((rows, width), lambda i: (0, at)),
            pl.BlockSpec((rows, width), lambda i: (0, at + 1)),
            whole,
            whole,
        ],
        out_specs=pl.BlockSpec((rows, 2 * width), lambda i: (0, 0)),
        out_shape=jax.ShapeDtypeStruct((rows, 2 * width), BF),
        name="own_keys",
    )(qkv, qkv, cosine, sine)


def own_key_grads_kernel(*refs):
    *pieces, cos_ref, sin_ref, out_ref = refs
    width = out_ref.shape[1] // 2

    def total(i, lanes):
        return sum(piece[i, :, lanes].astype(F32) for piece in pieces)

    for p in range(width // LANES):
        lanes = slice(p * LANES, (p + 1) * LANES)
        z = total(0, lanes)
        out_ref[:, lanes] = (z * cos_ref[...] - swap_halves(z) * sin_ref[...]).astype(BF)
        out_ref[:, width + p * LANES : width + (p + 1) * LANES] = total(1, lanes).astype(BF)


def own_key_grads(pieces, cosine, sine):
    rows, width = pieces[0].shape[1], pieces[0].shape[2]
    return pl.pallas_call(
        own_key_grads_kernel,
        out_shape=jax.ShapeDtypeStruct((rows, 2 * width), BF),
        name="own_key_grads",
    )(*pieces, cosine, sine)


def pick_columns_kernel(order, gate_ref, up_ref, out_ref):
    part = gate_ref.shape[1]
    out_ref[0, :, :part] = gate_ref[...]
    out_ref[0, :, part:] = up_ref[...]


def pick_columns(order, share, shares, w_gate, w_up):
    rows, hidden = w_gate.shape[0] // shares, w_gate.shape[1]
    parts = order.shape[0]
    part = hidden // parts
    if part % 128:
        both = [
            lax.dynamic_slice_in_dim(w, share * rows, rows).reshape(rows, parts, part)
            for w in (w_gate, w_up)
        ]
        return jnp.take(jnp.concatenate(both, axis=2).transpose(1, 0, 2), order, axis=0)
    columns = pl.BlockSpec((rows, part), lambda k, t: (t[parts], t[k]))
    return pl.pallas_call(
        pick_columns_kernel,
        grid_spec=pltpu.PrefetchScalarGridSpec(
            num_scalar_prefetch=1,
            grid=(parts,),
            in_specs=[columns, columns],
            out_specs=pl.BlockSpec((1, rows, 2 * part), lambda k, t: (k, 0, 0)),
        ),
        out_shape=jax.ShapeDtypeStruct((parts, rows, 2 * part), BF),
        name="pick_columns",
    )(jnp.concatenate([order, share[None]]), w_gate, w_up)


def assemble_kernel(nc, *refs):
    *pieces, out, sems = refs
    chips = pieces[0].shape[0]
    place, here = lax.axis_index("fsdp"), lax.axis_index("ctx")
    chip, core = place // 2, place % 2

    def copies(ref, other, share, at, go):
        for k in range(chips):
            owner = 2 * (chip ^ k) + (core ^ other)
            copy = pltpu.make_async_copy(
                ref.at[k], out.at[owner, share], sems.at[other, at, k]
            )
            if go:
                copy.start()
            else:
                copy.wait()

    for go in (True, False):
        for other in range(2):
            mine = pieces[other * (2 * nc - 1) : (other + 1) * (2 * nc - 1)]
            copies(mine[0], other, here, 0, go)
            for d in range(1, nc):

                @pl.when(here >= d)
                def _():
                    copies(mine[d], other, here - d, d, go)

                @pl.when(here + d < nc)
                def _():
                    copies(mine[nc - 1 + d], other, here + d, nc - 1 + d, go)


def assemble(nf, nc, pieces):
    chips, rows, columns = pieces[0].shape
    anywhere = pl.BlockSpec(memory_space=pl.ANY)
    return pl.pallas_call(
        functools.partial(assemble_kernel, nc),
        in_specs=[anywhere] * len(pieces),
        out_specs=pl.BlockSpec(memory_space=pltpu.VMEM),
        out_shape=jax.ShapeDtypeStruct((nf, nc, rows, columns), BF),
        scratch_shapes=[pltpu.SemaphoreType.DMA((2, 2 * nc - 1, chips))],
        compiler_params=pltpu.CompilerParams(vmem_limit_bytes=24 << 20),
        name="assemble",
    )(*pieces)


def place_columns_kernel(order, both_ref, gate_ref, up_ref):
    part = gate_ref.shape[1]
    gate_ref[...] = both_ref[0, :, :part].astype(F32)
    up_ref[...] = both_ref[0, :, part:].astype(F32)


def place_columns(order, both):
    parts, shard, part = both.shape[0], both.shape[1], both.shape[2] // 2
    out = jax.ShapeDtypeStruct((shard, parts * part), F32)
    if part % 128:
        both = jnp.take(both, order, axis=0).transpose(1, 0, 2).astype(F32)
        return [both[:, :, i * part : (i + 1) * part].reshape(out.shape) for i in range(2)]
    columns = pl.BlockSpec((shard, part), lambda k, t: (0, t[k]))
    return pl.pallas_call(
        place_columns_kernel,
        grid_spec=pltpu.PrefetchScalarGridSpec(
            num_scalar_prefetch=1,
            grid=(parts,),
            in_specs=[pl.BlockSpec((1, shard, 2 * part), lambda k, t: (k, 0, 0))],
            out_specs=[columns, columns],
        ),
        out_shape=[out, out],
        name="place_columns",
    )(order, both)


def chunk_rows(rows):
    return max(r for r in range(16, 65, 16) if rows % r == 0)


def finish_kernel(nf, nc, *refs):
    sources, outs, owns, ins, xs = (refs[i : i + 5] for i in range(0, 25, 5))
    plane_send, plane_recv, local, in_sem, x_sem, first_send, second_send, out_sem = refs[25:]
    chips = nf // 2
    place, here = lax.axis_index("fsdp"), lax.axis_index("ctx")
    chip = place // 2
    lower = here < nc // 2
    depth = jnp.where(lower, here, nc - 1 - here)
    inner = jnp.where(lower, here + 1, here - 1)
    outer = jnp.where(lower, here - 1, here + 1)
    mesh_id = pl.DeviceIdType.MESH

    barrier = pltpu.get_barrier_semaphore()
    for k in range(1, chips):
        pl.semaphore_signal(
            barrier, inc=1, device_id={"fsdp": place ^ (2 * k)}, device_id_type=mesh_id
        )
    pl.semaphore_signal(barrier, inc=1, device_id={"ctx": inner}, device_id_type=mesh_id)

    @pl.when(depth > 0)
    def _():
        pl.semaphore_signal(barrier, inc=1, device_id={"ctx": outer}, device_id_type=mesh_id)
        pl.semaphore_wait(barrier, chips + 1)

    @pl.when(depth == 0)
    def _():
        pl.semaphore_wait(barrier, chips)

    def plane_copy(u, k):
        return pltpu.make_async_remote_copy(
            src_ref=sources[u].at[chip ^ k],
            dst_ref=owns[u].at[k],
            send_sem=plane_send.at[u, k],
            recv_sem=plane_recv.at[u, k],
            device_id={"fsdp": place ^ (2 * k)},
            device_id_type=mesh_id,
        )

    def local_copy(u):
        if u == 0:
            return pltpu.make_async_copy(sources[0], owns[0], local.at[0])
        return pltpu.make_async_copy(sources[u].at[chip], owns[u].at[0], local.at[u])

    for u in range(5):
        local_copy(u).start()
    for u in range(1, 5):
        for k in range(1, chips):
            plane_copy(u, k).start()

    units = [(0, None)] + [(1, k) for k in range(chips)] + [(u, None) for u in (2, 3, 4)]
    chunks = []
    for u, k in units:
        total = outs[u].shape[-2]
        size = chunk_rows(total)
        chunks += [(u, k, r, size) for r in range(0, total, size)]

    def views(c):
        u, k, r, size = chunks[c]
        rows = pl.ds(r, size)
        own = owns[u].at[rows] if u == 0 else owns[u].at[k or 0, rows]
        return [own] + [
            ref.at[rows] if k is None else ref.at[k, rows] for ref in (ins[u], xs[u], outs[u])
        ]

    def first_copy(c, across):
        own, arriving, x, _ = views(c)
        return pltpu.make_async_remote_copy(
            src_ref=own,
            dst_ref=x if across else arriving,
            send_sem=first_send.at[c],
            recv_sem=(x_sem if across else in_sem).at[c],
            device_id={"ctx": inner},
            device_id_type=mesh_id,
        )

    def second_copy(c, across):
        _, arriving, x, _ = views(c)
        return pltpu.make_async_remote_copy(
            src_ref=arriving if across else x,
            dst_ref=x,
            send_sem=second_send.at[c],
            recv_sem=x_sem.at[c],
            device_id={"ctx": outer},
            device_id_type=mesh_id,
        )

    def out_copy(c, across):
        _, arriving, x, out = views(c)
        return pltpu.make_async_copy(arriving if across else x, out, out_sem.at[c])

    def add_into(target, terms, size):
        @pl.loop(0, size // 16)
        def _(i):
            strip = pl.ds(pl.multiple_of(i * 16, 16), 16)
            target[strip, :] = sum(term[strip, :].astype(F32) for term in terms).astype(BF)

    def inward(c, level):
        u, k, r, size = chunks[c]
        own, arriving, _, _ = views(c)
        terms = [own]
        if r == 0:
            if not k:
                local_copy(u).wait()
            else:
                plane_copy(u, k).wait_recv()
            if u >= 2:
                for j in range(1, chips):
                    plane_copy(u, j).wait_recv()
        if u >= 2:
            terms += [owns[u].at[j, pl.ds(r, size)] for j in range(1, chips)]
        if level > 0:
            first_copy(c, False).wait_recv()
            terms.append(arriving)
        if len(terms) > 1:
            add_into(own, terms, size)
        if c >= FLIGHT:
            first_copy(c - FLIGHT, False).wait_send()
        first_copy(c, level == top).start()

    def outward(c, level):
        size = chunks[c][3]
        own, arriving, x, _ = views(c)
        first_copy(c, True).wait_recv()
        if level == top:
            add_into(arriving, [own, x], size)
        out_copy(c, level == top).start()
        if level > 0:
            if c >= FLIGHT:
                second_copy(c - FLIGHT, False).wait_send()
            second_copy(c, level == top).start()

    top = nc // 2 - 1
    count = len(chunks)
    for level in range(top + 1):

        @pl.when(depth == level)
        def _():
            lag = 1 + 2 * (top - level)
            for t in range(count + lag):
                if t < count:
                    inward(t, level)
                if t >= lag:
                    outward(t - lag, level)
            for c in range(max(0, count - FLIGHT), count):
                first_copy(c, False).wait_send()
                if level > 0:
                    second_copy(c, False).wait_send()
            for c in range(count):
                out_copy(c, False).wait()

    for u in range(1, 5):
        for k in range(1, chips):
            plane_copy(u, k).wait_send()


def finish(nf, nc, down, gate_up, *sums):
    chips = nf // 2
    arrays = (down, gate_up) + sums
    shapes = [down.shape, gate_up.shape] + [x.shape[1:] for x in sums]
    count = sum(
        (shape[0] if len(shape) == 3 else 1) * (shape[-2] // chunk_rows(shape[-2]))
        for shape in shapes
    )
    anywhere = pl.BlockSpec(memory_space=pl.ANY)
    dma = pltpu.SemaphoreType.DMA
    return pl.pallas_call(
        functools.partial(finish_kernel, nf, nc),
        in_specs=[anywhere] * 5,
        out_specs=[anywhere] * 5,
        out_shape=[jax.ShapeDtypeStruct(shape, BF) for shape in shapes],
        scratch_shapes=[pltpu.VMEM(x.shape, BF) for x in arrays]
        + [pltpu.VMEM(shape, BF) for shape in shapes]
        + [pltpu.VMEM(shape, BF) for shape in shapes]
        + [dma((5, chips)), dma((5, chips)), dma((5,))]
        + [dma((count,))] * 5,
        compiler_params=pltpu.CompilerParams(
            collective_id=0, has_side_effects=True, vmem_limit_bytes=56 << 20
        ),
        name="finish",
    )(*arrays)


def solution(mesh):
    nf, nc = mesh.shape["fsdp"], mesh.shape["ctx"]
    chips = nf // 2

    def swap(x, k):
        return lax.ppermute(x, "fsdp", [(i, i ^ k) for i in range(nf)])

    def cross(x, k):
        return lax.ppermute(x, "ctx", [(i, i ^ k) for i in range(nc)])

    def shards(
        tokens,
        attn_gain,
        w_query,
        w_key,
        w_value,
        w_out,
        ffn_gain,
        w_gate,
        w_up,
        w_down,
        block_table,
        positions,
        out_grad,
    ):
        place = lax.axis_index("fsdp")
        chip, core = place // 2, place % 2
        x = tokens[0].astype(F32)
        gb = out_grad[0]
        rows, width = x.shape
        hidden = w_gate.shape[1]
        part = hidden // chips
        shard = w_gate.shape[0]
        key_width = KV_HEADS * HEAD_DIM

        def core_sum(x):
            other = lax.dynamic_index_in_dim(x, 1 - core, 1, keepdims=False)
            mine = lax.dynamic_index_in_dim(x, core, 1, keepdims=False)
            return (mine.astype(F32) + swap(other, 1).astype(F32)).astype(BF)

        def rows_grad(left, right):
            columns = [left[:, i * shard : (i + 1) * shard] for i in range(nf)]
            even = jnp.concatenate(columns[::2], axis=1)
            odd = jnp.concatenate(columns[1::2], axis=1)
            mine = jnp.where(core == 0, even, odd)
            other = jnp.where(core == 0, odd, even)
            left = jnp.concatenate([mine, swap(other, 1)], axis=0)
            right = jnp.concatenate([right, swap(right, 1)], axis=0)
            return dot(left, right, (0, 0)).astype(BF).reshape(chips, shard, right.shape[1])

        gains = lax.all_gather(jnp.stack([attn_gain, ffn_gain]), "fsdp", axis=1, tiled=True)
        gains = gains.astype(F32)
        w_qkv = lax.all_gather(
            jnp.concatenate([w_query, w_key, w_value], axis=1), "fsdp", axis=0, tiled=True
        )
        w_o = lax.all_gather(w_out, "fsdp", axis=0, tiled=True)

        order = chip ^ jnp.arange(chips, dtype=jnp.int32)
        w_gate, w_up, gains = lax.optimization_barrier((w_gate, w_up, gains))
        gate_up = pick_columns(order, lax.axis_index("ctx"), nc, w_gate, w_up)
        first = jnp.stack([swap(gate_up[k], 2 * k) if k else gate_up[k] for k in range(chips)])
        upward = [(i, i + 1) for i in range(nc - 1)]
        downward = [(i + 1, i) for i in range(nc - 1)]
        below, above = [first], [first]
        for _ in range(nc - 2):
            below.append(lax.ppermute(below[-1], "ctx", upward))
            above.append(lax.ppermute(above[-1], "ctx", downward))
        w_d = jnp.zeros((2,) + w_down.shape, BF)
        w_d = lax.dynamic_update_index_in_dim(w_d, w_down, core, 0)
        w_d = lax.dynamic_update_index_in_dim(w_d, swap(w_down, 1), 1 - core, 0)
        w_d = w_d.reshape(part, width)

        half = HEAD_DIM // 2
        frequency = THETA ** (-jnp.arange(half, dtype=F32) * (2.0 / HEAD_DIM))
        angle = positions[0].astype(F32)[:, None] * frequency[None, :]
        cosine, sine = jnp.cos(angle), jnp.sin(angle)
        cos_lanes = jnp.tile(cosine, (1, 4))
        sin_lanes = jnp.tile(jnp.concatenate([-sine, sine], axis=1), (1, 2))
        blocks = 2 * nc
        stored = block_table.reshape(-1)
        number = jnp.arange(blocks, dtype=jnp.int32)
        where = jnp.sum(
            jnp.where(stored[None, :] == number[:, None], number[None, :], 0), axis=1
        )
        here = lax.axis_index("ctx")
        own = lax.dynamic_slice_in_dim(stored, 2 * here, 2)
        where = 2 * ((where // 2) ^ here) + where % 2
        table = jnp.concatenate([own, where]).astype(jnp.int32)

        inverse_one = lax.rsqrt(jnp.mean(x * x, axis=1, keepdims=True) + EPS)
        unit_one = x * inverse_one
        xn = (unit_one * gains[0][None, :]).astype(BF)
        qkv = dot(xn, w_qkv, (1, 0))
        kv = own_keys(qkv, cos_lanes, sin_lanes)
        sent, _ = lax.optimization_barrier((gb, kv))
        gb_of = [swap(sent, k) if k else gb for k in range(0, nf, 2)]
        _, below[-1], above[-1] = lax.optimization_barrier((kv, below[-1], above[-1]))
        below.append(lax.ppermute(below[-1], "ctx", upward))
        above.append(lax.ppermute(above[-1], "ctx", downward))
        kv = jnp.concatenate([cross(kv, k) if k else kv for k in range(nc)], axis=0)
        qr, o, ob, lse = attention_forward(table, qkv, cos_lanes, sin_lanes, kv)
        h1 = x + dot(ob, w_o, (1, 0))
        inverse_two = lax.rsqrt(jnp.mean(h1 * h1, axis=1, keepdims=True) + EPS)
        unit_two = h1 * inverse_two
        hn = (unit_two * gains[1][None, :]).astype(BF)

        pieces = [first] + below[1:] + above[1:]
        hn, gb_of, pieces = lax.optimization_barrier((hn, gb_of, pieces))
        w_gu = assemble(nf, nc, pieces + [swap(piece, 1) for piece in pieces])
        w_gu = w_gu.reshape(width, 2 * part)

        outs, dhns = [], []
        hn_of, act_of, dgu_of = [], [], []
        for k in range(0, nf, 2):
            hn_k = swap(hn, k) if k else hn
            gu = dot(hn_k, w_gu, (1, 0))
            dact = dot(gb_of[k // 2], w_d, (1, 1))
            gate, up = gu[:, :part], gu[:, part:]
            sg = jax.nn.sigmoid(gate)
            silu = gate * sg
            act = (silu * up).astype(BF)
            dgate = (dact * up * sg * (1.0 + gate * (1.0 - sg))).astype(BF)
            dgu = jnp.concatenate([dgate, (dact * silu).astype(BF)], axis=1)
            out_k = dot(act, w_d, (1, 0))
            dhn_k = dot(dgu, w_gu, (1, 1))
            outs.append(out_k.astype(BF) if k else out_k)
            dhns.append(dhn_k.astype(BF) if k else dhn_k)
            hn_of.append(hn_k)
            act_of.append(act)
            dgu_of.append(dgu)
        got = [swap(dhns[k], 2 * k) for k in range(1, chips)]
        act_of, dgu_of, got[:-1], _ = lax.optimization_barrier(
            (act_of, dgu_of, got[:-1], dhns[1:])
        )
        grad_hn = dhns[0]
        for piece in got:
            grad_hn = grad_hn + piece.astype(F32)

        gb_all = jnp.concatenate(gb_of, axis=0)
        down = dot(jnp.concatenate(act_of, axis=0), gb_all, (0, 0)).astype(BF)
        wide = rows_grad(jnp.concatenate(hn_of, axis=0), jnp.concatenate(dgu_of, axis=0))
        down_sum = core_sum(down.reshape((1, 2) + w_down.shape))[0]
        down_sum, wide, grad_hn = lax.optimization_barrier((down_sum, wide, grad_hn))
        branch = h1 + outs[0]
        for k in range(1, chips):
            branch = branch + swap(outs[k], 2 * k).astype(F32)
        layer_out = branch.astype(BF)

        gain_two_grad = jnp.sum(grad_hn * unit_two, axis=0)
        grad_unit = grad_hn * gains[1][None, :]
        dh1 = gb.astype(F32) + inverse_two * (
            grad_unit - unit_two * jnp.mean(grad_unit * unit_two, axis=1, keepdims=True)
        )
        dab = dh1.astype(BF)
        dob = dot(dab, w_o, (1, 1)).astype(BF)
        out_term = rows_grad(ob, dab)
        dq, dkv = attention_backward(table, qr, dob, o, lse, kv, cos_lanes, sin_lanes)
        pieces = [dkv[:, k * rows : (k + 1) * rows] for k in range(nc)]
        pieces = [cross(piece, k) if k else piece for k, piece in enumerate(pieces)]
        dqkv = jnp.concatenate([dq, own_key_grads(pieces, cos_lanes, sin_lanes)], axis=1)
        grad_xn = dot(dqkv, w_qkv, (1, 1))
        gain_one_grad = jnp.sum(grad_xn * unit_one, axis=0)
        grad_unit = grad_xn * gains[0][None, :]
        tokens_grad = dh1 + inverse_one * (
            grad_unit - unit_one * jnp.mean(grad_unit * unit_one, axis=1, keepdims=True)
        )
        qkv_term = rows_grad(xn, dqkv)

        gains_of = jnp.stack([gain_one_grad, gain_two_grad]).reshape(2, chips, 2, shard)
        other = lax.dynamic_index_in_dim(gains_of, 1 - core, 2, keepdims=False)
        mine = lax.dynamic_index_in_dim(gains_of, core, 2, keepdims=False)
        gains_of = (mine + swap(other, 1)).transpose(1, 0, 2).reshape(chips, 1, 2 * shard)
        gains_of = jnp.pad(gains_of.astype(BF), ((0, 0), (0, 15), (0, 0)))
        down_sum, gu_sum, out_sum, qkv_sum, gain_sum = finish(
            nf, nc, down_sum, wide, out_term, qkv_term, gains_of
        )
        qkv_sum = qkv_sum.astype(F32)
        gain_sum = gain_sum[0].reshape(2, shard).astype(F32)
        gate_grad, up_grad = place_columns(order, gu_sum)
        query_width = HEADS * HEAD_DIM
        return (
            layer_out.reshape(1, rows, width),
            tokens_grad.reshape(1, rows, width),
            gain_sum[0],
            qkv_sum[:, :query_width],
            qkv_sum[:, query_width : query_width + key_width],
            qkv_sum[:, query_width + key_width :],
            out_sum.astype(F32),
            gain_sum[1],
            gate_grad,
            up_grad,
            down_sum.astype(F32),
        )

    weight = P("fsdp", None)
    activation = P("fsdp", "ctx", None)
    return jax.shard_map(
        shards,
        mesh=mesh,
        in_specs=(
            activation,
            P("fsdp"),
            weight,
            weight,
            weight,
            weight,
            P("fsdp"),
            weight,
            weight,
            weight,
            P(),
            P("fsdp", "ctx"),
            activation,
        ),
        out_specs=(
            activation,
            activation,
            P("fsdp"),
            weight,
            weight,
            weight,
            weight,
            P("fsdp"),
            weight,
            weight,
            weight,
        ),
        check_vma=False,
    )
```

time: 3210 us -> 838 us (0.26)
  waiting for transfers between devices: 2600 us -> 150 us
  Pallas kernels: 0 us -> 331 us
  matrix products: 350 us -> 178 us
  blocking collectives: 89.2 us -> 10.3 us
  local copies, waits for them, and re-layouts: 110 us -> 42.7 us
  starting transfers between devices: 1.1 us -> 59.7 us
    unnamed x17 -> x2, waiting for transfers between devices: 989 us -> 0.71 us
    psum x1 -> x0, waiting for transfers between devices: 676 us -> none  [shards(): lax.psum((gain_one_shard, query_shard, key_shard, value_shard, out_shard,...]
    reduce_scatter x7 -> x0, waiting for transfers between devices: 604 us -> none  [the longest x1 268 us: shards(): lax.psum_scatter(contract_rows(activated, grad_branch), 'fsdp', scatter_d...]
    pallas_call x0 -> x8, Pallas kernels: none -> 331 us  [the longest x1 264 us: finish(): pl.pallas_call(functools.partial(finish_kernel, nf, nc), in_specs=[anywhe...]
    all_gather x7 -> x2, waiting for transfers between devices: 335 us -> 6.12 us  [the longest x1 6.11 us: shards(): w_o = lax.all_gather(w_out, 'fsdp', axis=0, tiled=True)]
    dot_general x244 -> x24, matrix products: 350 us -> 178 us  [dot(): lax.dot_general(left, right, ((contract[:1], contract[1:]), ((), ())), pr...]
    ppermute x0 -> x43, waiting for transfers between devices: none -> 143 us  [the longest x31 68.5 us: swap(): return lax.ppermute(x, 'fsdp', [(i, i ^ k) for i in range(nf)])]
    ppermute x0 -> x43, starting transfers between devices: none -> 59.6 us  [the longest x31 20.9 us: swap(): return lax.ppermute(x, 'fsdp', [(i, i ^ k) for i in range(nf)])]
  transfers between devices with their start and end apart: 16 -> 45, of which waited for: 14 -> 13; matrix products, arithmetic and copies ran while one was open for 7% -> 28% of each run, Pallas kernels for 0% -> 7%
where the time goes in v1:
time: 838 us; the launch traced here: 830 us
  Pallas kernels  331 us (39%)
  matrix products  178 us (21%)
  waiting for transfers between devices  150 us (18%)
  starting transfers between devices  59.7 us (7%)
  other arithmetic  44.1 us (5%)
  local copies, waits for them, and re-layouts  42.7 us (5%)
  between operations  15.2 us (2%)
  blocking collectives  10.3 us (1%)
    pallas_call x1, Pallas kernels, finish(): pl.pallas_call(functools.partial(finish_kernel, nf, nc), in_specs=[anywhe...  264 us
    dot_general x24, matrix products, dot(): lax.dot_general(left, right, ((contract[:1], contract[1:]), ((), ())), pr...  178 us
    ppermute x31, waiting for transfers between devices, swap(): return lax.ppermute(x, 'fsdp', [(i, i ^ k) for i in range(nf)])  68.5 us
    ppermute x3, waiting for transfers between devices, shards(): above.append(lax.ppermute(above[-1], 'ctx', downward))  50.8 us
    ppermute x6, waiting for transfers between devices, cross(): return lax.ppermute(x, 'ctx', [(i, i ^ k) for i in range(nc)])  23.7 us
    pallas_call x1, Pallas kernels, attention_backward(): pl.pallas_call(attention_backward_kernel, grid_spec=pltpu.PrefetchScalarG...  22.6 us
    ppermute x31, starting transfers between devices, swap(): return lax.ppermute(x, 'fsdp', [(i, i ^ k) for i in range(nf)])  20.9 us
    pallas_call x1, Pallas kernels, attention_forward(): pl.pallas_call(attention_forward_kernel, grid_spec=pltpu.PrefetchScalarGr...  18.9 us
  transfers between devices with their start and end apart: 45, of which 13 were waited for; matrix products, arithmetic and copies ran while one was open for 28% of the time, Pallas kernels for 7%

profile of v1, /device:TPU:0, one launch (start us, length us, event | category | flops | bytes accessed | tf_op | source)
XLA Modules:
  0.0 830.3 jit_solution(1013593532905980449)
XLA Ops:
  10.6 10.3 %all_gather.9 = bf16[2,2048]{1,0:T(2,128)(2,1)S(1)} all-gather(bf16[2,256]{1,0:T(2,128)(2,1)S(1)} %pad_maximum_fusion.16), channel_id=1, replica_groups=mesh['ctx'=4,'fsdp'=8] {'fsdp'}, dimensions={1}, use_global_device_ids=true | all-gather | bytes 9216 | tf_op jit(solution)/shard_map/all_gather | solution.py:709
  22.1 4.4 pick_columns.1
  31.7 15.2 %collective-permute-done.8 = bf16[64,2816]{1,0:T(8,128)(2,1)S(1)} collective-permute-done((bf16[64,2816]{1,0:T(8,128)(2,1)S(1)}, bf16[64,2816]{1,0:T(8,128)(2,1)S(1)}, u32[]{:S(2)}, u32[]{:S(2)}) %collective-permute-start.8) | collective-permute-done | bytes 360480 | tf_op jit(solution)/shard_map/ppermute | solution.py:664
  46.9 7.1 collective-permute-done.7
  57.4 5.7 collective-permute-start.9
  65.3 26.2 %collective-permute-done.11.refs_4_ = bf16[4,64,2816]{2,1,0:T(8,128)(2,1)} collective-permute-done((bf16[4,64,2816]{2,1,0:T(8,128)(2,1)S(1)}, bf16[4,64,2816]{2,1,0:T(8,128)(2,1)}, u32[]{:S(2)}, u32[]{:S(2)}) %collective-permute-start.11) | collective-permute-done | bytes 1441824 | tf_op jit(solution)/shard_map/ppermute | solution.py:725
  92.8 5.7 collective-permute-start.10
  98.5 9.3 %fusion.73.k_ref.v_ref.q_ref = f32[256,2560]{1,0:T(8,128)} fusion(bf16[256,2048]{1,0:T(8,128)(2,1)S(1)} %fusion.35, bf16[2048,2560]{1,0:T(8,128)(2,1)} %all-gather.3.cloned.1.call-done), kind=kOutput, calls=%fused_computation.173 | convolution fusion | flops 2684354560 | bytes 14155776 | tf_op jit(solution)/shard_map/dot_general | solution.py:27
  119.2 7.2 collective-permute-done.12.refs_5_
  126.4 10.7 %collective-permute-start.1 = (bf16[256,512]{1,0:T(8,128)(2,1)S(1)}, bf16[256,512]{1,0:T(8,128)(2,1)S(1)}, u32[]{:S(2)}, u32[]{:S(2)}) collective-permute-start(bf16[256,512]{1,0:T(8,128)(2,1)S(1)} %copy-done.31), channel_id=1, source_target_pairs={{0,16},{8,24},{16,0},{24,8},{1,17},{9,25},{17,1},{25,9},{2,18},{10... | collective-permute-start | bytes 786440 | tf_op jit(solution)/shard_map/ppermute | solution.py:667
  140.4 9.1 %collective-permute-done.1 = bf16[256,512]{1,0:T(8,128)(2,1)S(1)} collective-permute-done((bf16[256,512]{1,0:T(8,128)(2,1)S(1)}, bf16[256,512]{1,0:T(8,128)(2,1)S(1)}, u32[]{:S(2)}, u32[]{:S(2)}) %collective-permute-start.1) | collective-permute-done | bytes 262176 | tf_op jit(solution)/shard_map/ppermute | solution.py:667
  151.0 4.9 collective-permute-start.13
  156.0 18.9 %attention_forward.1 = (bf16[256,2048]{1,0:T(8,128)(2,1)S(1)}, f32[256,2048]{1,0:T(8,128)S(1)}, bf16[256,2048]{1,0:T(8,128)(2,1)S(1)}, f32[4,2,1024]{2,1,0:T(2,128)S(1)}) custom-call(s32[10]{0:T(128)S(1)} %pad_add_fusion.table, f32[256,2560]{1,0:T(8,128)S(1)} %copy-done, f32[256,128]{1,0:T(8,128)S(1)} %copy-done.5, f32[256,128]{1,0:T(8,128)S(1)} %copy-done.3, ...), custom_call_target="tpu_custom_call" | custom-call | flops 4294967296 | bytes 8388608 | tf_op jit(solution)/shard_map/attention_forward/pallas_call | solution.py:154
  180.0 6.1 all-gather.5.cloned.1.call-done
  186.1 6.4 multiply_reduce_fusion.2
  193.7 17.4 %collective-permute-done.14.refs_6_ = bf16[4,64,2816]{2,1,0:T(8,128)(2,1)S(1)} collective-permute-done((bf16[4,64,2816]{2,1,0:T(8,128)(2,1)}, bf16[4,64,2816]{2,1,0:T(8,128)(2,1)S(1)}, u32[]{:S(2)}, u32[]{:S(2)}) %collective-permute-start.14) | collective-permute-done | bytes 1441824 | tf_op jit(solution)/shard_map/ppermute | solution.py:757
  223.6 18.3 %collective-permute-done.27 = bf16[256,2048]{1,0:T(8,128)(2,1)S(1)} collective-permute-done((bf16[256,2048]{1,0:T(8,128)(2,1)S(1)}, bf16[256,2048]{1,0:T(8,128)(2,1)S(1)}, u32[]{:S(2)}, u32[]{:S(2)}) %collective-permute-start.27) | collective-permute-done | bytes 1048608 | tf_op jit(solution)/shard_map/ppermute | solution.py:664
  241.8 21.2 %collective-permute-done.25 = bf16[256,2048]{1,0:T(8,128)(2,1)S(1)} collective-permute-done((bf16[256,2048]{1,0:T(8,128)(2,1)S(1)}, bf16[256,2048]{1,0:T(8,128)(2,1)S(1)}, u32[]{:S(2)}, u32[]{:S(2)}) %collective-permute-start.25) | collective-permute-done | bytes 1048608 | tf_op jit(solution)/shard_map/ppermute | solution.py:664
  274.2 8.4 %assemble.1 = bf16[8,4,64,2816]{3,2,1,0:T(8,128)(2,1)} custom-call(bf16[4,64,2816]{2,1,0:T(8,128)(2,1)S(1)} %copy-done.2, bf16[4,64,2816]{2,1,0:T(8,128)(2,1)} %collective-permute-done.9.refs_1_, bf16[4,64,2816]{2,1,0:T(8,128)(2,1)} %collective-permute-done.10.refs_2_, bf16[4,64,2816]{2,1,0:T(8,128)(2,1)} %collective-permute-done.13.refs_3_, ...), custom_call_target="tpu_custom_call" | custom-call | tf_op jit(solution)/shard_map/assemble/pallas_call | solution.py:436
  282.6 9.1 %fusion.74 = f32[256,2816]{1,0:T(8,128)} fusion(bf16[256,2048]{1,0:T(8,128)(2,1)S(1)} %copy-done.24, bf16[2048,2816]{1,0:T(8,128)(2,1)} %bitcast.98), kind=kOutput, calls=%fused_computation.174 | convolution fusion | flops 2952790016 | bytes 15466496 | tf_op jit(solution)/shard_map/dot_general | solution.py:27
  294.9 6.1 multiply_convert_fusion.6
  301.0 7.4 convolution_convert_fusion.6
  308.5 6.5 fusion.76
  315.0 6.1 multiply_convert_fusion.4
  321.1 7.4 convolution_convert_fusion.5
  330.5 6.7 fusion.77
  337.2 6.3 multiply_convert_fusion.2
  343.4 5.2 multiply_convert_fusion.8
  348.9 8.4 %convolution_convert_fusion.4 = bf16[256,2048]{1,0:T(8,128)(2,1)} fusion(bf16[2048,2816]{1,0:T(8,128)(2,1)} %bitcast.103, bf16[256,1408]{1,0:T(8,128)(2,1)S(1)} %get-tuple-element.104, bf16[256,1408]{1,0:T(8,128)(2,1)S(1)} %get-tuple-element.103), kind=kOutput, calls=%fused_computation.48 | convolution fusion | flops 2956197888 | bytes 14024704 | tf_op jit(solution)/shard_map/dot_general | solution.py:27
  357.4 11.3 %pad_maximum_fusion = bf16[1024,2816]{1,0:T(8,128)(2,1)} fusion(bf16[256,2816]{1,0:T(8,128)(2,1)S(1)} %pad_maximum_fusion.7, bf16[256,2816]{1,0:T(8,128)(2,1)S(1)} %pad_maximum_fusion.6, bf16[256,2816]{1,0:T(8,128)(2,1)S(1)} %pad_maximum_fusion.5, bf16[256,2816]{1,0:T(8,128)(2,1)S(1)} %pad_maximum_fusion.4), kind=kLoop, calls=%fused_computation.1 | loop fusion | flops 23068672 | bytes 11534336 | tf_op jit(solution)/shard_map/concatenate | solution.py:799
  368.8 5.5 convolution_convert_fusion.10
  376.0 5.4 convolution_convert_fusion.9
  381.5 10.9 %convolution_convert_fusion = bf16[1408,2048]{1,0:T(8,128)(2,1)} fusion(bf16[256,2048]{1,0:T(8,128)(2,1)} %collective-permute-done.5, bf16[256,2048]{1,0:T(8,128)(2,1)} %collective-permute-done.4, bf16[256,2048]{1,0:T(8,128)(2,1)} %collective-permute-done.3, bf16[256,2048]{1,0:T(8,128)(2,1)} %bitcast.7, bf16[256,1408]{1,0:T(8,128)(2,1)S(1)} %copy-done.56, ...), kind=kOutput, calls=%fused_computation | convolution fusion | flops 5936775168 | bytes 12845056 | tf_op jit(solution)/shard_map/dot_general | solution.py:27
  396.3 5.4 convolution_convert_fusion.8
  402.1 5.3 copy-done.38
  407.8 8.8 %fusion.32 = f32[256,2048]{1,0:T(8,128)S(1)} fusion(bf16[2048,2816]{1,0:T(8,128)(2,1)} %bitcast.104, bf16[256,2048]{1,0:T(8,128)(2,1)} %collective-permute-done.34, bf16[256,2048]{1,0:T(8,128)(2,1)} %copy-done.48, bf16[256,2048]{1,0:T(8,128)(2,1)} %copy-done.49, bf16[256,1408]{1,0:T(8,128)(2,1)S(1)} %get-tuple-element.110, ...), kind=kOutput, calls=%fused_computation.46 | convolution fusion | flops 2958819328 | bytes 18219008 | tf_op jit(solution)/shard_map/dot_general | solution.py:27
  421.9 5.4 constant_dynamic-update-slice_fusion.4
  428.5 18.9 %convolution_convert_fusion.2 = bf16[1024,2816]{1,0:T(8,128)(2,1)} fusion(bf16[2048,2816]{1,0:T(8,128)(2,1)} %constant_dynamic-update-slice_fusion.4, bf16[1024,1024]{1,0:T(8,128)(2,1)} %collective-permute-done.32, bf16[1024,1024]{1,0:T(8,128)(2,1)S(1)} %copy-done.28), kind=kOutput, calls=%fused_computation.5 | convolution fusion | flops 11822432256 | bytes 21495808 | tf_op jit(solution)/shard_map/dot_general | solution.py:27
  451.1 6.2 convolution_convert_fusion.7.do_ref
  457.4 22.6 %attention_backward.1 = (bf16[256,2048]{1,0:T(8,128)(2,1)S(1)}, bf16[2,1024,256]{2,1,0:T(8,128)(2,1)S(1)}) custom-call(s32[10]{0:T(128)S(1)} %copy-done.12, bf16[256,2048]{1,0:T(8,128)(2,1)S(1)} %copy-done.16, bf16[256,2048]{1,0:T(8,128)(2,1)S(1)} %convolution_convert_fusion.7.do_ref, f32[256,2048]{1,0:T(8,128)S(1)} %copy-done.14, ...), custom_call_target="tpu_custom_call" | custom-call | flops 10737418240 | bytes 8388608 | tf_op jit(solution)/shard_map/attention_backward/pallas_call | solution.py:280
  485.2 5.9 fusion.34
  491.9 13.7 %collective-permute-done.36.refs_2_ = bf16[2,256,256]{2,1,0:T(8,128)(2,1)S(1)} collective-permute-done((bf16[2,256,256]{2,1,0:T(8,128)(2,1)S(1)}, bf16[2,256,256]{2,1,0:T(8,128)(2,1)S(1)}, u32[]{:S(2)}, u32[]{:S(2)}) %collective-permute-start.36) | collective-permute-done | bytes 262176 | tf_op jit(solution)/shard_map/ppermute | solution.py:667
  510.9 8.4 %fusion.41 = (f32[2048]{0:T(1024)S(1)}, f32[256]{0:T(256)S(1)}, f32[256,2048]{1,0:T(8,128)}) fusion(bf16[1,256,2048]{2,1,0:T(8,128)(2,1)S(1)} %copy-done.23, f32[256]{0:T(256)S(1)} %copy-done.42, f32[2048]{0:T(1024)S(1)} %bitcast.122, bf16[2048,2560]{1,0:T(8,128)(2,1)} %all-gather.3.cloned.1.call-done, bf16[256,512]{1,0:T(8,128)(2,1)S(1)} %copy-done.30, ...), kind=kOutput, calls=%fused_computation.62 | convolution fusion | flops 2690643712 | bytes 14960640 | tf_op jit(solution)/shard_map/dot_general | solution.py:27
  520.0 5.3 fusion.40
  526.0 6.2 convolution_convert_fusion.3
  532.1 7.8 convolution_convert_fusion.1
  540.0 264.4 %finish.1 = (bf16[704,2048]{1,0:T(8,128)(2,1)}, bf16[4,256,2816]{2,1,0:T(8,128)(2,1)}, bf16[256,2048]{1,0:T(8,128)(2,1)}, bf16[256,2560]{1,0:T(8,128)(2,1)}, bf16[16,512]{1,0:T(8,128)(2,1)}) custom-call(bf16[704,2048]{1,0:T(8,128)(2,1)} %fusion.15.refs_0_, bf16[4,256,2816]{2,1,0:T(8,128)(2,1)} %bitcast.110, bf16[4,256,2048]{2,1,0:T(8,128)(2,1)} %bitcast.112, ...), custom_call_target="tpu_custom_call" | custom-call | tf_op jit(solution)/shard_map/finish/pallas_call | solution.py:642
  815.3 8.0 place_columns.1
  (275 shorter events, 107.9 us)
Async XLA Ops:
  7.2 91.3 %all-gather.3.cloned.1.call-start = ((), (), s32[]{:S(2)}) async-start(), calls=%async_computation | async-start | bytes 11796480 | tf_op jit(solution)/shard_map/all_gather | solution.py:711
  9.8 176.3 %all-gather.5.cloned.1.call-start = ((), (), s32[]{:S(2)}) async-start(), calls=%async_computation.1 | async-start | bytes 9437184 | tf_op jit(solution)/shard_map/all_gather | solution.py:714
  27.9 19.0 %collective-permute-start.8 = (bf16[64,2816]{1,0:T(8,128)(2,1)S(1)}, bf16[64,2816]{1,0:T(8,128)(2,1)S(1)}, u32[]{:S(2)}, u32[]{:S(2)}) collective-permute-start(bf16[64,2816]{1,0:T(8,128)(2,1)S(1)} %get-tuple-element.126), channel_id=1, source_target_pairs={{0,6},{1,7},{2,4},{3,5},{4,2},{5,3},{6,0},{7,1},{8,14},{9,15},{10,... | collective-permute-start | bytes 1081352 | tf_op jit(solution)/shard_map/ppermute | solution.py:664
  29.4 24.7 %collective-permute-start.7 = (bf16[64,2816]{1,0:T(8,128)(2,1)S(1)}, bf16[64,2816]{1,0:T(8,128)(2,1)S(1)}, u32[]{:S(2)}, u32[]{:S(2)}) collective-permute-start(bf16[64,2816]{1,0:T(8,128)(2,1)S(1)} %get-tuple-element.127), channel_id=1, source_target_pairs={{0,4},{1,5},{2,6},{3,7},{4,0},{5,1},{6,2},{7,3},{8,12},{9,13},{10,... | collective-permute-start | bytes 1081352 | tf_op jit(solution)/shard_map/ppermute | solution.py:664
  30.9 23.1 %collective-permute-start.6 = (bf16[64,2816]{1,0:T(8,128)(2,1)S(1)}, bf16[64,2816]{1,0:T(8,128)(2,1)}, u32[]{:S(2)}, u32[]{:S(2)}) collective-permute-start(bf16[64,2816]{1,0:T(8,128)(2,1)S(1)} %get-tuple-element.128), channel_id=1, source_target_pairs={{0,2},{1,3},{2,0},{3,1},{4,6},{5,7},{6,4},{7,5},{8,10},{9,11},{10,... | collective-permute-start | bytes 1081352 | tf_op jit(solution)/shard_map/ppermute | solution.py:664
  31.4 185.4 %collective-permute-start.22 = (bf16[704,2048]{1,0:T(8,128)(2,1)}, bf16[704,2048]{1,0:T(8,128)(2,1)}, u32[]{:S(2)}, u32[]{:S(2)}) collective-permute-start(bf16[704,2048]{1,0:T(8,128)(2,1)} %param.22), channel_id=1, source_target_pairs={{0,1},{1,0},{2,3},{3,2},{4,5},{5,4},{6,7},{7,6},{8,9},{9,8},{10,11... | collective-permute-start | bytes 8650760 | tf_op jit(solution)/shard_map/ppermute | solution.py:664
  56.1 35.4 %collective-permute-start.11 = (bf16[4,64,2816]{2,1,0:T(8,128)(2,1)S(1)}, bf16[4,64,2816]{2,1,0:T(8,128)(2,1)}, u32[]{:S(2)}, u32[]{:S(2)}) collective-permute-start(bf16[4,64,2816]{2,1,0:T(8,128)(2,1)S(1)} %pad_maximum_fusion.3.refs_0_), channel_id=1, source_target_pairs={{8,0},{16,8},{24,16},{9,1},{17,9},{25,17},{10,2},{18,10},{26,18},{... | collective-permute-start | bytes 4325384 | tf_op jit(solution)/shard_map/ppermute | solution.py:725
  57.4 35.4 %collective-permute-start.9 = (bf16[4,64,2816]{2,1,0:T(8,128)(2,1)S(1)}, bf16[4,64,2816]{2,1,0:T(8,128)(2,1)}, u32[]{:S(2)}, u32[]{:S(2)}) collective-permute-start(bf16[4,64,2816]{2,1,0:T(8,128)(2,1)S(1)} %pad_maximum_fusion.3.refs_0_), channel_id=1, source_target_pairs={{0,8},{8,16},{16,24},{1,9},{9,17},{17,25},{2,10},{10,18},{18,26},{... | collective-permute-start | bytes 4325384 | tf_op jit(solution)/shard_map/ppermute | solution.py:724
  65.2 42.5 %copy-start.25 = (bf16[256,2048]{1,0:T(8,128)(2,1)}, bf16[256,2048]{1,0:T(8,128)(2,1)S(1)}, u32[]{:S(2)}) copy-start(bf16[256,2048]{1,0:T(8,128)(2,1)S(1)} %fusion.35) | copy-start | bytes 3145732
  91.5 34.9 %collective-permute-start.12 = (bf16[4,64,2816]{2,1,0:T(8,128)(2,1)}, bf16[4,64,2816]{2,1,0:T(8,128)(2,1)}, u32[]{:S(2)}, u32[]{:S(2)}) collective-permute-start(bf16[4,64,2816]{2,1,0:T(8,128)(2,1)} %collective-permute-done.11.refs_4_), channel_id=1, source_target_pairs={{8,0},{16,8},{24,16},{9,1},{17,9},{25,17},{10,2},{18,10},{26,18},{... | collective-permute-start | bytes 4325384 | tf_op jit(solution)/shard_map/ppermute | solution.py:725
  92.8 44.3 %collective-permute-start.10 = (bf16[4,64,2816]{2,1,0:T(8,128)(2,1)}, bf16[4,64,2816]{2,1,0:T(8,128)(2,1)}, u32[]{:S(2)}, u32[]{:S(2)}) collective-permute-start(bf16[4,64,2816]{2,1,0:T(8,128)(2,1)} %collective-permute-done.9.refs_1_), channel_id=1, source_target_pairs={{0,8},{8,16},{16,24},{1,9},{9,17},{17,25},{2,10},{10,18},{18,26},{... | collective-permute-start | bytes 4325384 | tf_op jit(solution)/shard_map/ppermute | solution.py:724
  109.8 68.4 %collective-permute-start.5 = (bf16[256,2048]{1,0:T(8,128)(2,1)}, bf16[256,2048]{1,0:T(8,128)(2,1)}, u32[]{:S(2)}, u32[]{:S(2)}) collective-permute-start(bf16[256,2048]{1,0:T(8,128)(2,1)} %bitcast.7), channel_id=1, source_target_pairs={{0,6},{1,7},{2,4},{3,5},{4,2},{5,3},{6,0},{7,1},{8,14},{9,15},{10,... | collective-permute-start | bytes 3145736 | tf_op jit(solution)/shard_map/ppermute | solution.py:664
  114.3 41.6 %copy-start = (f32[256,2560]{1,0:T(8,128)S(1)}, f32[256,2560]{1,0:T(8,128)}, u32[]{:S(2)}) copy-start(f32[256,2560]{1,0:T(8,128)} %fusion.73.k_ref.v_ref.q_ref) | copy-start | bytes 7864324
  118.3 37.7 %copy-start.5 = (f32[256,128]{1,0:T(8,128)S(1)}, f32[256,128]{1,0:T(8,128)}, u32[]{:S(2)}) copy-start(f32[256,128]{1,0:T(8,128)} %copy.48.cos_ref.refs_4_) | copy-start | bytes 393220
  118.6 21.1 %collective-permute-start.2 = (bf16[256,512]{1,0:T(8,128)(2,1)S(1)}, bf16[256,512]{1,0:T(8,128)(2,1)S(1)}, u32[]{:S(2)}, u32[]{:S(2)}) collective-permute-start(bf16[256,512]{1,0:T(8,128)(2,1)S(1)} %copy-done.31), channel_id=1, source_target_pairs={{0,24},{8,16},{16,8},{24,0},{1,25},{9,17},{17,9},{25,1},{2,26},{10... | collective-permute-start | bytes 786440 | tf_op jit(solution)/shard_map/ppermute | solution.py:667
  126.4 23.2 %collective-permute-start.1 = (bf16[256,512]{1,0:T(8,128)(2,1)S(1)}, bf16[256,512]{1,0:T(8,128)(2,1)S(1)}, u32[]{:S(2)}, u32[]{:S(2)}) collective-permute-start(bf16[256,512]{1,0:T(8,128)(2,1)S(1)} %copy-done.31), channel_id=1, source_target_pairs={{0,16},{8,24},{16,0},{24,8},{1,17},{9,25},{17,1},{25,9},{2,18},{10... | collective-permute-start | bytes 786440 | tf_op jit(solution)/shard_map/ppermute | solution.py:667
  137.1 13.9 %collective-permute-start = (bf16[256,512]{1,0:T(8,128)(2,1)S(1)}, bf16[256,512]{1,0:T(8,128)(2,1)S(1)}, u32[]{:S(2)}, u32[]{:S(2)}) collective-permute-start(bf16[256,512]{1,0:T(8,128)(2,1)S(1)} %copy-done.31), channel_id=1, source_target_pairs={{0,8},{8,0},{16,24},{24,16},{1,9},{9,1},{17,25},{25,17},{2,10},{10... | collective-permute-start | bytes 786440 | tf_op jit(solution)/shard_map/ppermute | solution.py:667
  139.7 54.0 %collective-permute-start.4 = (bf16[256,2048]{1,0:T(8,128)(2,1)}, bf16[256,2048]{1,0:T(8,128)(2,1)}, u32[]{:S(2)}, u32[]{:S(2)}) collective-permute-start(bf16[256,2048]{1,0:T(8,128)(2,1)} %bitcast.7), channel_id=1, source_target_pairs={{0,4},{1,5},{2,6},{3,7},{4,0},{5,1},{6,2},{7,3},{8,12},{9,13},{10,... | collective-permute-start | bytes 3145736 | tf_op jit(solution)/shard_map/ppermute | solution.py:664
  149.5 44.2 %collective-permute-start.3 = (bf16[256,2048]{1,0:T(8,128)(2,1)}, bf16[256,2048]{1,0:T(8,128)(2,1)}, u32[]{:S(2)}, u32[]{:S(2)}) collective-permute-start(bf16[256,2048]{1,0:T(8,128)(2,1)} %bitcast.7), channel_id=1, source_target_pairs={{0,2},{1,3},{2,0},{3,1},{4,6},{5,7},{6,4},{7,5},{8,10},{9,11},{10,... | collective-permute-start | bytes 3145736 | tf_op jit(solution)/shard_map/ppermute | solution.py:664
  151.0 42.7 %collective-permute-start.13 = (bf16[4,64,2816]{2,1,0:T(8,128)(2,1)}, bf16[4,64,2816]{2,1,0:T(8,128)(2,1)}, u32[]{:S(2)}, u32[]{:S(2)}) collective-permute-start(bf16[4,64,2816]{2,1,0:T(8,128)(2,1)} %collective-permute-done.10.refs_2_), channel_id=1, source_target_pairs={{0,8},{8,16},{16,24},{1,9},{9,17},{17,25},{2,10},{10,18},{18,26},{... | collective-permute-start | bytes 4325384 | tf_op jit(solution)/shard_map/ppermute | solution.py:756
  178.2 32.9 %collective-permute-start.14 = (bf16[4,64,2816]{2,1,0:T(8,128)(2,1)}, bf16[4,64,2816]{2,1,0:T(8,128)(2,1)S(1)}, u32[]{:S(2)}, u32[]{:S(2)}) collective-permute-start(bf16[4,64,2816]{2,1,0:T(8,128)(2,1)} %collective-permute-done.12.refs_5_), channel_id=1, source_target_pairs={{8,0},{16,8},{24,16},{9,1},{17,9},{25,17},{10,2},{18,10},{26,18},{... | collective-permute-start | bytes 4325384 | tf_op jit(solution)/shard_map/ppermute | solution.py:757
  211.1 52.5 %collective-permute-start.15 = (bf16[4,64,2816]{2,1,0:T(8,128)(2,1)S(1)}, bf16[4,64,2816]{2,1,0:T(8,128)(2,1)}, u32[]{:S(2)}, u32[]{:S(2)}) collective-permute-start(bf16[4,64,2816]{2,1,0:T(8,128)(2,1)S(1)} %copy-done.2), channel_id=1, source_target_pairs={{0,1},{1,0},{2,3},{3,2},{4,5},{5,4},{6,7},{7,6},{8,9},{9,8},{10,11... | collective-permute-start | bytes 4325384 | tf_op jit(solution)/shard_map/ppermute | solution.py:664
  211.1 52.5 %collective-permute-start.16 = (bf16[4,64,2816]{2,1,0:T(8,128)(2,1)}, bf16[4,64,2816]{2,1,0:T(8,128)(2,1)}, u32[]{:S(2)}, u32[]{:S(2)}) collective-permute-start(bf16[4,64,2816]{2,1,0:T(8,128)(2,1)} %collective-permute-done.9.refs_1_), channel_id=1, source_target_pairs={{0,1},{1,0},{2,3},{3,2},{4,5},{5,4},{6,7},{7,6},{8,9},{9,8},{10,11... | collective-permute-start | bytes 4325384 | tf_op jit(solution)/shard_map/ppermute | solution.py:664
  214.9 27.0 %collective-permute-start.27 = (bf16[256,2048]{1,0:T(8,128)(2,1)S(1)}, bf16[256,2048]{1,0:T(8,128)(2,1)S(1)}, u32[]{:S(2)}, u32[]{:S(2)}) collective-permute-start(bf16[256,2048]{1,0:T(8,128)(2,1)S(1)} %copy-done.24), channel_id=1, source_target_pairs={{0,6},{1,7},{2,4},{3,5},{4,2},{5,3},{6,0},{7,1},{8,14},{9,15},{10,... | collective-permute-start | bytes 3145736 | tf_op jit(solution)/shard_map/ppermute | solution.py:664
  215.7 47.3 %collective-permute-start.25 = (bf16[256,2048]{1,0:T(8,128)(2,1)S(1)}, bf16[256,2048]{1,0:T(8,128)(2,1)S(1)}, u32[]{:S(2)}, u32[]{:S(2)}) collective-permute-start(bf16[256,2048]{1,0:T(8,128)(2,1)S(1)} %copy-done.24), channel_id=1, source_target_pairs={{0,4},{1,5},{2,6},{3,7},{4,0},{5,1},{6,2},{7,3},{8,12},{9,13},{10,... | collective-permute-start | bytes 3145736 | tf_op jit(solution)/shard_map/ppermute | solution.py:664
  216.8 46.2 %collective-permute-start.23 = (bf16[256,2048]{1,0:T(8,128)(2,1)S(1)}, bf16[256,2048]{1,0:T(8,128)(2,1)S(1)}, u32[]{:S(2)}, u32[]{:S(2)}) collective-permute-start(bf16[256,2048]{1,0:T(8,128)(2,1)S(1)} %copy-done.24), channel_id=1, source_target_pairs={{0,2},{1,3},{2,0},{3,1},{4,6},{5,7},{6,4},{7,5},{8,10},{9,11},{10,... | collective-permute-start | bytes 3145736 | tf_op jit(solution)/shard_map/ppermute | solution.py:664
  241.8 25.3 %collective-permute-start.17 = (bf16[4,64,2816]{2,1,0:T(8,128)(2,1)}, bf16[4,64,2816]{2,1,0:T(8,128)(2,1)S(1)}, u32[]{:S(2)}, u32[]{:S(2)}) collective-permute-start(bf16[4,64,2816]{2,1,0:T(8,128)(2,1)} %collective-permute-done.10.refs_2_), channel_id=1, source_target_pairs={{0,1},{1,0},{2,3},{3,2},{4,5},{5,4},{6,7},{7,6},{8,9},{9,8},{10,11... | collective-permute-start | bytes 4325384 | tf_op jit(solution)/shard_map/ppermute | solution.py:664
  263.1 4.1 collective-permute-start.18
  263.1 7.6 collective-permute-start.19
  263.6 10.6 %collective-permute-start.20 = (bf16[4,64,2816]{2,1,0:T(8,128)(2,1)}, bf16[4,64,2816]{2,1,0:T(8,128)(2,1)S(1)}, u32[]{:S(2)}, u32[]{:S(2)}) collective-permute-start(bf16[4,64,2816]{2,1,0:T(8,128)(2,1)} %collective-permute-done.12.refs_5_), channel_id=1, source_target_pairs={{0,1},{1,0},{2,3},{3,2},{4,5},{5,4},{6,7},{7,6},{8,9},{9,8},{10,11... | collective-permute-start | bytes 4325384 | tf_op jit(solution)/shard_map/ppermute | solution.py:664
  263.7 10.5 %collective-permute-start.21 = (bf16[4,64,2816]{2,1,0:T(8,128)(2,1)S(1)}, bf16[4,64,2816]{2,1,0:T(8,128)(2,1)S(1)}, u32[]{:S(2)}, u32[]{:S(2)}) collective-permute-start(bf16[4,64,2816]{2,1,0:T(8,128)(2,1)S(1)} %collective-permute-done.14.refs_6_), channel_id=1, source_target_pairs={{0,1},{1,0},{2,3},{3,2},{4,5},{5,4},{6,7},{7,6},{8,9},{9,8},{10,11... | collective-permute-start | bytes 4325384 | tf_op jit(solution)/shard_map/ppermute | solution.py:664
  267.1 265.0 %collective-permute-start.40 = (bf16[256,1024]{1,0:T(8,128)(2,1)}, bf16[256,1024]{1,0:T(8,128)(2,1)}, u32[]{:S(2)}, u32[]{:S(2)}) collective-permute-start(bf16[256,1024]{1,0:T(8,128)(2,1)} %get-tuple-element.132), channel_id=1, source_target_pairs={{0,1},{1,0},{2,3},{3,2},{4,5},{5,4},{6,7},{7,6},{8,9},{9,8},{10,11... | collective-permute-start | bytes 1572872 | tf_op jit(solution)/shard_map/ppermute | solution.py:664
  267.2 258.8 %collective-permute-start.38 = (bf16[256,1024]{1,0:T(8,128)(2,1)}, bf16[256,1024]{1,0:T(8,128)(2,1)}, u32[]{:S(2)}, u32[]{:S(2)}) collective-permute-start(bf16[256,1024]{1,0:T(8,128)(2,1)} %get-tuple-element.142), channel_id=1, source_target_pairs={{0,1},{1,0},{2,3},{3,2},{4,5},{5,4},{6,7},{7,6},{8,9},{9,8},{10,11... | collective-permute-start | bytes 1572872 | tf_op jit(solution)/shard_map/ppermute | solution.py:664
  328.7 28.7 %collective-permute-start.30 = (bf16[256,2048]{1,0:T(8,128)(2,1)S(1)}, bf16[256,2048]{1,0:T(8,128)(2,1)S(1)}, u32[]{:S(2)}, u32[]{:S(2)}) collective-permute-start(bf16[256,2048]{1,0:T(8,128)(2,1)S(1)} %convolution_convert_fusion.5), channel_id=1, source_target_pairs={{0,4},{1,5},{2,6},{3,7},{4,0},{5,1},{6,2},{7,3},{8,12},{9,13},{10,... | collective-permute-start | bytes 3145736 | tf_op jit(solution)/shard_map/ppermute | solution.py:664
  329.6 27.8 %collective-permute-start.29 = (bf16[256,2048]{1,0:T(8,128)(2,1)S(1)}, bf16[256,2048]{1,0:T(8,128)(2,1)S(1)}, u32[]{:S(2)}, u32[]{:S(2)}) collective-permute-start(bf16[256,2048]{1,0:T(8,128)(2,1)S(1)} %convolution_convert_fusion.6), channel_id=1, source_target_pairs={{0,2},{1,3},{2,0},{3,1},{4,6},{5,7},{6,4},{7,5},{8,10},{9,11},{10,... | collective-permute-start | bytes 3145736 | tf_op jit(solution)/shard_map/ppermute | solution.py:664
  368.7 52.0 %collective-permute-start.33 = (bf16[1024,2816]{1,0:T(8,128)(2,1)}, bf16[1024,2816]{1,0:T(8,128)(2,1)}, u32[]{:S(2)}, u32[]{:S(2)}) collective-permute-start(bf16[1024,2816]{1,0:T(8,128)(2,1)} %pad_maximum_fusion), channel_id=1, source_target_pairs={{0,1},{1,0},{2,3},{3,2},{4,5},{5,4},{6,7},{7,6},{8,9},{9,8},{10,11... | collective-permute-start | bytes 17301512 | tf_op jit(solution)/shard_map/ppermute | solution.py:664
  374.3 27.8 %collective-permute-start.34 = (bf16[256,2048]{1,0:T(8,128)(2,1)}, bf16[256,2048]{1,0:T(8,128)(2,1)}, u32[]{:S(2)}, u32[]{:S(2)}) collective-permute-start(bf16[256,2048]{1,0:T(8,128)(2,1)} %convolution_convert_fusion.4), channel_id=1, source_target_pairs={{0,6},{1,7},{2,4},{3,5},{4,2},{5,3},{6,0},{7,1},{8,14},{9,15},{10,... | collective-permute-start | bytes 3145736 | tf_op jit(solution)/shard_map/ppermute | solution.py:664
  396.1 20.5 %collective-permute-start.31 = (bf16[1,704,2048]{2,1,0:T(8,128)(2,1)}, bf16[1,704,2048]{2,1,0:T(8,128)(2,1)S(1)}, u32[]{:S(2)}, u32[]{:S(2)}) collective-permute-start(bf16[1,704,2048]{2,1,0:T(8,128)(2,1)} %dynamic-slice_bitcast_fusion), channel_id=1, source_target_pairs={{0,1},{1,0},{2,3},{3,2},{4,5},{5,4},{6,7},{7,6},{8,9},{9,8},{10,11... | collective-permute-start | bytes 8650760 | tf_op jit(solution)/shard_map/ppermute | solution.py:664
  407.4 19.8 %collective-permute-start.32 = (bf16[1024,1024]{1,0:T(8,128)(2,1)}, bf16[1024,1024]{1,0:T(8,128)(2,1)}, u32[]{:S(2)}, u32[]{:S(2)}) collective-permute-start(bf16[1024,1024]{1,0:T(8,128)(2,1)} %get-tuple-element.112), channel_id=1, source_target_pairs={{0,1},{1,0},{2,3},{3,2},{4,5},{5,4},{6,7},{7,6},{8,9},{9,8},{10,11... | collective-permute-start | bytes 6291464 | tf_op jit(solution)/shard_map/ppermute | solution.py:664
  416.6 64.1 %collective-permute-start.28 = (bf16[256,2048]{1,0:T(8,128)(2,1)}, bf16[256,2048]{1,0:T(8,128)(2,1)S(1)}, u32[]{:S(2)}, u32[]{:S(2)}) collective-permute-start(bf16[256,2048]{1,0:T(8,128)(2,1)} %convolution_convert_fusion.8), channel_id=1, source_target_pairs={{0,6},{1,7},{2,4},{3,5},{4,2},{5,3},{6,0},{7,1},{8,14},{9,15},{10,... | collective-permute-start | bytes 3145736 | tf_op jit(solution)/shard_map/ppermute | solution.py:664
  420.7 61.4 %collective-permute-start.26 = (bf16[256,2048]{1,0:T(8,128)(2,1)S(1)}, bf16[256,2048]{1,0:T(8,128)(2,1)S(1)}, u32[]{:S(2)}, u32[]{:S(2)}) collective-permute-start(bf16[256,2048]{1,0:T(8,128)(2,1)S(1)} %copy-done.47), channel_id=1, source_target_pairs={{0,4},{1,5},{2,6},{3,7},{4,0},{5,1},{6,2},{7,3},{8,12},{9,13},{10,... | collective-permute-start | bytes 3145736 | tf_op jit(solution)/shard_map/ppermute | solution.py:664
  427.3 56.0 %collective-permute-start.24 = (bf16[256,2048]{1,0:T(8,128)(2,1)S(1)}, bf16[256,2048]{1,0:T(8,128)(2,1)S(1)}, u32[]{:S(2)}, u32[]{:S(2)}) collective-permute-start(bf16[256,2048]{1,0:T(8,128)(2,1)S(1)} %copy-done.46), channel_id=1, source_target_pairs={{0,2},{1,3},{2,0},{3,1},{4,6},{5,7},{6,4},{7,5},{8,10},{9,11},{10,... | collective-permute-start | bytes 3145736 | tf_op jit(solution)/shard_map/ppermute | solution.py:664
  480.8 11.1 %collective-permute-start.37 = (bf16[2,256,256]{2,1,0:T(8,128)(2,1)S(1)}, bf16[2,256,256]{2,1,0:T(8,128)(2,1)S(1)}, u32[]{:S(2)}, u32[]{:S(2)}) collective-permute-start(bf16[2,256,256]{2,1,0:T(8,128)(2,1)S(1)} %get-tuple-element.151), channel_id=1, source_target_pairs={{0,24},{8,16},{16,8},{24,0},{1,25},{9,17},{17,9},{25,1},{2,26},{10... | collective-permute-start | bytes 786440 | tf_op jit(solution)/shard_map/ppermute | solution.py:667
  482.1 23.5 %collective-permute-start.36 = (bf16[2,256,256]{2,1,0:T(8,128)(2,1)S(1)}, bf16[2,256,256]{2,1,0:T(8,128)(2,1)S(1)}, u32[]{:S(2)}, u32[]{:S(2)}) collective-permute-start(bf16[2,256,256]{2,1,0:T(8,128)(2,1)S(1)} %get-tuple-element.152), channel_id=1, source_target_pairs={{0,16},{8,24},{16,0},{24,8},{1,17},{9,25},{17,1},{25,9},{2,18},{10... | collective-permute-start | bytes 786440 | tf_op jit(solution)/shard_map/ppermute | solution.py:667
  483.3 22.3 %collective-permute-start.35 = (bf16[2,256,256]{2,1,0:T(8,128)(2,1)S(1)}, bf16[2,256,256]{2,1,0:T(8,128)(2,1)S(1)}, u32[]{:S(2)}, u32[]{:S(2)}) collective-permute-start(bf16[2,256,256]{2,1,0:T(8,128)(2,1)S(1)} %get-tuple-element.153), channel_id=1, source_target_pairs={{0,8},{8,0},{16,24},{24,16},{1,9},{9,1},{17,25},{25,17},{2,10},{10... | collective-permute-start | bytes 786440 | tf_op jit(solution)/shard_map/ppermute | solution.py:667
  491.9 34.0 %collective-permute-start.39 = (bf16[256,2048]{1,0:T(8,128)(2,1)}, bf16[256,2048]{1,0:T(8,128)(2,1)}, u32[]{:S(2)}, u32[]{:S(2)}) collective-permute-start(bf16[256,2048]{1,0:T(8,128)(2,1)} %fusion.64), channel_id=1, source_target_pairs={{0,1},{1,0},{2,3},{3,2},{4,5},{5,4},{6,7},{7,6},{8,9},{9,8},{10,11... | collective-permute-start | bytes 3145736 | tf_op jit(solution)/shard_map/ppermute | solution.py:664
  519.3 12.8 %collective-permute-start.41 = (bf16[256,2560]{1,0:T(8,128)(2,1)}, bf16[256,2560]{1,0:T(8,128)(2,1)S(1)}, u32[]{:S(2)}, u32[]{:S(2)}) collective-permute-start(bf16[256,2560]{1,0:T(8,128)(2,1)} %pad_maximum_fusion.9), channel_id=1, source_target_pairs={{0,1},{1,0},{2,3},{3,2},{4,5},{5,4},{6,7},{7,6},{8,9},{9,8},{10,11... | collective-permute-start | bytes 3932168 | tf_op jit(solution)/shard_map/ppermute | solution.py:664
  519.4 5.8 collective-permute-start.42
  (57 other events, 581.5 us)
Sparse Core Ops, SparseCore 0:
  10.5 80.1 all-gather.2
  92.5 93.4 all-gather.4

commit v2 on v1

--- a/solution.py
+++ b/solution.py
@@ -374,74 +374,251 @@
     out_ref[0, :, part:] = up_ref[...]
 
 
-def pick_columns(order, share, shares, w_gate, w_up):
-    rows, hidden = w_gate.shape[0] // shares, w_gate.shape[1]
+def pick_columns(order, w_gate, w_up):
+    shard, hidden = w_gate.shape
     parts = order.shape[0]
     part = hidden // parts
     if part % 128:
-        both = [
-            lax.dynamic_slice_in_dim(w, share * rows, rows).reshape(rows, parts, part)
-            for w in (w_gate, w_up)
-        ]
-        return jnp.take(jnp.concatenate(both, axis=2).transpose(1, 0, 2), order, axis=0)
-    columns = pl.BlockSpec((rows, part), lambda k, t: (t[parts], t[k]))
+        both = [w.reshape(shard, parts, part).transpose(1, 0, 2) for w in (w_gate, w_up)]
+        return jnp.take(jnp.concatenate(both, axis=2), order, axis=0)
+    columns = pl.BlockSpec((shard, part), lambda k, t: (0, t[k]))
     return pl.pallas_call(
         pick_columns_kernel,
         grid_spec=pltpu.PrefetchScalarGridSpec(
             num_scalar_prefetch=1,
             grid=(parts,),
             in_specs=[columns, columns],
-            out_specs=pl.BlockSpec((1, rows, 2 * part), lambda k, t: (k, 0, 0)),
+            out_specs=pl.BlockSpec((1, shard, 2 * part), lambda k, t: (k, 0, 0)),
         ),
-        out_shape=jax.ShapeDtypeStruct((parts, rows, 2 * part), BF),
+        out_shape=jax.ShapeDtypeStruct((parts, shard, 2 * part), BF),
         name="pick_columns",
-    )(jnp.concatenate([order, share[None]]), w_gate, w_up)
-
-
-def assemble_kernel(nc, *refs):
-    *pieces, out, sems = refs
-    chips = pieces[0].shape[0]
+    )(order, w_gate, w_up)
+
+
+def share_kernel(nf, nc, low, size, *refs):
+    (qkv, picked, down, gains, wqkv, wide, downs, all_gains) = refs[:8]
+    (qkv_own, wide_own, down_own, gains_own) = refs[8:12]
+    (local, plane_send, plane_recv, along_send, along_recv, core_send, core_recv) = refs[12:19]
+    (gain_send, gain_recv, down_sem, qkv_send, qkv_recv, qkv_core) = refs[19:]
+    chips = nf // 2
     place, here = lax.axis_index("fsdp"), lax.axis_index("ctx")
-    chip, core = place // 2, place % 2
-
-    def copies(ref, other, share, at, go):
-        for k in range(chips):
-            owner = 2 * (chip ^ k) + (core ^ other)
-            copy = pltpu.make_async_copy(
-                ref.at[k], out.at[owner, share], sems.at[other, at, k]
-            )
-            if go:
-                copy.start()
-            else:
-                copy.wait()
-
-    for go in (True, False):
-        for other in range(2):
-            mine = pieces[other * (2 * nc - 1) : (other + 1) * (2 * nc - 1)]
-            copies(mine[0], other, here, 0, go)
+    core = place % 2
+    mesh_id = pl.DeviceIdType.MESH
+
+    barrier = pltpu.get_barrier_semaphore()
+
+    def greet(target):
+        pl.semaphore_signal(barrier, inc=1, device_id=target, device_id_type=mesh_id)
+
+    for j in range(1, nf):
+        greet({"fsdp": place ^ j})
+    for pos in range(nc):
+
+        @pl.when(here == pos)
+        def _():
+            near = [i for i in (pos - 1, pos + 1) if 0 <= i < nc]
+            for i in near:
+                greet({"ctx": i})
+            pl.semaphore_wait(barrier, nf - 1 + len(near))
+
+    def remote(source, target, sends, recvs, where):
+        return pltpu.make_async_remote_copy(
+            src_ref=source,
+            dst_ref=target,
+            send_sem=sends,
+            recv_sem=recvs,
+            device_id=where,
+            device_id_type=mesh_id,
+        )
+
+    def rows_of(share):
+        return pl.ds(low + share * size, size)
+
+    def plane_copy(k, kind):
+        rows = rows_of(here) if kind else pl.ds(0, low)
+        return remote(
+            picked.at[k, rows],
+            wide.at[place, rows],
+            plane_send.at[kind, k],
+            plane_recv.at[kind, k],
+            {"fsdp": place ^ (2 * k)},
+        )
+
+    def along_copy(k, share, up, target):
+        block = wide.at[place ^ (2 * k), rows_of(share)]
+        return remote(
+            block, block, along_send.at[up, share, k], along_recv.at[share, k], {"ctx": target}
+        )
+
+    def core_copy(k, share):
+        rows = rows_of(share) if share < nc else pl.ds(0, low)
+        block = wide.at[place ^ (2 * k), rows] if k else wide.at[place]
+        source = block if k else picked.at[0]
+        return remote(
+            source, block, core_send.at[k, share], core_recv.at[k, share], {"fsdp": place ^ 1}
+        )
+
+    half = qkv.shape[0] // 2
+    relayed = chips == 4
+
+    def qkv_copy(k, part=0):
+        if part == 0:
+            source, owner, rows = qkv, place, pl.ds(0, 2 * half)
+        else:
+            owner, rows = place ^ (2 * (3 - k)), pl.ds((2 - k) * half, half)
+            source = wqkv.at[owner, rows]
+        at = 2 * k + part
+        return remote(
+            source,
+            wqkv.at[owner, rows],
+            qkv_send.at[at],
+            qkv_recv.at[at],
+            {"fsdp": place ^ (2 * k)},
+        )
+
+    def qkv_core_copy(k):
+        block = wqkv.at[place ^ (2 * k)]
+        return remote(
+            block if k else qkv, block, qkv_core.at[0, k], qkv_core.at[1, k], {"fsdp": place ^ 1}
+        )
+
+    def down_copy():
+        return remote(down, downs.at[core], down_sem.at[0], down_sem.at[1], {"fsdp": place ^ 1})
+
+    def gain_copy(j):
+        return remote(
+            gains, all_gains.at[place], gain_send.at[j], gain_recv.at[j], {"fsdp": place ^ j}
+        )
+
+    direct = (1, 2) if relayed else tuple(range(1, chips))
+    for k in range(1, chips):
+        plane_copy(k, 1).start()
+    for j in range(1, nf):
+        gain_copy(j).start()
+    core_copy(0, nc).start()
+    qkv_core_copy(0).start()
+    down_copy().start()
+    own = (
+        (qkv, qkv_own, wqkv.at[place]),
+        (picked.at[0], wide_own, wide.at[place]),
+        (down, down_own, downs.at[core]),
+        (gains, gains_own, all_gains.at[place]),
+    )
+    for i, (source, stage, _) in enumerate(own):
+        pltpu.make_async_copy(source, stage, local.at[0, i]).start()
+    for i, (source, stage, target) in enumerate(own):
+        pltpu.make_async_copy(source, stage, local.at[0, i]).wait()
+        pltpu.make_async_copy(stage, target, local.at[1, i]).start()
+
+    for k in range(1, chips):
+        plane_copy(k, 1).wait_send()
+    for k in direct:
+        qkv_copy(k).start()
+
+    for pos in range(nc):
+
+        @pl.when(here == pos)
+        def _():
+            def pass_on(k, share):
+                if share <= pos < nc - 1:
+                    along_copy(k, share, 1, pos + 1).start()
+                if share >= pos > 0:
+                    along_copy(k, share, 0, pos - 1).start()
+                core_copy(k, share).start()
+
+            for k in range(1, chips):
+                plane_copy(k, 1).wait_recv()
+                pass_on(k, pos)
+            if low:
+                for k in range(1, chips):
+                    plane_copy(k, 0).start()
+            for k in direct:
+                qkv_copy(k).wait_recv()
+                if relayed:
+                    qkv_copy(3 - k, 1).start()
+                qkv_core_copy(k).start()
             for d in range(1, nc):
-
-                @pl.when(here >= d)
-                def _():
-                    copies(mine[d], other, here - d, d, go)
-
-                @pl.when(here + d < nc)
-                def _():
-                    copies(mine[nc - 1 + d], other, here + d, nc - 1 + d, go)
-
-
-def assemble(nf, nc, pieces):
-    chips, rows, columns = pieces[0].shape
+                for share in (pos - d, pos + d):
+                    if 0 <= share < nc:
+                        for k in range(1, chips):
+                            along_copy(k, share, 0, 0).wait_recv()
+                            pass_on(k, share)
+            if low:
+                for k in range(1, chips):
+                    plane_copy(k, 0).wait_recv()
+                    core_copy(k, nc).start()
+            if relayed:
+                for k in direct:
+                    qkv_copy(k, 1).wait_recv()
+                qkv_core_copy(3).start()
+            for k in range(1, chips):
+                for share in range(nc):
+                    if share <= pos < nc - 1:
+                        along_copy(k, share, 1, pos + 1).wait_send()
+                    if share >= pos > 0:
+                        along_copy(k, share, 0, pos - 1).wait_send()
+
+    for k in range(chips):
+        for share in range(nc + 1):
+            if (share < nc and k) or (share == nc and (low or not k)):
+                core_copy(k, share).wait_send()
+                core_copy(k, share).wait_recv()
+    if low:
+        for k in range(1, chips):
+            plane_copy(k, 0).wait_send()
+    for j in range(1, nf):
+        gain_copy(j).wait()
+    for k in direct:
+        qkv_copy(k).wait_send()
+        if relayed:
+            qkv_copy(k, 1).wait_send()
+    for k in range(chips):
+        qkv_core_copy(k).wait()
+    down_copy().wait()
+    for i, (_, stage, target) in enumerate(own):
+        pltpu.make_async_copy(stage, target, local.at[1, i]).wait()
+
+
+def share_weights(nf, nc, qkv, picked, down, gains):
+    chips, shard, columns = picked.shape
+    size = 16 * max(1, (shard * 3 // 4) // (16 * nc))
+    low = shard - nc * size
     anywhere = pl.BlockSpec(memory_space=pl.ANY)
+    dma = pltpu.SemaphoreType.DMA
     return pl.pallas_call(
-        functools.partial(assemble_kernel, nc),
-        in_specs=[anywhere] * len(pieces),
-        out_specs=pl.BlockSpec(memory_space=pltpu.VMEM),
-        out_shape=jax.ShapeDtypeStruct((nf, nc, rows, columns), BF),
-        scratch_shapes=[pltpu.SemaphoreType.DMA((2, 2 * nc - 1, chips))],
-        compiler_params=pltpu.CompilerParams(vmem_limit_bytes=24 << 20),
-        name="assemble",
-    )(*pieces)
+        functools.partial(share_kernel, nf, nc, low, size),
+        in_specs=[anywhere] * 4,
+        out_specs=[anywhere] * 4,
+        out_shape=[
+            jax.ShapeDtypeStruct((nf,) + qkv.shape, BF),
+            jax.ShapeDtypeStruct((nf, shard, columns), BF),
+            jax.ShapeDtypeStruct((2,) + down.shape, BF),
+            jax.ShapeDtypeStruct((nf,) + gains.shape, BF),
+        ],
+        scratch_shapes=[
+            pltpu.VMEM(qkv.shape, BF),
+            pltpu.VMEM((shard, columns), BF),
+            pltpu.VMEM(down.shape, BF),
+            pltpu.VMEM(gains.shape, BF),
+            dma((2, 4)),
+            dma((2, chips)),
+            dma((2, chips)),
+            dma((2, nc, chips)),
+            dma((nc, chips)),
+            dma((chips, nc + 1)),
+            dma((chips, nc + 1)),
+            dma((nf,)),
+            dma((nf,)),
+            dma((2,)),
+            dma((2 * chips,)),
+            dma((2 * chips,)),
+            dma((2, chips)),
+        ],
+        compiler_params=pltpu.CompilerParams(
+            collective_id=1, has_side_effects=True, vmem_limit_bytes=56 << 20
+        ),
+        name="share_weights",
+    )(qkv, picked, down, gains)
 
 
 def place_columns_kernel(order, both_ref, gate_ref, up_ref):
@@ -475,8 +652,9 @@
 
 
 def finish_kernel(nf, nc, *refs):
-    sources, outs, owns, ins, xs = (refs[i : i + 5] for i in range(0, 25, 5))
-    plane_send, plane_recv, local, in_sem, x_sem, first_send, second_send, out_sem = refs[25:]
+    pieces, refs = refs[: nf // 2], refs[nf // 2 - 1 :]
+    sources, (outs, owns, ins, xs) = refs[:4], (refs[i : i + 4] for i in range(4, 20, 4))
+    plane_send, plane_recv, local, in_sem, x_sem, first_send, second_send, out_sem = refs[20:]
     chips = nf // 2
     place, here = lax.axis_index("fsdp"), lax.axis_index("ctx")
     chip = place // 2
@@ -512,18 +690,18 @@
             device_id_type=mesh_id,
         )
 
-    def local_copy(u):
-        if u == 0:
-            return pltpu.make_async_copy(sources[0], owns[0], local.at[0])
-        return pltpu.make_async_copy(sources[u].at[chip], owns[u].at[0], local.at[u])
-
-    for u in range(5):
-        local_copy(u).start()
-    for u in range(1, 5):
-        for k in range(1, chips):
-            plane_copy(u, k).start()
-
-    units = [(0, None)] + [(1, k) for k in range(chips)] + [(u, None) for u in (2, 3, 4)]
+    def local_copy(u, k):
+        source = sources[u].at[chip] if u else pieces[k]
+        return pltpu.make_async_copy(source, owns[u].at[k], local.at[u, k])
+
+    for u in range(4):
+        for k in range(chips):
+            if u == 0 or k == 0:
+                local_copy(u, k).start()
+            else:
+                plane_copy(u, k).start()
+
+    units = [(0, k) for k in range(chips)] + [(u, None) for u in (1, 2, 3)]
     chunks = []
     for u, k in units:
         total = outs[u].shape[-2]
@@ -533,8 +711,7 @@
     def views(c):
         u, k, r, size = chunks[c]
         rows = pl.ds(r, size)
-        own = owns[u].at[rows] if u == 0 else owns[u].at[k or 0, rows]
-        return [own] + [
+        return [owns[u].at[k or 0, rows]] + [
             ref.at[rows] if k is None else ref.at[k, rows] for ref in (ins[u], xs[u], outs[u])
         ]
 
@@ -575,14 +752,11 @@
         own, arriving, _, _ = views(c)
         terms = [own]
         if r == 0:
-            if not k:
-                local_copy(u).wait()
-            else:
-                plane_copy(u, k).wait_recv()
-            if u >= 2:
+            local_copy(u, k or 0).wait()
+            if u >= 1:
                 for j in range(1, chips):
                     plane_copy(u, j).wait_recv()
-        if u >= 2:
+        if u >= 1:
             terms += [owns[u].at[j, pl.ds(r, size)] for j in range(1, chips)]
         if level > 0:
             first_copy(c, False).wait_recv()
@@ -624,15 +798,15 @@
             for c in range(count):
                 out_copy(c, False).wait()
 
-    for u in range(1, 5):
+    for u in range(1, 4):
         for k in range(1, chips):
             plane_copy(u, k).wait_send()
 
 
-def finish(nf, nc, down, gate_up, *sums):
+def finish(nf, nc, pieces, sums):
     chips = nf // 2
-    arrays = (down, gate_up) + sums
-    shapes = [down.shape, gate_up.shape] + [x.shape[1:] for x in sums]
+    pieces_shape = (chips,) + pieces[0].shape
+    shapes = [pieces_shape] + [x.shape[1:] for x in sums]
     count = sum(
         (shape[0] if len(shape) == 3 else 1) * (shape[-2] // chunk_rows(shape[-2]))
         for shape in shapes
@@ -641,19 +815,22 @@
     dma = pltpu.SemaphoreType.DMA
     return pl.pallas_call(
         functools.partial(finish_kernel, nf, nc),
-        in_specs=[anywhere] * 5,
-        out_specs=[anywhere] * 5,
+        in_specs=[anywhere] * (chips + 3),
+        out_specs=[anywhere] * 4,
         out_shape=[jax.ShapeDtypeStruct(shape, BF) for shape in shapes],
-        scratch_shapes=[pltpu.VMEM(x.shape, BF) for x in arrays]
+        scratch_shapes=[pltpu.VMEM(x, BF) for x in [pieces_shape] + [x.shape for x in sums]]
         + [pltpu.VMEM(shape, BF) for shape in shapes]
         + [pltpu.VMEM(shape, BF) for shape in shapes]
-        + [dma((5, chips)), dma((5, chips)), dma((5,))]
+        + [dma((4, chips)), dma((4, chips)), dma((4, chips))]
         + [dma((count,))] * 5,
         compiler_params=pltpu.CompilerParams(
-            collective_id=0, has_side_effects=True, vmem_limit_bytes=56 << 20
+            collective_id=0, has_side_effects=True, vmem_limit_bytes=48 << 20
+        ),
+        cost_estimate=pl.CostEstimate(
+            flops=200_000_000_000, bytes_accessed=60_000_000, transcendentals=0
         ),
         name="finish",
-    )(*arrays)
+    )(*pieces, *sums)
 
 
 def solution(mesh):
@@ -662,6 +839,13 @@
 
     def swap(x, k):
         return lax.ppermute(x, "fsdp", [(i, i ^ k) for i in range(nf)])
+
+    def plane_gather(x):
+        if chips != 4:
+            return [swap(x, 2 * k) for k in range(1, chips)]
+        one, two = swap(x, 2), swap(x, 4)
+        half = x.shape[0] // 2
+        return [one, two, jnp.concatenate([swap(one[:half], 4), swap(two[half:], 2)], axis=0)]
 
     def cross(x, k):
         return lax.ppermute(x, "ctx", [(i, i ^ k) for i in range(nc)])
@@ -706,27 +890,23 @@
             right = jnp.concatenate([right, swap(right, 1)], axis=0)
             return dot(left, right, (0, 0)).astype(BF).reshape(chips, shard, right.shape[1])
 
-        gains = lax.all_gather(jnp.stack([attn_gain, ffn_gain]), "fsdp", axis=1, tiled=True)
-        gains = gains.astype(F32)
-        w_qkv = lax.all_gather(
-            jnp.concatenate([w_query, w_key, w_value], axis=1), "fsdp", axis=0, tiled=True
-        )
+
+        order = chip ^ jnp.arange(chips, dtype=jnp.int32)
+        both_gains = jnp.pad(jnp.stack([attn_gain, ffn_gain]), ((0, 14), (0, 0)))
+        w_qkv, w_gu, w_d, gains = share_weights(
+            nf,
+            nc,
+            jnp.concatenate([w_query, w_key, w_value], axis=1),
+            pick_columns(order, w_gate, w_up),
+            w_down,
+            both_gains,
+        )
+        w_out, w_qkv = lax.optimization_barrier((w_out, w_qkv))
         w_o = lax.all_gather(w_out, "fsdp", axis=0, tiled=True)
-
-        order = chip ^ jnp.arange(chips, dtype=jnp.int32)
-        w_gate, w_up, gains = lax.optimization_barrier((w_gate, w_up, gains))
-        gate_up = pick_columns(order, lax.axis_index("ctx"), nc, w_gate, w_up)
-        first = jnp.stack([swap(gate_up[k], 2 * k) if k else gate_up[k] for k in range(chips)])
-        upward = [(i, i + 1) for i in range(nc - 1)]
-        downward = [(i + 1, i) for i in range(nc - 1)]
-        below, above = [first], [first]
-        for _ in range(nc - 2):
-            below.append(lax.ppermute(below[-1], "ctx", upward))
-            above.append(lax.ppermute(above[-1], "ctx", downward))
-        w_d = jnp.zeros((2,) + w_down.shape, BF)
-        w_d = lax.dynamic_update_index_in_dim(w_d, w_down, core, 0)
-        w_d = lax.dynamic_update_index_in_dim(w_d, swap(w_down, 1), 1 - core, 0)
+        w_qkv = w_qkv.reshape(width, -1)
+        w_gu = w_gu.reshape(width, 2 * part)
         w_d = w_d.reshape(part, width)
+        gains = gains[:, :2].astype(F32).transpose(1, 0, 2).reshape(2, width)
 
         half = HEAD_DIM // 2
         frequency = THETA ** (-jnp.arange(half, dtype=F32) * (2.0 / HEAD_DIM))
@@ -750,11 +930,8 @@
         xn = (unit_one * gains[0][None, :]).astype(BF)
         qkv = dot(xn, w_qkv, (1, 0))
         kv = own_keys(qkv, cos_lanes, sin_lanes)
-        sent, _ = lax.optimization_barrier((gb, kv))
-        gb_of = [swap(sent, k) if k else gb for k in range(0, nf, 2)]
-        _, below[-1], above[-1] = lax.optimization_barrier((kv, below[-1], above[-1]))
-        below.append(lax.ppermute(below[-1], "ctx", upward))
-        above.append(lax.ppermute(above[-1], "ctx", downward))
+        sent, _ = lax.optimization_barrier((gb, qkv))
+        gb_of = [gb] + plane_gather(sent)
         kv = jnp.concatenate([cross(kv, k) if k else kv for k in range(nc)], axis=0)
         qr, o, ob, lse = attention_forward(table, qkv, cos_lanes, sin_lanes, kv)
         h1 = x + dot(ob, w_o, (1, 0))
@@ -762,26 +939,20 @@
         unit_two = h1 * inverse_two
         hn = (unit_two * gains[1][None, :]).astype(BF)
 
-        pieces = [first] + below[1:] + above[1:]
-        hn, gb_of, pieces = lax.optimization_barrier((hn, gb_of, pieces))
-        w_gu = assemble(nf, nc, pieces + [swap(piece, 1) for piece in pieces])
-        w_gu = w_gu.reshape(width, 2 * part)
-
-        outs, dhns = [], []
+        hn, gb_of = lax.optimization_barrier((hn, gb_of))
+
+        dhns = []
         hn_of, act_of, dgu_of = [], [], []
-        for k in range(0, nf, 2):
-            hn_k = swap(hn, k) if k else hn
+        for k, hn_k in enumerate([hn] + plane_gather(hn)):
             gu = dot(hn_k, w_gu, (1, 0))
-            dact = dot(gb_of[k // 2], w_d, (1, 1))
+            dact = dot(gb_of[k], w_d, (1, 1))
             gate, up = gu[:, :part], gu[:, part:]
             sg = jax.nn.sigmoid(gate)
             silu = gate * sg
             act = (silu * up).astype(BF)
             dgate = (dact * up * sg * (1.0 + gate * (1.0 - sg))).astype(BF)
             dgu = jnp.concatenate([dgate, (dact * silu).astype(BF)], axis=1)
-            out_k = dot(act, w_d, (1, 0))
             dhn_k = dot(dgu, w_gu, (1, 1))
-            outs.append(out_k.astype(BF) if k else out_k)
             dhns.append(dhn_k.astype(BF) if k else dhn_k)
             hn_of.append(hn_k)
             act_of.append(act)
@@ -796,13 +967,10 @@
 
         gb_all = jnp.concatenate(gb_of, axis=0)
         down = dot(jnp.concatenate(act_of, axis=0), gb_all, (0, 0)).astype(BF)
-        wide = rows_grad(jnp.concatenate(hn_of, axis=0), jnp.concatenate(dgu_of, axis=0))
         down_sum = core_sum(down.reshape((1, 2) + w_down.shape))[0]
-        down_sum, wide, grad_hn = lax.optimization_barrier((down_sum, wide, grad_hn))
-        branch = h1 + outs[0]
-        for k in range(1, chips):
-            branch = branch + swap(outs[k], 2 * k).astype(F32)
-        layer_out = branch.astype(BF)
+        down_sum, grad_hn = lax.optimization_barrier((down_sum, grad_hn))
+        down_sum = lax.psum_scatter(down_sum, "ctx", scatter_dimension=0, tiled=True)
+        hn_all, dgu_all = jnp.concatenate(hn_of, axis=0), jnp.concatenate(dgu_of, axis=0)
 
         gain_two_grad = jnp.sum(grad_hn * unit_two, axis=0)
         grad_unit = grad_hn * gains[1][None, :]
@@ -811,11 +979,28 @@
         )
         dab = dh1.astype(BF)
         dob = dot(dab, w_o, (1, 1)).astype(BF)
-        out_term = rows_grad(ob, dab)
         dq, dkv = attention_backward(table, qr, dob, o, lse, kv, cos_lanes, sin_lanes)
+        act_of, xn, ob, dab, hn_all, dgu_all, _ = lax.optimization_barrier(
+            (act_of, xn, ob, dab, hn_all, dgu_all, dq)
+        )
+        down_sum, hn_all, dgu_all = lax.optimization_barrier((down_sum, hn_all, dgu_all))
+        down_sum = lax.all_gather(down_sum, "ctx", axis=0, tiled=True)
+        wide = rows_grad(hn_all, dgu_all)
+        wide = [
+            lax.dynamic_index_in_dim(wide, chip ^ k, 0, keepdims=False) for k in range(chips)
+        ]
+        act_of, _ = lax.optimization_barrier((act_of, wide))
+        wide = [swap(piece, 2 * k) if k else piece for k, piece in enumerate(wide)]
+        outs = [dot(act, w_d, (1, 0)) for act in act_of]
+        sent = [out.astype(BF) for out in outs[1:]]
         pieces = [dkv[:, k * rows : (k + 1) * rows] for k in range(nc)]
         pieces = [cross(piece, k) if k else piece for k, piece in enumerate(pieces)]
-        dqkv = jnp.concatenate([dq, own_key_grads(pieces, cos_lanes, sin_lanes)], axis=1)
+        out_term = rows_grad(ob, dab)
+        pieces, outs[0], sent, out_term = lax.optimization_barrier(
+            (pieces, outs[0], sent, out_term)
+        )
+        own = own_key_grads(pieces, cos_lanes, sin_lanes)
+        dqkv = jnp.concatenate([dq, own], axis=1)
         grad_xn = dot(dqkv, w_qkv, (1, 1))
         gain_one_grad = jnp.sum(grad_xn * unit_one, axis=0)
         grad_unit = grad_xn * gains[0][None, :]
@@ -829,9 +1014,17 @@
         mine = lax.dynamic_index_in_dim(gains_of, core, 2, keepdims=False)
         gains_of = (mine + swap(other, 1)).transpose(1, 0, 2).reshape(chips, 1, 2 * shard)
         gains_of = jnp.pad(gains_of.astype(BF), ((0, 0), (0, 15), (0, 0)))
-        down_sum, gu_sum, out_sum, qkv_sum, gain_sum = finish(
-            nf, nc, down_sum, wide, out_term, qkv_term, gains_of
-        )
+        wide, down_sum, out_term, qkv_term, outs[0], sent = lax.optimization_barrier(
+            (wide, down_sum, out_term, qkv_term, outs[0], sent)
+        )
+        gu_sum, out_sum, qkv_sum, gain_sum = finish(
+            nf, nc, wide, [out_term, qkv_term, gains_of]
+        )
+        h1, gain_sum = lax.optimization_barrier((h1, gain_sum))
+        branch = h1 + outs[0]
+        for k in range(1, chips):
+            branch = branch + swap(sent[k - 1], 2 * k).astype(F32)
+        layer_out = branch.astype(BF)
         qkv_sum = qkv_sum.astype(F32)
         gain_sum = gain_sum[0].reshape(2, shard).astype(F32)
         gate_grad, up_grad = place_columns(order, gu_sum)

time: 838 us -> 738 us (0.88)
  waiting for transfers between devices: 150 us -> 96.6 us
  starting transfers between devices: 59.7 us -> 29.9 us
  matrix products: 178 us -> 154 us
  Pallas kernels: 331 us -> 350 us
  blocking collectives: 10.3 us -> 0 us
    pallas_call x1, Pallas kernels: 8.38 us -> 89.4 us  [share_weights(): pl.pallas_call(functools.partial(share_kernel, nf, nc, low, size), in_spe...]
    pallas_call x1, Pallas kernels: 264 us -> 200 us  [finish(): pl.pallas_call(functools.partial(finish_kernel, nf, nc), in_specs=[anywhe...]
    ppermute x6 -> x0, waiting for transfers between devices: 50.8 us -> none  [the longest x3 50.8 us: shards(): above.append(lax.ppermute(above[-1], 'ctx', downward))]
    ppermute x6, waiting for transfers between devices: 23.7 us -> 0.02 us  [cross(): return lax.ppermute(x, 'ctx', [(i, i ^ k) for i in range(nc)])]
    dot_general x24, matrix products: 178 us -> 154 us  [dot(): lax.dot_general(left, right, ((contract[:1], contract[1:]), ((), ())), pr...]
    ppermute x6 -> x0, starting transfers between devices: 20.5 us -> none  [the longest x3 16.2 us: shards(): below.append(lax.ppermute(below[-1], 'ctx', upward))]
    ppermute x31 -> x25, waiting for transfers between devices: 68.5 us -> 87.2 us  [swap(): return lax.ppermute(x, 'fsdp', [(i, i ^ k) for i in range(nf)])]
    all_gather x1 -> x0, blocking collectives: 10.3 us -> none  [shards(): lax.all_gather(jnp.stack([attn_gain, ffn_gain]), 'fsdp', axis=1, tiled=True)]
  transfers between devices with their start and end apart: 45 -> 34, of which waited for: 13 -> 10; matrix products, arithmetic and copies ran while one was open for 28% -> 27% of each run, Pallas kernels for 7% -> 35%
where the time goes in v2:
time: 738 us; the launch traced here: 731 us
  Pallas kernels  350 us (47%)
  matrix products  154 us (21%)
  waiting for transfers between devices  96.6 us (13%)
  other arithmetic  50.7 us (7%)
  local copies, waits for them, and re-layouts  34.5 us (5%)
  starting transfers between devices  29.9 us (4%)
  between operations  14.9 us (2%)
    pallas_call x1, Pallas kernels, finish(): pl.pallas_call(functools.partial(finish_kernel, nf, nc), in_specs=[anywhe...  200 us
    dot_general x24, matrix products, dot(): lax.dot_general(left, right, ((contract[:1], contract[1:]), ((), ())), pr...  154 us
    pallas_call x1, Pallas kernels, share_weights(): pl.pallas_call(functools.partial(share_kernel, nf, nc, low, size), in_spe...  89.4 us
    ppermute x25, waiting for transfers between devices, swap(): return lax.ppermute(x, 'fsdp', [(i, i ^ k) for i in range(nf)])  87.2 us
    pallas_call x1, Pallas kernels, attention_backward(): pl.pallas_call(attention_backward_kernel, grid_spec=pltpu.PrefetchScalarG...  22.4 us
    ppermute x25, starting transfers between devices, swap(): return lax.ppermute(x, 'fsdp', [(i, i ^ k) for i in range(nf)])  21.4 us
    pallas_call x1, Pallas kernels, attention_forward(): pl.pallas_call(attention_forward_kernel, grid_spec=pltpu.PrefetchScalarGr...  19.4 us
    unnamed x177, local copies, waits for them, and re-layouts  16.8 us
  transfers between devices with their start and end apart: 34, of which 10 were waited for; matrix products, arithmetic and copies ran while one was open for 27% of the time, Pallas kernels for 35%

profile of v2, /device:TPU:0, one launch (start us, length us, event | category | flops | bytes accessed | tf_op | source)
XLA Modules:
  0.0 731.0 jit_solution(1061297059869754365)
XLA Ops:
  9.7 6.4 pick_columns.1.refs_1_
  17.3 89.4 %share_weights.1 = (bf16[8,256,2560]{2,1,0:T(8,128)(2,1)}, bf16[8,256,2816]{2,1,0:T(8,128)(2,1)}, bf16[2,704,2048]{2,1,0:T(8,128)(2,1)}, bf16[8,16,256]{2,1,0:T(8,128)(2,1)}) custom-call(bf16[256,2560]{1,0:T(8,128)(2,1)} %pad_maximum_fusion.7.refs_0_, bf16[4,256,2816]{2,1,0:T(8,128)(2,1)} %pick_columns.1.refs_1_, bf16[704,2048]{1,0:T(8,128)(2,1)} %refs_2_.1, ...), custom_call_target="tpu_custom_call" | custom-call | tf_op jit(solution)/shard_map/share_weights/pallas_call | solution.py:588
  107.9 8.5 %fusion.57.k_ref.v_ref.q_ref = f32[256,2560]{1,0:T(8,128)} fusion(bf16[2048,2560]{1,0:T(8,128)(2,1)} %bitcast.151, bf16[1,256,2048]{2,1,0:T(8,128)(2,1)S(1)} %copy-done.16, f32[2048]{0:T(1024)S(1)} %bitcast.132, f32[256]{0:T(256)S(1)} %add_rsqrt_fusion.1), kind=kOutput, calls=%fused_computation.107 | convolution fusion | flops 2686451712 | bytes 14164992 | tf_op jit(solution)/shard_map/dot_general | solution.py:27
  122.7 3.0 collective-permute-start.1
  127.6 27.1 %collective-permute-done.3 = bf16[256,2048]{1,0:T(8,128)(2,1)S(1)} collective-permute-done((bf16[256,2048]{1,0:T(8,128)(2,1)S(1)}, bf16[256,2048]{1,0:T(8,128)(2,1)S(1)}, u32[]{:S(2)}, u32[]{:S(2)}) %collective-permute-start.3) | collective-permute-done | bytes 1048608 | tf_op jit(solution)/shard_map/ppermute | solution.py:841
  158.8 19.4 %attention_forward.1 = (bf16[256,2048]{1,0:T(8,128)(2,1)S(1)}, f32[256,2048]{1,0:T(8,128)S(1)}, bf16[256,2048]{1,0:T(8,128)(2,1)S(1)}, f32[4,2,1024]{2,1,0:T(2,128)S(1)}) custom-call(s32[10]{0:T(128)S(1)} %pad_add_fusion.table, f32[256,2560]{1,0:T(8,128)S(1)} %copy-done, f32[256,128]{1,0:T(8,128)S(1)} %copy-done.2, f32[256,128]{1,0:T(8,128)S(1)} %copy-done.1, ...), custom_call_target="tpu_custom_call" | custom-call | flops 4294967296 | bytes 8388608 | tf_op jit(solution)/shard_map/attention_forward/pallas_call | solution.py:154
  180.5 2.4 collective-permute-done.6
  184.0 3.0 all-gather.3.cloned.1.call-done
  187.1 6.0 multiply_reduce_fusion.2
  196.8 3.3 fusion.92
  200.1 3.2 multiply_convert_fusion.8
  203.3 16.8 %collective-permute-done.8 = bf16[256,2048]{1,0:T(8,128)(2,1)S(1)} collective-permute-done((bf16[256,2048]{1,0:T(8,128)(2,1)S(1)}, bf16[256,2048]{1,0:T(8,128)(2,1)S(1)}, u32[]{:S(2)}, u32[]{:S(2)}) %collective-permute-start.8) | collective-permute-done | bytes 1048608 | tf_op jit(solution)/shard_map/ppermute | solution.py:841
  221.6 4.8 fusion.94
  226.5 5.5 multiply_convert_fusion.4
  233.2 8.4 %convolution_convert_fusion.4 = bf16[256,2048]{1,0:T(8,128)(2,1)} fusion(bf16[2048,2816]{1,0:T(8,128)(2,1)} %bitcast.141, bf16[256,1408]{1,0:T(8,128)(2,1)S(1)} %get-tuple-element.170, bf16[256,1408]{1,0:T(8,128)(2,1)S(1)} %get-tuple-element.169), kind=kOutput, calls=%fused_computation.45 | convolution fusion | flops 2956197888 | bytes 14024704 | tf_op jit(solution)/shard_map/dot_general | solution.py:27
  243.8 6.5 fusion.93
  250.3 3.2 multiply_convert_fusion.6
  253.6 8.4 %convolution_convert_fusion.5 = bf16[256,2048]{1,0:T(8,128)(2,1)} fusion(bf16[2048,2816]{1,0:T(8,128)(2,1)} %bitcast.143, bf16[256,1408]{1,0:T(8,128)(2,1)S(1)} %get-tuple-element.172, bf16[256,1408]{1,0:T(8,128)(2,1)S(1)} %get-tuple-element.171), kind=kOutput, calls=%fused_computation.46 | convolution fusion | flops 2956197888 | bytes 14024704 | tf_op jit(solution)/shard_map/dot_general | solution.py:27
  266.0 6.7 fusion.59
  272.7 3.2 multiply_convert_fusion.2
  277.1 8.4 %convolution_convert_fusion.3 = bf16[256,2048]{1,0:T(8,128)(2,1)} fusion(bf16[2048,2816]{1,0:T(8,128)(2,1)} %bitcast.145, bf16[256,1408]{1,0:T(8,128)(2,1)S(1)} %get-tuple-element.168, bf16[256,1408]{1,0:T(8,128)(2,1)S(1)} %get-tuple-element.167), kind=kOutput, calls=%fused_computation.44 | convolution fusion | flops 2956197888 | bytes 14024704 | tf_op jit(solution)/shard_map/dot_general | solution.py:27
  287.4 8.3 %convolution_convert_fusion = bf16[1408,2048]{1,0:T(8,128)(2,1)S(1)} fusion(bf16[256,2048]{1,0:T(8,128)(2,1)S(1)} %copy-done.42, bf16[256,2048]{1,0:T(8,128)(2,1)} %collective-permute-done.4, bf16[256,2048]{1,0:T(8,128)(2,1)S(1)} %copy-done.57, bf16[256,2048]{1,0:T(8,128)(2,1)S(1)} %bitcast.125, bf16[256,1408]{1,0:T(8,128)(2,1)} %get-tuple-element.127, ...), kind=kOutput, calls=%fused_computation.4 | convolution fusion | flops 5936775168 | bytes 12845056 | tf_op jit(solution)/shard_map/dot_general | solution.py:27
  300.0 6.8 fusion.83
  306.8 19.1 %collective-permute-done.14 = bf16[256,2048]{1,0:T(8,128)(2,1)} collective-permute-done((bf16[256,2048]{1,0:T(8,128)(2,1)}, bf16[256,2048]{1,0:T(8,128)(2,1)}, u32[]{:S(2)}, u32[]{:S(2)}) %collective-permute-start.14) | collective-permute-done | bytes 1048608 | tf_op jit(solution)/shard_map/ppermute | solution.py:841
  325.9 3.2 convert_add_fusion.1
  329.1 4.6 fusion.18
  340.6 11.1 %pad_maximum_fusion = bf16[1024,2816]{1,0:T(8,128)(2,1)} fusion(bf16[256,2816]{1,0:T(8,128)(2,1)S(1)} %copy-done.22, bf16[256,2816]{1,0:T(8,128)(2,1)S(1)} %copy-done.21, bf16[256,2816]{1,0:T(8,128)(2,1)S(1)} %copy-done.24, bf16[256,2816]{1,0:T(8,128)(2,1)S(1)} %copy-done.23), kind=kLoop, calls=%fused_computation.5 | loop fusion | flops 23068672 | bytes 11534336 | tf_op jit(solution)/shard_map/concatenate | solution.py:973
  353.5 6.2 convolution_convert_fusion.9.do_ref
  359.8 22.4 %attention_backward.1 = (bf16[256,2048]{1,0:T(8,128)(2,1)S(1)}, bf16[2,1024,256]{2,1,0:T(8,128)(2,1)S(1)}) custom-call(s32[10]{0:T(128)S(1)} %pad_add_fusion.table, bf16[256,2048]{1,0:T(8,128)(2,1)S(1)} %copy-done.10, bf16[256,2048]{1,0:T(8,128)(2,1)S(1)} %convolution_convert_fusion.9.do_ref, f32[256,2048]{1,0:T(8,128)S(1)} %copy-done.8, ...), custom_call_target="tpu_custom_call" | custom-call | flops 10737418240 | bytes 8388608 | tf_op jit(solution)/shard_map/attention_backward/pallas_call | solution.py:280
  383.2 6.3 reduce-scatter.2.cloned.1.call-done
  389.5 2.5 fusion.85
  392.0 2.8 broadcast_select_fusion.1
  400.8 3.7 collective-permute-done.23
  404.5 2.3 collective-permute-start.21
  407.7 5.8 convolution_convert_fusion.2
  413.5 17.9 %fusion.5 = bf16[1024,2816]{1,0:T(8,128)(2,1)S(1)} fusion(bf16[1024,2816]{1,0:T(8,128)(2,1)} %collective-permute-done.16, bf16[1024,2816]{1,0:T(8,128)(2,1)} %pad_maximum_fusion, bf16[1024,1024]{1,0:T(8,128)(2,1)} %collective-permute-done.15, bf16[1024,1024]{1,0:T(8,128)(2,1)} %get-tuple-element.175), kind=kOutput, calls=%fused_computation.9 | convolution fusion | flops 11845500928 | bytes 21495808 | tf_op jit(solution)/shard_map/dot_general | solution.py:27
  436.6 5.6 convolution_convert_fusion.6
  442.2 5.7 convolution_convert_fusion.7
  448.0 2.8 convolution_convert_fusion.8
  450.8 3.1 fusion.95
  456.7 9.0 %fusion.40 = (f32[256]{0:T(256)}, f32[2048]{0:T(1024)}, f32[256,2048]{1,0:T(8,128)}) fusion(bf16[1,256,2048]{2,1,0:T(8,128)(2,1)S(1)} %copy-done.18, f32[2048]{0:T(1024)S(1)} %bitcast.134, f32[256]{0:T(256)} %copy-done.63, bf16[2048,2560]{1,0:T(8,128)(2,1)} %bitcast.152, bf16[256,512]{1,0:T(8,128)(2,1)} %own_key_grads.1, ...), kind=kOutput, calls=%fused_computation.53 | convolution fusion | flops 2690643712 | bytes 14960640 | tf_op jit(solution)/shard_map/dot_general | solution.py:27
  471.5 5.1 fusion.44
  476.6 7.0 convolution_convert_fusion.1
  483.6 15.5 %collective-permute-done.18.refs_2_ = bf16[256,2816]{1,0:T(8,128)(2,1)} collective-permute-done((bf16[256,2816]{1,0:T(8,128)(2,1)}, bf16[256,2816]{1,0:T(8,128)(2,1)}, u32[]{:S(2)}, u32[]{:S(2)}) %collective-permute-start.18) | collective-permute-done | bytes 1441824 | tf_op jit(solution)/shard_map/ppermute | solution.py:841
  502.6 200.1 %finish.1 = (bf16[4,256,2816]{2,1,0:T(8,128)(2,1)}, bf16[256,2048]{1,0:T(8,128)(2,1)S(1)}, bf16[256,2560]{1,0:T(8,128)(2,1)S(1)}, bf16[16,512]{1,0:T(8,128)(2,1)S(1)}) custom-call(bf16[256,2816]{1,0:T(8,128)(2,1)S(1)} %get-tuple-element.140.refs_0_, bf16[256,2816]{1,0:T(8,128)(2,1)} %collective-permute-done.17.refs_1_, ...), custom_call_target="tpu_custom_call" | custom-call | flops 199999995904 | bytes 60000000 | tf_op jit(solution)/shard_map/finish/pallas_call | solution.py:816
  703.6 8.1 %place_columns.1 = (f32[256,5632]{1,0:T(8,128)}, f32[256,5632]{1,0:T(8,128)}) custom-call(s32[4]{0:T(128)} %iota_xor_fusion.order, bf16[4,256,2816]{2,1,0:T(8,128)(2,1)} %get-tuple-element.155.both_ref), custom_call_target="tpu_custom_call" | custom-call | tf_op jit(solution)/shard_map/place_columns/pallas_call | solution.py:637
  715.9 3.3 convert_element_type.232
  720.6 3.6 fusion.55
  (304 shorter events, 80.7 us)
Async XLA Ops:
  7.2 179.9 %all-gather.3.cloned.1.call-start = ((), (), s32[]{:S(2)}) async-start(), calls=%async_computation.1 | async-start | bytes 9437184 | tf_op jit(solution)/shard_map/all_gather | solution.py:905
  17.3 89.5 %copy-start.16 = (bf16[1,256,2048]{2,1,0:T(8,128)(2,1)S(1)}, bf16[1,256,2048]{2,1,0:T(8,128)(2,1)}, u32[]{:S(2)}) copy-start(bf16[1,256,2048]{2,1,0:T(8,128)(2,1)} %param.13) | copy-start | bytes 3145732
  106.7 282.8 %reduce-scatter.2.cloned.1.call-start = ((), (), s32[]{:S(2)}) async-start(), calls=%async_computation.2 | async-start | bytes 3604480 | tf_op jit(solution)/shard_map/reduce_scatter | solution.py:972
  107.0 226.7 %copy-start.63 = (f32[256]{0:T(256)}, f32[256]{0:T(256)S(1)}, u32[]{:S(2)}) copy-start(f32[256]{0:T(256)S(1)} %add_rsqrt_fusion.1) | copy-start | bytes 3076
  116.3 38.4 %collective-permute-start.3 = (bf16[256,2048]{1,0:T(8,128)(2,1)S(1)}, bf16[256,2048]{1,0:T(8,128)(2,1)S(1)}, u32[]{:S(2)}, u32[]{:S(2)}) collective-permute-start(bf16[256,2048]{1,0:T(8,128)(2,1)S(1)} %bitcast.122), channel_id=1, source_target_pairs={{0,2},{1,3},{2,0},{3,1},{4,6},{5,7},{6,4},{7,5},{8,10},{9,11},{10,... | collective-permute-start | bytes 3145736 | tf_op jit(solution)/shard_map/ppermute | solution.py:841
  117.4 38.9 %collective-permute-start.4 = (bf16[256,2048]{1,0:T(8,128)(2,1)S(1)}, bf16[256,2048]{1,0:T(8,128)(2,1)}, u32[]{:S(2)}, u32[]{:S(2)}) collective-permute-start(bf16[256,2048]{1,0:T(8,128)(2,1)S(1)} %bitcast.123), channel_id=1, source_target_pairs={{0,4},{1,5},{2,6},{3,7},{4,0},{5,1},{6,2},{7,3},{8,12},{9,13},{10,... | collective-permute-start | bytes 3145736 | tf_op jit(solution)/shard_map/ppermute | solution.py:841
  122.7 35.9 %copy-start.46 = (bf16[256,512]{1,0:T(8,128)(2,1)S(1)}, bf16[256,512]{1,0:T(8,128)(2,1)}, u32[]{:S(2)}) copy-start(bf16[256,512]{1,0:T(8,128)(2,1)} %own_keys.1) | copy-start | bytes 786436
  122.7 35.9 %collective-permute-start = (bf16[256,512]{1,0:T(8,128)(2,1)}, bf16[256,512]{1,0:T(8,128)(2,1)S(1)}, u32[]{:S(2)}, u32[]{:S(2)}) collective-permute-start(bf16[256,512]{1,0:T(8,128)(2,1)} %own_keys.1), channel_id=1, source_target_pairs={{0,8},{8,0},{16,24},{24,16},{1,9},{9,1},{17,25},{25,17},{2,10},{10... | collective-permute-start | bytes 786440 | tf_op jit(solution)/shard_map/ppermute | solution.py:851
  122.7 35.9 %collective-permute-start.1 = (bf16[256,512]{1,0:T(8,128)(2,1)}, bf16[256,512]{1,0:T(8,128)(2,1)S(1)}, u32[]{:S(2)}, u32[]{:S(2)}) collective-permute-start(bf16[256,512]{1,0:T(8,128)(2,1)} %own_keys.1), channel_id=1, source_target_pairs={{0,16},{8,24},{16,0},{24,8},{1,17},{9,25},{17,1},{25,9},{2,18},{10... | collective-permute-start | bytes 786440 | tf_op jit(solution)/shard_map/ppermute | solution.py:851
  125.8 32.9 %collective-permute-start.2 = (bf16[256,512]{1,0:T(8,128)(2,1)}, bf16[256,512]{1,0:T(8,128)(2,1)S(1)}, u32[]{:S(2)}, u32[]{:S(2)}) collective-permute-start(bf16[256,512]{1,0:T(8,128)(2,1)} %own_keys.1), channel_id=1, source_target_pairs={{0,24},{8,16},{16,8},{24,0},{1,25},{9,17},{17,9},{25,1},{2,26},{10... | collective-permute-start | bytes 786440 | tf_op jit(solution)/shard_map/ppermute | solution.py:851
  127.6 31.1 %copy-start = (f32[256,2560]{1,0:T(8,128)S(1)}, f32[256,2560]{1,0:T(8,128)}, u32[]{:S(2)}) copy-start(f32[256,2560]{1,0:T(8,128)} %fusion.57.k_ref.v_ref.q_ref) | copy-start | bytes 7864324
  127.6 31.1 %copy-start.1 = (f32[256,128]{1,0:T(8,128)S(1)}, f32[256,128]{1,0:T(8,128)}, u32[]{:S(2)}) copy-start(f32[256,128]{1,0:T(8,128)} %copy.49.sin_ref.refs_5_) | copy-start | bytes 393220
  127.6 31.2 %copy-start.2 = (f32[256,128]{1,0:T(8,128)S(1)}, f32[256,128]{1,0:T(8,128)}, u32[]{:S(2)}) copy-start(f32[256,128]{1,0:T(8,128)} %copy.48.cos_ref.refs_4_) | copy-start | bytes 393220
  154.7 25.7 %collective-permute-start.5 = (bf16[128,2048]{1,0:T(8,128)(2,1)S(1)}, bf16[128,2048]{1,0:T(8,128)(2,1)S(1)}, u32[]{:S(2)}, u32[]{:S(2)}) collective-permute-start(bf16[128,2048]{1,0:T(8,128)(2,1)S(1)} %slice.204), channel_id=1, source_target_pairs={{0,4},{1,5},{2,6},{3,7},{4,0},{5,1},{6,2},{7,3},{8,12},{9,13},{10,... | collective-permute-start | bytes 1572872 | tf_op jit(solution)/shard_map/ppermute | solution.py:841
  157.4 25.5 %collective-permute-start.6 = (bf16[128,2048]{1,0:T(8,128)(2,1)S(1)}, bf16[128,2048]{1,0:T(8,128)(2,1)S(1)}, u32[]{:S(2)}, u32[]{:S(2)}) collective-permute-start(bf16[128,2048]{1,0:T(8,128)(2,1)S(1)} %slice.205), channel_id=1, source_target_pairs={{0,2},{1,3},{2,0},{3,1},{4,6},{5,7},{6,4},{7,5},{8,10},{9,11},{10,... | collective-permute-start | bytes 1572872 | tf_op jit(solution)/shard_map/ppermute | solution.py:841
  193.1 159.2 %copy-start.61 = (f32[256]{0:T(256)}, f32[256]{0:T(256)S(1)}, u32[]{:S(2)}) copy-start(f32[256]{0:T(256)S(1)} %add_rsqrt_fusion) | copy-start | bytes 3076
  194.6 25.4 %collective-permute-start.8 = (bf16[256,2048]{1,0:T(8,128)(2,1)S(1)}, bf16[256,2048]{1,0:T(8,128)(2,1)S(1)}, u32[]{:S(2)}, u32[]{:S(2)}) collective-permute-start(bf16[256,2048]{1,0:T(8,128)(2,1)S(1)} %multiply_convert_fusion), channel_id=1, source_target_pairs={{0,4},{1,5},{2,6},{3,7},{4,0},{5,1},{6,2},{7,3},{8,12},{9,13},{10,... | collective-permute-start | bytes 3145736 | tf_op jit(solution)/shard_map/ppermute | solution.py:841
  195.3 46.3 %collective-permute-start.7 = (bf16[256,2048]{1,0:T(8,128)(2,1)S(1)}, bf16[256,2048]{1,0:T(8,128)(2,1)S(1)}, u32[]{:S(2)}, u32[]{:S(2)}) collective-permute-start(bf16[256,2048]{1,0:T(8,128)(2,1)S(1)} %multiply_convert_fusion), channel_id=1, source_target_pairs={{0,2},{1,3},{2,0},{3,1},{4,6},{5,7},{6,4},{7,5},{8,10},{9,11},{10,... | collective-permute-start | bytes 3145736 | tf_op jit(solution)/shard_map/ppermute | solution.py:841
  203.3 59.3 %copy-start.47 = (bf16[256,1408]{1,0:T(8,128)(2,1)}, bf16[256,1408]{1,0:T(8,128)(2,1)S(1)}, u32[]{:S(2)}) copy-start(bf16[256,1408]{1,0:T(8,128)(2,1)S(1)} %get-tuple-element.173) | copy-start | bytes 2162692
  203.3 59.3 %copy-start.48 = (bf16[256,1408]{1,0:T(8,128)(2,1)}, bf16[256,1408]{1,0:T(8,128)(2,1)S(1)}, u32[]{:S(2)}) copy-start(bf16[256,1408]{1,0:T(8,128)(2,1)S(1)} %get-tuple-element.174) | copy-start | bytes 2162692
  220.1 44.4 %collective-permute-start.10 = (bf16[128,2048]{1,0:T(8,128)(2,1)S(1)}, bf16[128,2048]{1,0:T(8,128)(2,1)S(1)}, u32[]{:S(2)}, u32[]{:S(2)}) collective-permute-start(bf16[128,2048]{1,0:T(8,128)(2,1)S(1)} %slice.213), channel_id=1, source_target_pairs={{0,2},{1,3},{2,0},{3,1},{4,6},{5,7},{6,4},{7,5},{8,10},{9,11},{10,... | collective-permute-start | bytes 1572872 | tf_op jit(solution)/shard_map/ppermute | solution.py:841
  241.7 22.8 %collective-permute-start.9 = (bf16[128,2048]{1,0:T(8,128)(2,1)S(1)}, bf16[128,2048]{1,0:T(8,128)(2,1)S(1)}, u32[]{:S(2)}, u32[]{:S(2)}) collective-permute-start(bf16[128,2048]{1,0:T(8,128)(2,1)S(1)} %slice.212), channel_id=1, source_target_pairs={{0,4},{1,5},{2,6},{3,7},{4,0},{5,1},{6,2},{7,3},{8,12},{9,13},{10,... | collective-permute-start | bytes 1572872 | tf_op jit(solution)/shard_map/ppermute | solution.py:841
  242.3 43.2 %collective-permute-start.12 = (bf16[256,2048]{1,0:T(8,128)(2,1)}, bf16[256,2048]{1,0:T(8,128)(2,1)S(1)}, u32[]{:S(2)}, u32[]{:S(2)}) collective-permute-start(bf16[256,2048]{1,0:T(8,128)(2,1)} %convolution_convert_fusion.4), channel_id=1, source_target_pairs={{0,4},{1,5},{2,6},{3,7},{4,0},{5,1},{6,2},{7,3},{8,12},{9,13},{10,... | collective-permute-start | bytes 3145736 | tf_op jit(solution)/shard_map/ppermute | solution.py:841
  262.0 24.4 %collective-permute-start.11 = (bf16[256,2048]{1,0:T(8,128)(2,1)}, bf16[256,2048]{1,0:T(8,128)(2,1)S(1)}, u32[]{:S(2)}, u32[]{:S(2)}) collective-permute-start(bf16[256,2048]{1,0:T(8,128)(2,1)} %convolution_convert_fusion.5), channel_id=1, source_target_pairs={{0,2},{1,3},{2,0},{3,1},{4,6},{5,7},{6,4},{7,5},{8,10},{9,11},{10,... | collective-permute-start | bytes 3145736 | tf_op jit(solution)/shard_map/ppermute | solution.py:841
  299.1 29.9 %collective-permute-start.13 = (bf16[1,704,2048]{2,1,0:T(8,128)(2,1)}, bf16[1,704,2048]{2,1,0:T(8,128)(2,1)}, u32[]{:S(2)}, u32[]{:S(2)}) collective-permute-start(bf16[1,704,2048]{2,1,0:T(8,128)(2,1)} %dynamic-slice_bitcast_fusion), channel_id=1, source_target_pairs={{0,1},{1,0},{2,3},{3,2},{4,5},{5,4},{6,7},{7,6},{8,9},{9,8},{10,11... | collective-permute-start | bytes 8650760 | tf_op jit(solution)/shard_map/ppermute | solution.py:841
  299.1 26.8 %collective-permute-start.14 = (bf16[256,2048]{1,0:T(8,128)(2,1)}, bf16[256,2048]{1,0:T(8,128)(2,1)}, u32[]{:S(2)}, u32[]{:S(2)}) collective-permute-start(bf16[256,2048]{1,0:T(8,128)(2,1)} %convolution_convert_fusion.3), channel_id=1, source_target_pairs={{0,6},{1,7},{2,4},{3,5},{4,2},{5,3},{6,0},{7,1},{8,14},{9,15},{10,... | collective-permute-start | bytes 3145736 | tf_op jit(solution)/shard_map/ppermute | solution.py:841
  300.0 25.9 %copy-start.38 = (bf16[256,2048]{1,0:T(8,128)(2,1)S(1)}, bf16[256,2048]{1,0:T(8,128)(2,1)}, u32[]{:S(2)}) copy-start(bf16[256,2048]{1,0:T(8,128)(2,1)} %copy-done.37) | copy-start | bytes 3145732
  300.0 25.9 %copy-start.40 = (bf16[256,2048]{1,0:T(8,128)(2,1)S(1)}, bf16[256,2048]{1,0:T(8,128)(2,1)}, u32[]{:S(2)}) copy-start(bf16[256,2048]{1,0:T(8,128)(2,1)} %copy-done.39) | copy-start | bytes 3145732
  306.8 22.3 %copy-start.20 = (bf16[1408,2048]{1,0:T(8,128)(2,1)S(1)}, bf16[1408,2048]{1,0:T(8,128)(2,1)}, u32[]{:S(2)}) copy-start(bf16[1408,2048]{1,0:T(8,128)(2,1)} %copy-done.19) | copy-start | bytes 17301508
  333.7 149.9 %all-gather.5.cloned.1.call-start = ((), (), s32[]{:S(2)}) async-start(), calls=%async_computation.3 | async-start | bytes 3604480 | tf_op jit(solution)/shard_map/all_gather | solution.py:987
  340.6 11.1 %copy-start.15 = (f32[256,2048]{1,0:T(8,128)S(1)}, f32[256,2048]{1,0:T(8,128)}, u32[]{:S(2)}) copy-start(f32[256,2048]{1,0:T(8,128)} %convert_add_fusion.1) | copy-start | bytes 6291460
  389.5 24.0 %collective-permute-start.16 = (bf16[1024,2816]{1,0:T(8,128)(2,1)}, bf16[1024,2816]{1,0:T(8,128)(2,1)}, u32[]{:S(2)}, u32[]{:S(2)}) collective-permute-start(bf16[1024,2816]{1,0:T(8,128)(2,1)} %pad_maximum_fusion), channel_id=1, source_target_pairs={{0,1},{1,0},{2,3},{3,2},{4,5},{5,4},{6,7},{7,6},{8,9},{9,8},{10,11... | collective-permute-start | bytes 17301512 | tf_op jit(solution)/shard_map/ppermute | solution.py:841
  394.7 18.8 %collective-permute-start.15 = (bf16[1024,1024]{1,0:T(8,128)(2,1)}, bf16[1024,1024]{1,0:T(8,128)(2,1)}, u32[]{:S(2)}, u32[]{:S(2)}) collective-permute-start(bf16[1024,1024]{1,0:T(8,128)(2,1)} %get-tuple-element.176), channel_id=1, source_target_pairs={{0,1},{1,0},{2,3},{3,2},{4,5},{5,4},{6,7},{7,6},{8,9},{9,8},{10,11... | collective-permute-start | bytes 6291464 | tf_op jit(solution)/shard_map/ppermute | solution.py:841
  395.2 11.5 %collective-permute-start.24 = (bf16[256,2048]{1,0:T(8,128)(2,1)S(1)}, bf16[256,2048]{1,0:T(8,128)(2,1)}, u32[]{:S(2)}, u32[]{:S(2)}) collective-permute-start(bf16[256,2048]{1,0:T(8,128)(2,1)S(1)} %copy-done.45), channel_id=1, source_target_pairs={{0,1},{1,0},{2,3},{3,2},{4,5},{5,4},{6,7},{7,6},{8,9},{9,8},{10,11... | collective-permute-start | bytes 3145736 | tf_op jit(solution)/shard_map/ppermute | solution.py:841
  396.5 8.0 %collective-permute-start.23 = (bf16[256,1024]{1,0:T(8,128)(2,1)}, bf16[256,1024]{1,0:T(8,128)(2,1)}, u32[]{:S(2)}, u32[]{:S(2)}) collective-permute-start(bf16[256,1024]{1,0:T(8,128)(2,1)} %get-tuple-element.202), channel_id=1, source_target_pairs={{0,1},{1,0},{2,3},{3,2},{4,5},{5,4},{6,7},{7,6},{8,9},{9,8},{10,11... | collective-permute-start | bytes 1572872 | tf_op jit(solution)/shard_map/ppermute | solution.py:841
  398.0 55.9 %collective-permute-start.20 = (bf16[2,256,256]{2,1,0:T(8,128)(2,1)}, bf16[2,256,256]{2,1,0:T(8,128)(2,1)}, u32[]{:S(2)}, u32[]{:S(2)}) collective-permute-start(bf16[2,256,256]{2,1,0:T(8,128)(2,1)} %get-tuple-element.213), channel_id=1, source_target_pairs={{0,8},{8,0},{16,24},{24,16},{1,9},{9,1},{17,25},{25,17},{2,10},{10... | collective-permute-start | bytes 786440 | tf_op jit(solution)/shard_map/ppermute | solution.py:851
  404.5 50.0 %collective-permute-start.21 = (bf16[2,256,256]{2,1,0:T(8,128)(2,1)}, bf16[2,256,256]{2,1,0:T(8,128)(2,1)}, u32[]{:S(2)}, u32[]{:S(2)}) collective-permute-start(bf16[2,256,256]{2,1,0:T(8,128)(2,1)} %get-tuple-element.212), channel_id=1, source_target_pairs={{0,16},{8,24},{16,0},{24,8},{1,17},{9,25},{17,1},{25,9},{2,18},{10... | collective-permute-start | bytes 786440 | tf_op jit(solution)/shard_map/ppermute | solution.py:851
  406.8 47.7 %collective-permute-start.22 = (bf16[2,256,256]{2,1,0:T(8,128)(2,1)}, bf16[2,256,256]{2,1,0:T(8,128)(2,1)}, u32[]{:S(2)}, u32[]{:S(2)}) collective-permute-start(bf16[2,256,256]{2,1,0:T(8,128)(2,1)} %get-tuple-element.211), channel_id=1, source_target_pairs={{0,24},{8,16},{16,8},{24,0},{1,25},{9,17},{17,9},{25,1},{2,26},{10... | collective-permute-start | bytes 786440 | tf_op jit(solution)/shard_map/ppermute | solution.py:851
  433.6 50.0 %collective-permute-start.17 = (bf16[256,2816]{1,0:T(8,128)(2,1)}, bf16[256,2816]{1,0:T(8,128)(2,1)}, u32[]{:S(2)}, u32[]{:S(2)}) collective-permute-start(bf16[256,2816]{1,0:T(8,128)(2,1)} %get-tuple-element.165), channel_id=1, source_target_pairs={{0,2},{1,3},{2,0},{3,1},{4,6},{5,7},{6,4},{7,5},{8,10},{9,11},{10,... | collective-permute-start | bytes 4325384 | tf_op jit(solution)/shard_map/ppermute | solution.py:841
  435.1 64.0 %collective-permute-start.18 = (bf16[256,2816]{1,0:T(8,128)(2,1)}, bf16[256,2816]{1,0:T(8,128)(2,1)}, u32[]{:S(2)}, u32[]{:S(2)}) collective-permute-start(bf16[256,2816]{1,0:T(8,128)(2,1)} %get-tuple-element.164), channel_id=1, source_target_pairs={{0,4},{1,5},{2,6},{3,7},{4,0},{5,1},{6,2},{7,3},{8,12},{9,13},{10,... | collective-permute-start | bytes 4325384 | tf_op jit(solution)/shard_map/ppermute | solution.py:841
  436.6 11.4 %slice-start.9 = ((s8[5767168]{0:T(1024)(128)(4,1)}), s8[4194304]{0:T(1024)(128)(4,1)S(1)}, s32[]{:S(2)}) async-start(s8[5767168]{0:T(1024)(128)(4,1)} %bitcast.165), calls=%async_computation.13 | async-start | bytes 8388608
  453.9 45.2 %collective-permute-start.19 = (bf16[256,2816]{1,0:T(8,128)(2,1)}, bf16[256,2816]{1,0:T(8,128)(2,1)}, u32[]{:S(2)}, u32[]{:S(2)}) collective-permute-start(bf16[256,2816]{1,0:T(8,128)(2,1)} %get-tuple-element.163), channel_id=1, source_target_pairs={{0,6},{1,7},{2,4},{3,5},{4,2},{5,3},{6,0},{7,1},{8,14},{9,15},{10,... | collective-permute-start | bytes 4325384 | tf_op jit(solution)/shard_map/ppermute | solution.py:841
  468.2 8.4 %collective-permute-start.26 = (bf16[256,2560]{1,0:T(8,128)(2,1)S(1)}, bf16[256,2560]{1,0:T(8,128)(2,1)S(1)}, u32[]{:S(2)}, u32[]{:S(2)}) collective-permute-start(bf16[256,2560]{1,0:T(8,128)(2,1)S(1)} %pad_maximum_fusion.8), channel_id=1, source_target_pairs={{0,1},{1,0},{2,3},{3,2},{4,5},{5,4},{6,7},{7,6},{8,9},{9,8},{10,11... | collective-permute-start | bytes 3932168 | tf_op jit(solution)/shard_map/ppermute | solution.py:841
  469.0 2.3 collective-permute-start.27
  471.3 5.3 collective-permute-start.25
  499.1 221.5 %collective-permute-start.28 = (bf16[256,2048]{1,0:T(8,128)(2,1)}, bf16[256,2048]{1,0:T(8,128)(2,1)}, u32[]{:S(2)}, u32[]{:S(2)}) collective-permute-start(bf16[256,2048]{1,0:T(8,128)(2,1)} %convolution_convert_fusion.8), channel_id=1, source_target_pairs={{0,2},{1,3},{2,0},{3,1},{4,6},{5,7},{6,4},{7,5},{8,10},{9,11},{10,... | collective-permute-start | bytes 3145736 | tf_op jit(solution)/shard_map/ppermute | solution.py:841
  500.3 220.3 %collective-permute-start.29 = (bf16[256,2048]{1,0:T(8,128)(2,1)}, bf16[256,2048]{1,0:T(8,128)(2,1)}, u32[]{:S(2)}, u32[]{:S(2)}) collective-permute-start(bf16[256,2048]{1,0:T(8,128)(2,1)} %convolution_convert_fusion.7), channel_id=1, source_target_pairs={{0,4},{1,5},{2,6},{3,7},{4,0},{5,1},{6,2},{7,3},{8,12},{9,13},{10,... | collective-permute-start | bytes 3145736 | tf_op jit(solution)/shard_map/ppermute | solution.py:841
  501.1 219.5 %collective-permute-start.30 = (bf16[256,2048]{1,0:T(8,128)(2,1)}, bf16[256,2048]{1,0:T(8,128)(2,1)}, u32[]{:S(2)}, u32[]{:S(2)}) collective-permute-start(bf16[256,2048]{1,0:T(8,128)(2,1)} %convolution_convert_fusion.6), channel_id=1, source_target_pairs={{0,6},{1,7},{2,4},{3,5},{4,2},{5,3},{6,0},{7,1},{8,14},{9,15},{10,... | collective-permute-start | bytes 3145736 | tf_op jit(solution)/shard_map/ppermute | solution.py:841
  (71 other events, 345.8 us)
Sparse Core Ops, SparseCore 0:
  106.8 80.1 all-gather.2
  333.8 55.6 reduce-scatter.1
  413.6 63.9 all-gather.4

commit v3 on v2

--- a/solution.py
+++ b/solution.py
@@ -19,6 +19,7 @@
 THETA = 10000.0
 NEG = -1e30
 FLIGHT = 2
+USED = (0, 1, 2, 3)
 BF = jnp.bfloat16
 F32 = jnp.float32
 
@@ -326,31 +327,53 @@
     kv_ref[:, width:] = v_ref[...].astype(BF)
 
 
-def own_keys(qkv, cosine, sine):
-    rows, width = qkv.shape[0], KV_HEADS * HEAD_DIM
-    at = HEADS * HEAD_DIM // width
+def own_keys(kv, cosine, sine):
+    rows, width = kv.shape[0], KV_HEADS * HEAD_DIM
     whole = pl.BlockSpec((rows, LANES), lambda i: (0, 0))
     return pl.pallas_call(
         own_keys_kernel,
         grid=(1,),
         in_specs=[
-            pl.BlockSpec((rows, width), lambda i: (0, at)),
-            pl.BlockSpec((rows, width), lambda i: (0, at + 1)),
+            pl.BlockSpec((rows, width), lambda i: (0, 0)),
+            pl.BlockSpec((rows, width), lambda i: (0, 1)),
             whole,
             whole,
         ],
         out_specs=pl.BlockSpec((rows, 2 * width), lambda i: (0, 0)),
         out_shape=jax.ShapeDtypeStruct((rows, 2 * width), BF),
         name="own_keys",
-    )(qkv, qkv, cosine, sine)
-
-
-def own_key_grads_kernel(*refs):
-    *pieces, cos_ref, sin_ref, out_ref = refs
-    width = out_ref.shape[1] // 2
+    )(kv, kv, cosine, sine)
+
+
+def own_key_grads_kernel(nc, dkv_ref, cos_ref, sin_ref, out_ref, got, send_sem, recv_sem):
+    rows, width = out_ref.shape[0], out_ref.shape[1] // 2
+    here = lax.axis_index("ctx")
+    mesh_id = pl.DeviceIdType.MESH
+    barrier = pltpu.get_barrier_semaphore()
+    for k in range(1, nc):
+        pl.semaphore_signal(barrier, inc=1, device_id={"ctx": here ^ k}, device_id_type=mesh_id)
+    pl.semaphore_wait(barrier, nc - 1)
+
+    def copy(k):
+        source = dkv_ref.at[:, pl.ds(k * rows, rows)]
+        if k == 0:
+            return pltpu.make_async_copy(source, got.at[0], recv_sem.at[0])
+        return pltpu.make_async_remote_copy(
+            src_ref=source,
+            dst_ref=got.at[k],
+            send_sem=send_sem.at[k],
+            recv_sem=recv_sem.at[k],
+            device_id={"ctx": here ^ k},
+            device_id_type=mesh_id,
+        )
+
+    for k in reversed(range(nc)):
+        copy(k).start()
+    for k in range(nc):
+        copy(k).wait()
 
     def total(i, lanes):
-        return sum(piece[i, :, lanes].astype(F32) for piece in pieces)
+        return sum(got[k, i, :, lanes].astype(F32) for k in range(nc))
 
     for p in range(width // LANES):
         lanes = slice(p * LANES, (p + 1) * LANES)
@@ -359,51 +382,45 @@
         out_ref[:, width + p * LANES : width + (p + 1) * LANES] = total(1, lanes).astype(BF)
 
 
-def own_key_grads(pieces, cosine, sine):
-    rows, width = pieces[0].shape[1], pieces[0].shape[2]
+def own_key_grads(nc, dkv, cosine, sine):
+    rows, width = dkv.shape[1] // nc, dkv.shape[2]
+    vmem = pl.BlockSpec(memory_space=pltpu.VMEM)
     return pl.pallas_call(
-        own_key_grads_kernel,
+        functools.partial(own_key_grads_kernel, nc),
+        in_specs=[pl.BlockSpec(memory_space=pl.ANY), vmem, vmem],
+        out_specs=vmem,
         out_shape=jax.ShapeDtypeStruct((rows, 2 * width), BF),
+        scratch_shapes=[
+            pltpu.VMEM((nc, 2, rows, width), BF),
+            pltpu.SemaphoreType.DMA((nc,)),
+            pltpu.SemaphoreType.DMA((nc,)),
+        ],
+        compiler_params=pltpu.CompilerParams(collective_id=2, has_side_effects=True),
         name="own_key_grads",
-    )(*pieces, cosine, sine)
-
-
-def pick_columns_kernel(order, gate_ref, up_ref, out_ref):
-    part = gate_ref.shape[1]
-    out_ref[0, :, :part] = gate_ref[...]
-    out_ref[0, :, part:] = up_ref[...]
-
-
-def pick_columns(order, w_gate, w_up):
-    shard, hidden = w_gate.shape
-    parts = order.shape[0]
-    part = hidden // parts
-    if part % 128:
-        both = [w.reshape(shard, parts, part).transpose(1, 0, 2) for w in (w_gate, w_up)]
-        return jnp.take(jnp.concatenate(both, axis=2), order, axis=0)
-    columns = pl.BlockSpec((shard, part), lambda k, t: (0, t[k]))
-    return pl.pallas_call(
-        pick_columns_kernel,
-        grid_spec=pltpu.PrefetchScalarGridSpec(
-            num_scalar_prefetch=1,
-            grid=(parts,),
-            in_specs=[columns, columns],
-            out_specs=pl.BlockSpec((1, shard, 2 * part), lambda k, t: (k, 0, 0)),
-        ),
-        out_shape=jax.ShapeDtypeStruct((parts, shard, 2 * part), BF),
-        name="pick_columns",
-    )(order, w_gate, w_up)
-
-
-def share_kernel(nf, nc, low, size, *refs):
-    (qkv, picked, down, gains, wqkv, wide, downs, all_gains) = refs[:8]
-    (qkv_own, wide_own, down_own, gains_own) = refs[8:12]
+    )(dkv, cosine, sine)
+
+
+def share_kernel(nf, nc, low, size, raw, *refs):
+    w_query, w_key, w_value, w_out, *halves, down, gains = refs[: 8 if raw else 7]
+    refs = refs[8 if raw else 7 :]
+    query, key_value, out, wide, downs, all_gains = refs[:6]
+    query_own, key_value_own, out_own, wide_own, down_own, gains_own = refs[6:12]
     (local, plane_send, plane_recv, along_send, along_recv, core_send, core_recv) = refs[12:19]
-    (gain_send, gain_recv, down_sem, qkv_send, qkv_recv, qkv_core) = refs[19:]
+    (gain_send, gain_recv, down_sem, gather_send, gather_recv, gather_core) = refs[19:]
     chips = nf // 2
     place, here = lax.axis_index("fsdp"), lax.axis_index("ctx")
-    core = place % 2
+    chip, core = place // 2, place % 2
     mesh_id = pl.DeviceIdType.MESH
+    shard, columns = wide.shape[1:]
+    part = columns // 2
+    count = len(halves)
+    key_width = w_key.shape[1]
+    gathered = [
+        (w_query, query, query_own, pl.ds(0, w_query.shape[1])),
+        (w_key, key_value, key_value_own, pl.ds(0, key_width)),
+        (w_value, key_value, key_value_own, pl.ds(key_width, key_width)),
+        (w_out, out, out_own, pl.ds(0, w_out.shape[1])),
+    ]
 
     barrier = pltpu.get_barrier_semaphore()
 
@@ -431,16 +448,25 @@
             device_id_type=mesh_id,
         )
 
+    def piece(k, h, rows):
+        if raw:
+            at = pl.ds(pl.multiple_of((chip ^ k) * part, 128), part)
+            return halves[h].at[rows, at]
+        return halves[0].at[k, rows]
+
+    def side(h):
+        return pl.ds(h * part, part) if raw else pl.ds(0, columns)
+
     def rows_of(share):
         return pl.ds(low + share * size, size)
 
-    def plane_copy(k, kind):
+    def plane_copy(k, kind, h):
         rows = rows_of(here) if kind else pl.ds(0, low)
         return remote(
-            picked.at[k, rows],
-            wide.at[place, rows],
-            plane_send.at[kind, k],
-            plane_recv.at[kind, k],
+            piece(k, h, rows),
+            wide.at[place, rows, side(h)],
+            plane_send.at[kind, k, h],
+            plane_recv.at[kind, k, h],
             {"fsdp": place ^ (2 * k)},
         )
 
@@ -452,34 +478,48 @@
 
     def core_copy(k, share):
         rows = rows_of(share) if share < nc else pl.ds(0, low)
-        block = wide.at[place ^ (2 * k), rows] if k else wide.at[place]
-        source = block if k else picked.at[0]
+        block = wide.at[place ^ (2 * k), rows]
         return remote(
-            source, block, core_send.at[k, share], core_recv.at[k, share], {"fsdp": place ^ 1}
-        )
-
-    half = qkv.shape[0] // 2
+            block, block, core_send.at[k, share], core_recv.at[k, share], {"fsdp": place ^ 1}
+        )
+
+    def own_core_copy(h):
+        return remote(
+            piece(0, h, pl.ds(0, shard)),
+            wide.at[place, :, side(h)],
+            core_send.at[0, h],
+            core_recv.at[0, h],
+            {"fsdp": place ^ 1},
+        )
+
+    half = shard // 2
     relayed = chips == 4
 
-    def qkv_copy(k, part=0):
-        if part == 0:
-            source, owner, rows = qkv, place, pl.ds(0, 2 * half)
+    def gather_copy(u, k, relay=0):
+        source, target, _, at = gathered[u]
+        if relay:
+            owner, rows = place ^ (2 * (3 - k)), pl.ds((2 - k) * half, half)
+            source = target.at[owner, rows, at]
         else:
-            owner, rows = place ^ (2 * (3 - k)), pl.ds((2 - k) * half, half)
-            source = wqkv.at[owner, rows]
-        at = 2 * k + part
+            owner, rows = place, pl.ds(0, shard)
+        number = 2 * k + relay
         return remote(
             source,
-            wqkv.at[owner, rows],
-            qkv_send.at[at],
-            qkv_recv.at[at],
+            target.at[owner, rows, at],
+            gather_send.at[u, number],
+            gather_recv.at[u, number],
             {"fsdp": place ^ (2 * k)},
         )
 
-    def qkv_core_copy(k):
-        block = wqkv.at[place ^ (2 * k)]
+    def gather_core_copy(u, k):
+        source, target, _, at = gathered[u]
+        block = target.at[place ^ (2 * k), :, at]
         return remote(
-            block if k else qkv, block, qkv_core.at[0, k], qkv_core.at[1, k], {"fsdp": place ^ 1}
+            block if k else source,
+            block,
+            gather_core.at[0, u, k],
+            gather_core.at[1, u, k],
+            {"fsdp": place ^ 1},
         )
 
     def down_copy():
@@ -492,28 +532,39 @@
 
     direct = (1, 2) if relayed else tuple(range(1, chips))
     for k in range(1, chips):
-        plane_copy(k, 1).start()
+        for h in range(count):
+            plane_copy(k, 1, h).start()
     for j in range(1, nf):
         gain_copy(j).start()
-    core_copy(0, nc).start()
-    qkv_core_copy(0).start()
+    for h in range(count):
+        own_core_copy(h).start()
+    for u in USED:
+        gather_core_copy(u, 0).start()
     down_copy().start()
-    own = (
-        (qkv, qkv_own, wqkv.at[place]),
-        (picked.at[0], wide_own, wide.at[place]),
-        (down, down_own, downs.at[core]),
-        (gains, gains_own, all_gains.at[place]),
-    )
+    own = [(source, stage.at[:, at], None) for source, _, stage, at in (gathered[u] for u in USED)]
+    own += [(piece(0, h, pl.ds(0, shard)), wide_own.at[:, side(h)], None) for h in range(count)]
+    own += [(down, down_own, downs.at[core]), (gains, gains_own, all_gains.at[place])]
+    back = [(query_own, query.at[place]), (key_value_own, key_value.at[place])]
+    if 3 in USED:
+        back.append((out_own, out.at[place]))
+    back += [
+        (wide_own, wide.at[place]),
+        (down_own, downs.at[core]),
+        (gains_own, all_gains.at[place]),
+    ]
     for i, (source, stage, _) in enumerate(own):
         pltpu.make_async_copy(source, stage, local.at[0, i]).start()
-    for i, (source, stage, target) in enumerate(own):
+    for i, (source, stage, _) in enumerate(own):
         pltpu.make_async_copy(source, stage, local.at[0, i]).wait()
+    for i, (stage, target) in enumerate(back):
         pltpu.make_async_copy(stage, target, local.at[1, i]).start()
 
     for k in range(1, chips):
-        plane_copy(k, 1).wait_send()
-    for k in direct:
-        qkv_copy(k).start()
+        for h in range(count):
+            plane_copy(k, 1, h).wait_send()
+    for u in USED:
+        for k in direct:
+            gather_copy(u, k).start()
 
     for pos in range(nc):
 
@@ -527,16 +578,19 @@
                 core_copy(k, share).start()
 
             for k in range(1, chips):
-                plane_copy(k, 1).wait_recv()
+                for h in range(count):
+                    plane_copy(k, 1, h).wait_recv()
                 pass_on(k, pos)
             if low:
                 for k in range(1, chips):
-                    plane_copy(k, 0).start()
-            for k in direct:
-                qkv_copy(k).wait_recv()
-                if relayed:
-                    qkv_copy(3 - k, 1).start()
-                qkv_core_copy(k).start()
+                    for h in range(count):
+                        plane_copy(k, 0, h).start()
+            for u in USED:
+                for k in direct:
+                    gather_copy(u, k).wait_recv()
+                    if relayed:
+                        gather_copy(u, 3 - k, 1).start()
+                    gather_core_copy(u, k).start()
             for d in range(1, nc):
                 for share in (pos - d, pos + d):
                     if 0 <= share < nc:
@@ -545,12 +599,14 @@
                             pass_on(k, share)
             if low:
                 for k in range(1, chips):
-                    plane_copy(k, 0).wait_recv()
+                    for h in range(count):
+                        plane_copy(k, 0, h).wait_recv()
                     core_copy(k, nc).start()
             if relayed:
-                for k in direct:
-                    qkv_copy(k, 1).wait_recv()
-                qkv_core_copy(3).start()
+                for u in USED:
+                    for k in direct:
+                        gather_copy(u, k, 1).wait_recv()
+                    gather_core_copy(u, 3).start()
             for k in range(1, chips):
                 for share in range(nc):
                     if share <= pos < nc - 1:
@@ -558,51 +614,58 @@
                     if share >= pos > 0:
                         along_copy(k, share, 0, pos - 1).wait_send()
 
-    for k in range(chips):
-        for share in range(nc + 1):
-            if (share < nc and k) or (share == nc and (low or not k)):
-                core_copy(k, share).wait_send()
-                core_copy(k, share).wait_recv()
-    if low:
-        for k in range(1, chips):
-            plane_copy(k, 0).wait_send()
+    for h in range(count):
+        own_core_copy(h).wait()
+    for k in range(1, chips):
+        for share in range(nc + 1 if low else nc):
+            core_copy(k, share).wait()
+        if low:
+            for h in range(count):
+                plane_copy(k, 0, h).wait_send()
     for j in range(1, nf):
         gain_copy(j).wait()
-    for k in direct:
-        qkv_copy(k).wait_send()
-        if relayed:
-            qkv_copy(k, 1).wait_send()
-    for k in range(chips):
-        qkv_core_copy(k).wait()
+    for u in USED:
+        for k in direct:
+            gather_copy(u, k).wait_send()
+            if relayed:
+                gather_copy(u, k, 1).wait_send()
+        for k in range(chips):
+            gather_core_copy(u, k).wait()
     down_copy().wait()
-    for i, (_, stage, target) in enumerate(own):
+    for i, (stage, target) in enumerate(back):
         pltpu.make_async_copy(stage, target, local.at[1, i]).wait()
 
 
-def share_weights(nf, nc, qkv, picked, down, gains):
-    chips, shard, columns = picked.shape
+def share_weights(nf, nc, w_query, w_key, w_value, w_out, w_gate, w_up, order, down, gains):
+    chips = nf // 2
+    shard, hidden = w_gate.shape
+    part = hidden // chips
     size = 16 * max(1, (shard * 3 // 4) // (16 * nc))
     low = shard - nc * size
+    raw = part % 128 == 0
+    halves = [w_gate, w_up]
+    if not raw:
+        both = [w.reshape(shard, chips, part).transpose(1, 0, 2) for w in halves]
+        halves = [jnp.take(jnp.concatenate(both, axis=2), order, axis=0)]
     anywhere = pl.BlockSpec(memory_space=pl.ANY)
     dma = pltpu.SemaphoreType.DMA
+    widths = [w_query.shape[1], 2 * w_key.shape[1], w_out.shape[1], 2 * part]
     return pl.pallas_call(
-        functools.partial(share_kernel, nf, nc, low, size),
-        in_specs=[anywhere] * 4,
-        out_specs=[anywhere] * 4,
-        out_shape=[
-            jax.ShapeDtypeStruct((nf,) + qkv.shape, BF),
-            jax.ShapeDtypeStruct((nf, shard, columns), BF),
+        functools.partial(share_kernel, nf, nc, low, size, raw),
+        in_specs=[anywhere] * (6 + len(halves)),
+        out_specs=[anywhere] * 6,
+        out_shape=[jax.ShapeDtypeStruct((nf, shard, width), BF) for width in widths]
+        + [
             jax.ShapeDtypeStruct((2,) + down.shape, BF),
             jax.ShapeDtypeStruct((nf,) + gains.shape, BF),
         ],
-        scratch_shapes=[
-            pltpu.VMEM(qkv.shape, BF),
-            pltpu.VMEM((shard, columns), BF),
+        scratch_shapes=[pltpu.VMEM((shard, width), BF) for width in widths]
+        + [
             pltpu.VMEM(down.shape, BF),
             pltpu.VMEM(gains.shape, BF),
-            dma((2, 4)),
-            dma((2, chips)),
-            dma((2, chips)),
+            dma((2, 8)),
+            dma((2, chips, 2)),
+            dma((2, chips, 2)),
             dma((2, nc, chips)),
             dma((nc, chips)),
             dma((chips, nc + 1)),
@@ -610,15 +673,15 @@
             dma((nf,)),
             dma((nf,)),
             dma((2,)),
-            dma((2 * chips,)),
-            dma((2 * chips,)),
-            dma((2, chips)),
+            dma((4, 2 * chips)),
+            dma((4, 2 * chips)),
+            dma((2, 4, chips)),
         ],
         compiler_params=pltpu.CompilerParams(
             collective_id=1, has_side_effects=True, vmem_limit_bytes=56 << 20
         ),
         name="share_weights",
-    )(qkv, picked, down, gains)
+    )(w_query, w_key, w_value, w_out, *halves, down, gains)
 
 
 def place_columns_kernel(order, both_ref, gate_ref, up_ref):
@@ -645,6 +708,288 @@
         out_shape=[out, out],
         name="place_columns",
     )(order, both)
+
+
+def feed_forward_kernel(nf, *refs):
+    chips = nf // 2
+    hn, *gbs, w_gu, w_d, grad, left, right, downs, outs = refs[: chips + 8]
+    w_gu_v, w_d_v, hn_v, gb_v, dact_v, act_v, dgu_v, sent, got, outs_v = refs[chips + 8 : chips + 18]
+    tiles, *sems = refs[chips + 18 :]
+    load, load_gb, hn_send, hn_recv, dhn_send, dhn_recv, store = sems[:7]
+    left_local, left_send, left_recv, right_local, right_send, right_recv = sems[7:13]
+    down_local, down_send, down_recv = sems[13:]
+    place = lax.axis_index("fsdp")
+    core = place % 2
+    rows, width = hn.shape
+    part = w_d.shape[0]
+    shard = width // nf
+    half = rows // 2
+    relayed = chips == 4
+    direct = (1, 2) if relayed else tuple(range(1, chips))
+    mesh_id = pl.DeviceIdType.MESH
+
+    barrier = pltpu.get_barrier_semaphore()
+    for j in [1] + [2 * k for k in range(1, chips)]:
+        pl.semaphore_signal(
+            barrier, inc=1, device_id={"fsdp": place ^ j}, device_id_type=mesh_id
+        )
+    pl.semaphore_wait(barrier, chips)
+
+    def remote(source, target, sends, recvs, step):
+        return pltpu.make_async_remote_copy(
+            src_ref=source,
+            dst_ref=target,
+            send_sem=sends,
+            recv_sem=recvs,
+            device_id={"fsdp": place ^ step},
+            device_id_type=mesh_id,
+        )
+
+    def hn_copy(k, relay=0):
+        at = 2 * k + relay
+        if relay:
+            lines = pl.ds((2 - k) * half, half)
+            source, target = hn_v.at[3 - k, lines], hn_v.at[3, lines]
+        else:
+            source, target = hn, hn_v.at[k]
+        return remote(source, target, hn_send.at[at], hn_recv.at[at], 2 * k)
+
+    def dhn_copy(k):
+        return remote(sent.at[k - 1], got.at[k - 1], dhn_send.at[k], dhn_recv.at[k], 2 * k)
+
+    def left_copy(k, j, other):
+        number = 1 - core if other else core
+        columns = pl.ds(pl.multiple_of((2 * j + number) * shard, shard), shard)
+        source = hn_v.at[k, :, columns]
+        target = left.at[other, k, :, pl.ds(j * shard, shard)]
+        if other:
+            return remote(source, target, left_send.at[k, j], left_recv.at[k, j], 1)
+        return pltpu.make_async_copy(source, target, left_local.at[k, j])
+
+    def right_copy(k, other):
+        if other:
+            return remote(dgu_v.at[k], right.at[1, k], right_send.at[k], right_recv.at[k], 1)
+        return pltpu.make_async_copy(dgu_v.at[k], right.at[0, k], right_local.at[k])
+
+    loads = [
+        pltpu.make_async_copy(w_d, w_d_v, load.at[0]),
+        pltpu.make_async_copy(hn, hn_v.at[0], load.at[1]),
+        pltpu.make_async_copy(w_gu, w_gu_v, load.at[2]),
+    ]
+    gb_loads = [
+        pltpu.make_async_copy(gb, gb_v.at[k], load_gb.at[k]) for k, gb in enumerate(gbs)
+    ]
+    store_outs = pltpu.make_async_copy(outs_v, outs, store.at[0])
+    for k in direct:
+        hn_copy(k).start()
+    for copy in loads[:1] + gb_loads + loads[1:]:
+        copy.start()
+
+    for copy in loads[:1] + gb_loads:
+        copy.wait()
+
+    def dact_tile(start, size):
+        tile = w_d_v[pl.ds(start, size), :]
+        for k in range(chips):
+            dact_v[k, :, pl.ds(start, size)] = dot(gb_v[k], tile, (1, 1))
+
+    @pl.loop(0, part // 256)
+    def _(i):
+        dact_tile(pl.multiple_of(i * 256, 256), 256)
+
+    if part % 256:
+        dact_tile(part - 128, 128)
+
+    def forward(k):
+        for j in range(chips):
+            left_copy(k, j, 1).start()
+            left_copy(k, j, 0).start()
+
+        def tile(start, size):
+            one, two = pl.ds(start, size), pl.ds(pl.multiple_of(part + start, 128), size)
+            gate = dot(hn_v[k], w_gu_v[:, one], (1, 0))
+            up = dot(hn_v[k], w_gu_v[:, two], (1, 0))
+            dact = dact_v[k, :, one]
+            sg = jax.nn.sigmoid(gate)
+            silu = gate * sg
+            act_v[k, :, one] = (silu * up).astype(BF)
+            dgu_v[k, :, one] = (dact * up * sg * (1.0 + gate * (1.0 - sg))).astype(BF)
+            dgu_v[k, :, two] = (dact * silu).astype(BF)
+
+        @pl.loop(0, part // 256)
+        def _(i):
+            tile(pl.multiple_of(i * 256, 256), 256)
+
+        if part % 256:
+            tile(part - 128, 128)
+
+        right_copy(k, 1).start()
+        right_copy(k, 0).start()
+
+    def backward(k):
+        @pl.loop(0, width // 256)
+        def _(i):
+            lines = pl.ds(pl.multiple_of(i * 256, 256), 256)
+            dhn = dot(dgu_v[k], w_gu_v[lines, :], (1, 1))
+            if k:
+                sent[k - 1, :, lines] = dhn.astype(BF)
+            else:
+                grad[:, lines] = dhn
+
+        if k:
+            dhn_copy(k).start()
+
+    for copy in loads[1:]:
+        copy.wait()
+    forward(0)
+    for k in direct:
+        hn_copy(k).wait_recv()
+        if relayed:
+            hn_copy(3 - k, 1).start()
+    for k in range(1, chips):
+        if relayed and k == 3:
+            for i in direct:
+                hn_copy(i, 1).wait_recv()
+        forward(k)
+        backward(k)
+    backward(0)
+
+    @pl.loop(0, width // 256)
+    def _(i):
+        columns = pl.ds(pl.multiple_of(i * 256, 256), 256)
+        for k in range(chips):
+            outs_v[k, :, columns] = dot(act_v[k], w_d_v[:, columns], (1, 0)).astype(BF)
+
+    store_outs.start()
+
+    lower = part // 2
+    spans = []
+    for start in range(0, part, 128):
+        cuts = sorted({start, min(max(lower, start), start + 128), start + 128})
+        spans += [(start, a, b) for a, b in zip(cuts, cuts[1:])]
+
+    def span_copies(n):
+        start, a, b = spans[n]
+        number = int(a >= lower)
+        source = tiles.at[(start // 128) % 2, pl.ds(a - start, b - a)]
+        at = pl.ds(a - number * lower, b - a)
+
+        def keep():
+            return pltpu.make_async_copy(source, downs.at[0, at], down_local.at[n])
+
+        def send():
+            return remote(source, downs.at[1, at], down_send.at[n], down_recv.at[n], 1)
+
+        return number, keep, send
+
+    def each_span(chosen, go):
+        for n in chosen:
+            number, keep, send = span_copies(n)
+
+            @pl.when(core == number)
+            def _():
+                keep().start() if go else keep().wait()
+
+            @pl.when(core != number)
+            def _():
+                send().start() if go else send().wait_send()
+
+    for start in range(0, part, 128):
+        before = [n for n, span in enumerate(spans) if span[0] == start - 256]
+        each_span(before, False)
+        tile = sum(
+            dot(act_v[k, :, start : start + 128], gb_v[k], (0, 0)) for k in range(chips)
+        )
+        tiles[(start // 128) % 2] = tile.astype(BF)
+        each_span([n for n, span in enumerate(spans) if span[0] == start], True)
+    each_span([n for n, span in enumerate(spans) if span[0] >= part - 256], False)
+    for n in range(len(spans)):
+        number, _, send = span_copies(n)
+
+        @pl.when(core == number)
+        def _():
+            send().wait_recv()
+
+    for k in range(1, chips):
+        dhn_copy(k).wait_recv()
+
+    @pl.loop(0, rows // 16)
+    def _(i):
+        lines = pl.ds(pl.multiple_of(i * 16, 16), 16)
+        grad[lines, :] += sum(got[k, lines, :].astype(F32) for k in range(chips - 1))
+
+    store_outs.wait()
+    for k in range(chips):
+        for j in range(chips):
+            left_copy(k, j, 0).wait()
+            left_copy(k, j, 1).wait()
+        right_copy(k, 0).wait()
+        right_copy(k, 1).wait()
+        if k:
+            dhn_copy(k).wait_send()
+    for k in direct:
+        hn_copy(k).wait_send()
+        if relayed:
+            hn_copy(k, 1).wait_send()
+
+
+def feed_forward(nf, hn, gbs, w_gu, w_d):
+    chips = nf // 2
+    rows, width = hn.shape
+    part = w_d.shape[0]
+    anywhere = pl.BlockSpec(memory_space=pl.ANY)
+    dma = pltpu.SemaphoreType.DMA
+    shape = jax.ShapeDtypeStruct
+    return pl.pallas_call(
+        functools.partial(feed_forward_kernel, nf),
+        in_specs=[anywhere] * (chips + 3),
+        out_specs=[pl.BlockSpec(memory_space=pltpu.VMEM)] + [anywhere] * 4,
+        out_shape=[
+            shape((rows, width), F32),
+            shape((2, chips, rows, width // 2), BF),
+            shape((2, chips, rows, 2 * part), BF),
+            shape((2, part // 2, width), BF),
+            shape((chips, rows, width), BF),
+        ],
+        scratch_shapes=[
+            pltpu.VMEM((width, 2 * part), BF),
+            pltpu.VMEM((part, width), BF),
+            pltpu.VMEM((chips, rows, width), BF),
+            pltpu.VMEM((chips, rows, width), BF),
+            pltpu.VMEM((chips, rows, part), F32),
+            pltpu.VMEM((chips, rows, part), BF),
+            pltpu.VMEM((chips, rows, 2 * part), BF),
+            pltpu.VMEM((chips - 1, rows, width), BF),
+            pltpu.VMEM((chips - 1, rows, width), BF),
+            pltpu.VMEM((chips, rows, width), BF),
+            pltpu.VMEM((2, 128, width), BF),
+            dma((3,)),
+            dma((chips,)),
+            dma((2 * chips,)),
+            dma((2 * chips,)),
+            dma((chips,)),
+            dma((chips,)),
+            dma((1,)),
+            dma((chips, chips)),
+            dma((chips, chips)),
+            dma((chips, chips)),
+            dma((chips,)),
+            dma((chips,)),
+            dma((chips,)),
+            dma((part // 128 + 1,)),
+            dma((part // 128 + 1,)),
+            dma((part // 128 + 1,)),
+        ],
+        compiler_params=pltpu.CompilerParams(
+            collective_id=3, has_side_effects=True, vmem_limit_bytes=60 << 20
+        ),
+        cost_estimate=pl.CostEstimate(
+            flops=12 * chips * rows * width * part,
+            bytes_accessed=40_000_000,
+            transcendentals=chips * rows * part,
+        ),
+        name="feed_forward",
+    )(hn, *gbs, w_gu, w_d)
 
 
 def chunk_rows(rows):
@@ -893,17 +1238,27 @@
 
         order = chip ^ jnp.arange(chips, dtype=jnp.int32)
         both_gains = jnp.pad(jnp.stack([attn_gain, ffn_gain]), ((0, 14), (0, 0)))
-        w_qkv, w_gu, w_d, gains = share_weights(
+        w_q, w_kv, w_o, w_gu, w_d, gains = share_weights(
             nf,
             nc,
-            jnp.concatenate([w_query, w_key, w_value], axis=1),
-            pick_columns(order, w_gate, w_up),
+            w_query,
+            w_key,
+            w_value,
+            w_out,
+            w_gate,
+            w_up,
+            order,
             w_down,
             both_gains,
         )
-        w_out, w_qkv = lax.optimization_barrier((w_out, w_qkv))
-        w_o = lax.all_gather(w_out, "fsdp", axis=0, tiled=True)
-        w_qkv = w_qkv.reshape(width, -1)
+        w_q = w_q.reshape(width, -1)
+        w_kv = w_kv.reshape(width, -1)
+        gb_sent, w_kv = lax.optimization_barrier((gb, w_kv))
+        if 3 in USED:
+            w_o = w_o.reshape(-1, width)
+        else:
+            w_out, w_kv = lax.optimization_barrier((w_out, w_kv))
+            w_o = lax.all_gather(w_out, "fsdp", axis=0, tiled=True)
         w_gu = w_gu.reshape(width, 2 * part)
         w_d = w_d.reshape(part, width)
         gains = gains[:, :2].astype(F32).transpose(1, 0, 2).reshape(2, width)
@@ -928,12 +1283,11 @@
         inverse_one = lax.rsqrt(jnp.mean(x * x, axis=1, keepdims=True) + EPS)
         unit_one = x * inverse_one
         xn = (unit_one * gains[0][None, :]).astype(BF)
-        qkv = dot(xn, w_qkv, (1, 0))
-        kv = own_keys(qkv, cos_lanes, sin_lanes)
-        sent, _ = lax.optimization_barrier((gb, qkv))
-        gb_of = [gb] + plane_gather(sent)
+        kv = own_keys(dot(xn, w_kv, (1, 0)), cos_lanes, sin_lanes)
+        q_sum = dot(xn, w_q, (1, 0))
+        gb_of = [gb] + [swap(gb_sent, 2 * k) for k in range(1, chips)]
         kv = jnp.concatenate([cross(kv, k) if k else kv for k in range(nc)], axis=0)
-        qr, o, ob, lse = attention_forward(table, qkv, cos_lanes, sin_lanes, kv)
+        qr, o, ob, lse = attention_forward(table, q_sum, cos_lanes, sin_lanes, kv)
         h1 = x + dot(ob, w_o, (1, 0))
         inverse_two = lax.rsqrt(jnp.mean(h1 * h1, axis=1, keepdims=True) + EPS)
         unit_two = h1 * inverse_two
@@ -941,36 +1295,54 @@
 
         hn, gb_of = lax.optimization_barrier((hn, gb_of))
 
-        dhns = []
-        hn_of, act_of, dgu_of = [], [], []
-        for k, hn_k in enumerate([hn] + plane_gather(hn)):
-            gu = dot(hn_k, w_gu, (1, 0))
-            dact = dot(gb_of[k], w_d, (1, 1))
-            gate, up = gu[:, :part], gu[:, part:]
-            sg = jax.nn.sigmoid(gate)
-            silu = gate * sg
-            act = (silu * up).astype(BF)
-            dgate = (dact * up * sg * (1.0 + gate * (1.0 - sg))).astype(BF)
-            dgu = jnp.concatenate([dgate, (dact * silu).astype(BF)], axis=1)
-            dhn_k = dot(dgu, w_gu, (1, 1))
-            dhns.append(dhn_k.astype(BF) if k else dhn_k)
-            hn_of.append(hn_k)
-            act_of.append(act)
-            dgu_of.append(dgu)
-        got = [swap(dhns[k], 2 * k) for k in range(1, chips)]
-        act_of, dgu_of, got[:-1], _ = lax.optimization_barrier(
-            (act_of, dgu_of, got[:-1], dhns[1:])
-        )
-        grad_hn = dhns[0]
-        for piece in got:
-            grad_hn = grad_hn + piece.astype(F32)
-
-        gb_all = jnp.concatenate(gb_of, axis=0)
-        down = dot(jnp.concatenate(act_of, axis=0), gb_all, (0, 0)).astype(BF)
-        down_sum = core_sum(down.reshape((1, 2) + w_down.shape))[0]
-        down_sum, grad_hn = lax.optimization_barrier((down_sum, grad_hn))
+        fused = part % 128 == 0
+        if fused:
+            grad_hn, left, right, downs, outs = feed_forward(nf, hn, gb_of, w_gu, w_d)
+            left = left.reshape(2 * chips * rows, width // 2)
+            right = right.reshape(2 * chips * rows, 2 * part)
+            down_sum = (downs[0].astype(F32) + downs[1].astype(F32)).astype(BF)
+        else:
+            dhns = []
+            hn_of, act_of, dgu_of = [], [], []
+            for k, hn_k in enumerate([hn] + plane_gather(hn)):
+                gu = dot(hn_k, w_gu, (1, 0))
+                dact = dot(gb_of[k], w_d, (1, 1))
+                gate, up = gu[:, :part], gu[:, part:]
+                sg = jax.nn.sigmoid(gate)
+                silu = gate * sg
+                act = (silu * up).astype(BF)
+                dgate = (dact * up * sg * (1.0 + gate * (1.0 - sg))).astype(BF)
+                dgu = jnp.concatenate([dgate, (dact * silu).astype(BF)], axis=1)
+                dhn_k = dot(dgu, w_gu, (1, 1))
+                dhns.append(dhn_k.astype(BF) if k else dhn_k)
+                hn_of.append(hn_k)
+                act_of.append(act)
+                dgu_of.append(dgu)
+            got = [swap(dhns[k], 2 * k) for k in range(1, chips)]
+            act_of, dgu_of, got[:-1], _ = lax.optimization_barrier(
+                (act_of, dgu_of, got[:-1], dhns[1:])
+            )
+            grad_hn = dhns[0]
+            for piece in got:
+                grad_hn = grad_hn + piece.astype(F32)
+
+            gb_all = jnp.concatenate(gb_of, axis=0)
+            down = dot(jnp.concatenate(act_of, axis=0), gb_all, (0, 0)).astype(BF)
+            down_sum = core_sum(down.reshape((1, 2) + w_down.shape))[0]
+            left = jnp.concatenate(hn_of, axis=0)
+            right = jnp.concatenate(dgu_of, axis=0)
+
+        down_sum, left, right = lax.optimization_barrier((down_sum, left, right))
         down_sum = lax.psum_scatter(down_sum, "ctx", scatter_dimension=0, tiled=True)
-        hn_all, dgu_all = jnp.concatenate(hn_of, axis=0), jnp.concatenate(dgu_of, axis=0)
+        if fused:
+            wide = dot(left, right, (0, 0)).astype(BF).reshape(chips, shard, 2 * part)
+        else:
+            wide = rows_grad(left, right)
+        wide = [
+            lax.dynamic_index_in_dim(wide, chip ^ k, 0, keepdims=False) for k in range(chips)
+        ]
+        wide, grad_hn = lax.optimization_barrier((wide, grad_hn))
+        wide = [swap(piece, 2 * k) if k else piece for k, piece in enumerate(wide)]
 
         gain_two_grad = jnp.sum(grad_hn * unit_two, axis=0)
         grad_unit = grad_hn * gains[1][None, :]
@@ -980,28 +1352,20 @@
         dab = dh1.astype(BF)
         dob = dot(dab, w_o, (1, 1)).astype(BF)
         dq, dkv = attention_backward(table, qr, dob, o, lse, kv, cos_lanes, sin_lanes)
-        act_of, xn, ob, dab, hn_all, dgu_all, _ = lax.optimization_barrier(
-            (act_of, xn, ob, dab, hn_all, dgu_all, dq)
-        )
-        down_sum, hn_all, dgu_all = lax.optimization_barrier((down_sum, hn_all, dgu_all))
+        xn, ob, dab, _ = lax.optimization_barrier((xn, ob, dab, dq))
+        if fused:
+            outs = [outs[k] for k in range(chips)]
+        else:
+            act_of, _ = lax.optimization_barrier((act_of, dq))
+            outs = [dot(act, w_d, (1, 0)).astype(BF) for act in act_of]
+        sent = outs[1:]
+        own = own_key_grads(nc, dkv, cos_lanes, sin_lanes)
+        own, wide, down_sum = lax.optimization_barrier((own, wide, down_sum))
         down_sum = lax.all_gather(down_sum, "ctx", axis=0, tiled=True)
-        wide = rows_grad(hn_all, dgu_all)
-        wide = [
-            lax.dynamic_index_in_dim(wide, chip ^ k, 0, keepdims=False) for k in range(chips)
-        ]
-        act_of, _ = lax.optimization_barrier((act_of, wide))
-        wide = [swap(piece, 2 * k) if k else piece for k, piece in enumerate(wide)]
-        outs = [dot(act, w_d, (1, 0)) for act in act_of]
-        sent = [out.astype(BF) for out in outs[1:]]
-        pieces = [dkv[:, k * rows : (k + 1) * rows] for k in range(nc)]
-        pieces = [cross(piece, k) if k else piece for k, piece in enumerate(pieces)]
+        ob, dab, _ = lax.optimization_barrier((ob, dab, own))
         out_term = rows_grad(ob, dab)
-        pieces, outs[0], sent, out_term = lax.optimization_barrier(
-            (pieces, outs[0], sent, out_term)
-        )
-        own = own_key_grads(pieces, cos_lanes, sin_lanes)
         dqkv = jnp.concatenate([dq, own], axis=1)
-        grad_xn = dot(dqkv, w_qkv, (1, 1))
+        grad_xn = dot(dq, w_q, (1, 1)) + dot(own, w_kv, (1, 1))
         gain_one_grad = jnp.sum(grad_xn * unit_one, axis=0)
         grad_unit = grad_xn * gains[0][None, :]
         tokens_grad = dh1 + inverse_one * (
@@ -1021,7 +1385,7 @@
             nf, nc, wide, [out_term, qkv_term, gains_of]
         )
         h1, gain_sum = lax.optimization_barrier((h1, gain_sum))
-        branch = h1 + outs[0]
+        branch = h1 + outs[0].astype(F32)
         for k in range(1, chips):
             branch = branch + swap(sent[k - 1], 2 * k).astype(F32)
         layer_out = branch.astype(BF)

time: 738 us -> 659 us (0.89)
  Pallas kernels: 350 us -> 481 us
  matrix products: 154 us -> 52.5 us
  waiting for transfers between devices: 96.6 us -> 38.6 us
  other arithmetic: 50.7 us -> 29.3 us
  local copies, waits for them, and re-layouts: 34.5 us -> 21 us
  starting transfers between devices: 29.9 us -> 16.7 us
    pallas_call x3, Pallas kernels: 98 us -> 233 us  [the longest x1 115 us: share_weights(): pl.pallas_call(functools.partial(share_kernel, nf, nc, low, size, raw), i...]
    dot_general x24 -> x9, matrix products: 154 us -> 52.5 us  [dot(): lax.dot_general(left, right, ((contract[:1], contract[1:]), ((), ())), pr...]
    ppermute x25 -> x14, waiting for transfers between devices: 87.2 us -> 4.64 us  [swap(): return lax.ppermute(x, 'fsdp', [(i, i ^ k) for i in range(nf)])]
    all_gather x1, waiting for transfers between devices: 0.01 us -> 25.9 us  [shards(): down_sum = lax.all_gather(down_sum, 'ctx', axis=0, tiled=True)]
    concatenate x7 -> x0, other arithmetic: 18.8 us -> none  [the longest x1 11.1 us: shards(): jnp.concatenate(dgu_of, axis=0)]
    unnamed x177 -> x74, local copies, waits for them, and re-layouts: 16.8 us -> 7.26 us
    ppermute x25 -> x14, starting transfers between devices: 21.4 us -> 12.3 us  [swap(): return lax.ppermute(x, 'fsdp', [(i, i ^ k) for i in range(nf)])]
    ppermute x6 -> x3, waiting for transfers between devices: 0.02 us -> 7.99 us  [cross(): return lax.ppermute(x, 'ctx', [(i, i ^ k) for i in range(nc)])]
  transfers between devices with their start and end apart: 34 -> 19, of which waited for: 10 -> 4; matrix products, arithmetic and copies ran while one was open for 27% -> 12% of each run, Pallas kernels for 35% -> 42%
where the time goes in v3:
time: 659 us; the launch traced here: 654 us
  Pallas kernels  481 us (73%)
  matrix products  52.5 us (8%)
  waiting for transfers between devices  38.6 us (6%)
  other arithmetic  29.3 us (4%)
  local copies, waits for them, and re-layouts  21 us (3%)
  starting transfers between devices  16.7 us (3%)
  between operations  14.9 us (2%)
    pallas_call x1, Pallas kernels, finish(): pl.pallas_call(functools.partial(finish_kernel, nf, nc), in_specs=[anywhe...  196 us
    pallas_call x1, Pallas kernels, share_weights(): pl.pallas_call(functools.partial(share_kernel, nf, nc, low, size, raw), i...  115 us
    pallas_call x1, Pallas kernels, feed_forward(): pl.pallas_call(functools.partial(feed_forward_kernel, nf), in_specs=[anyw...  92 us
    dot_general x9, matrix products, dot(): lax.dot_general(left, right, ((contract[:1], contract[1:]), ((), ())), pr...  52.5 us
    pallas_call x1, Pallas kernels, own_key_grads(): pl.pallas_call(functools.partial(own_key_grads_kernel, nc), in_specs=[pl....  26.1 us
    all_gather x1, waiting for transfers between devices, shards(): down_sum = lax.all_gather(down_sum, 'ctx', axis=0, tiled=True)  25.9 us
    pallas_call x1, Pallas kernels, attention_backward(): pl.pallas_call(attention_backward_kernel, grid_spec=pltpu.PrefetchScalarG...  22.8 us
    pallas_call x1, Pallas kernels, attention_forward(): pl.pallas_call(attention_forward_kernel, grid_spec=pltpu.PrefetchScalarGr...  19.4 us
  transfers between devices with their start and end apart: 19, of which 4 were waited for; matrix products, arithmetic and copies ran while one was open for 12% of the time, Pallas kernels for 42%

profile of v3, /device:TPU:0, one launch (start us, length us, event | category | flops | bytes accessed | tf_op | source)
XLA Modules:
  0.0 654.1 jit_solution(3045136829493350247)
XLA Ops:
  9.2 114.5 %share_weights.1 = (bf16[8,256,2048]{2,1,0:T(8,128)(2,1)}, bf16[8,256,512]{2,1,0:T(8,128)(2,1)}, bf16[8,256,2048]{2,1,0:T(8,128)(2,1)}, bf16[8,256,2816]{2,1,0:T...) custom-call(bf16[256,2048]{1,0:T(8,128)(2,1)} %refs_0_.1, bf16[256,256]{1,0:T(8,128)(2,1)} %refs_1_.1, ...), custom_call_target="tpu_custom_call" | custom-call | tf_op jit(solution)/shard_map/share_weights/pallas_call | solution.py:653
  123.7 0.8 convert_bitcast_fusion.1
  125.8 0.8 copy.48.cos_ref
  126.9 1.0 copy-done.21
  127.9 1.5 fusion.50.k_ref.v_ref
  129.4 2.0 own_keys.1
  131.4 1.6 collective-permute-start
  133.0 2.4 collective-permute-start.1
  135.8 1.2 collective-permute-start.3
  137.0 1.1 collective-permute-start.4
  138.1 5.8 fusion.26.q_ref
  145.5 1.7 collective-permute-start.5
  147.2 7.5 %collective-permute-done.1 = bf16[256,512]{1,0:T(8,128)(2,1)} collective-permute-done((bf16[256,512]{1,0:T(8,128)(2,1)}, bf16[256,512]{1,0:T(8,128)(2,1)}, u32[]{:S(2)}, u32[]{:S(2)}) %collective-permute-start.1) | collective-permute-done | bytes 262176 | tf_op jit(solution)/shard_map/ppermute | solution.py:1196
  154.7 1.4 pad_maximum_fusion.k_pair.v_pair
  156.1 19.4 %attention_forward.1 = (bf16[256,2048]{1,0:T(8,128)(2,1)S(1)}, f32[256,2048]{1,0:T(8,128)S(1)}, bf16[256,2048]{1,0:T(8,128)(2,1)S(1)}, f32[4,2,1024]{2,1,0:T(2,128)S(1)}) custom-call(s32[10]{0:T(128)S(1)} %pad_add_fusion.table, f32[256,2048]{1,0:T(8,128)S(1)} %fusion.26.q_ref, f32[256,128]{1,0:T(8,128)S(1)} %copy-done.1, f32[256,128]{1,0:T(8,128)S(1)} %copy-done, ...), custom_call_target="tpu_custom_call" | custom-call | flops 4294967296 | bytes 8388608 | tf_op jit(solution)/shard_map/attention_forward/pallas_call | solution.py:155
  175.6 2.5 multiply_reduce_fusion.2
  178.2 1.4 multiply_convert_fusion.refs_0_
  179.6 4.6 collective-permute-done.4.refs_3_
  184.2 92.0 %feed_forward.1 = (f32[256,2048]{1,0:T(8,128)}, bf16[2,4,256,1024]{3,2,1,0:T(8,128)(2,1)}, bf16[2,4,256,2816]{3,2,1,0:T(8,128)(2,1)}, bf16[2,704,2048]{2,1,0:T(8,128)(2,1)}, bf16[4,256,2048]{2,1,0:T(8,128)(2,1)}) custom-call(bf16[256,2048]{1,0:T(8,128)(2,1)} %multiply_convert_fusion.refs_0_, bf16[256,2048]{1,0:T(8,128)(2,1)} %bitcast.8.refs_1_, ...), custom_call_target="tpu_custom_call" | custom-call | flops 35433480192 | bytes 40000000 | tf_op jit(solution)/shard_map/feed_forward/pallas_call | solution.py:943
  276.2 5.7 fusion
  281.9 17.5 %convolution_convert_fusion.1 = bf16[1024,2816]{1,0:T(8,128)(2,1)S(1)} fusion(bf16[2048,1024]{1,0:T(8,128)(2,1)} %bitcast.134, bf16[2048,2816]{1,0:T(8,128)(2,1)} %bitcast.131), kind=kOutput, calls=%fused_computation.2 | convolution fusion | flops 11814043648 | bytes 21495808 | tf_op jit(solution)/shard_map/dot_general | solution.py:28
  299.5 2.3 dynamic-slice_bitcast_fusion
  301.8 1.3 collective-permute-start.6
  303.8 1.5 collective-permute-start.8
  306.0 1.9 fusion.44
  307.9 6.2 convolution_convert_fusion.3.do_ref
  314.1 22.8 %attention_backward.1 = (bf16[256,2048]{1,0:T(8,128)(2,1)S(1)}, bf16[2,1024,256]{2,1,0:T(8,128)(2,1)S(1)}) custom-call(s32[10]{0:T(128)S(1)} %pad_add_fusion.table, bf16[256,2048]{1,0:T(8,128)(2,1)S(1)} %copy-done.13, bf16[256,2048]{1,0:T(8,128)(2,1)S(1)} %convolution_convert_fusion.3.do_ref, f32[256,2048]{1,0:T(8,128)S(1)} %copy-done.11, ...), custom_call_target="tpu_custom_call" | custom-call | flops 10737418240 | bytes 8388608 | tf_op jit(solution)/shard_map/attention_backward/pallas_call | solution.py:281
  337.0 1.0 copy-done.2
  338.0 1.0 copy-done.7
  338.9 26.1 %own_key_grads.1 = bf16[256,512]{1,0:T(8,128)(2,1)} custom-call(bf16[2,1024,256]{2,1,0:T(8,128)(2,1)} %copy-done.2, f32[256,128]{1,0:T(8,128)} %copy.48.cos_ref, f32[256,128]{1,0:T(8,128)} %copy.49.sin_ref), custom_call_target="tpu_custom_call" | custom-call | tf_op jit(solution)/shard_map/own_key_grads/pallas_call | solution.py:388
  365.2 1.0 broadcast_select_fusion.1
  366.4 1.0 constant_dynamic-update-slice_fusion.1
  367.5 4.5 slice_bitcast_fusion
  373.6 8.1 %fusion.13 = (f32[256]{0:T(256)S(1)}, f32[2048]{0:T(1024)S(1)}, f32[256,2048]{1,0:T(8,128)}) fusion(bf16[1,256,2048]{2,1,0:T(8,128)(2,1)S(1)} %copy-done.20, f32[2048]{0:T(1024)S(1)} %bitcast.116, f32[256]{0:T(256)S(1)} %add_rsqrt_fusion.1, f32[256,2048]{1,0:T(8,128)S(1)} %fusion.51, bf16[256,2048]{1,0:T(8,128)(2,1)S(1)} %copy-done.9, ...), kind=kOutput, calls=%fused_computation.21 | convolution fusion | flops 2151675648 | bytes 14698496 | tf_op jit(solution)/shard_map/dot_general | solution.py:28
  385.2 4.8 fusion.17
  390.1 4.4 convolution_convert_fusion.2
  394.6 5.7 convolution_convert_fusion
  400.3 25.9 %all-gather.2.cloned.1.call-done = bf16[704,2048]{1,0:T(8,128)(2,1)} async-done(((bf16[176,2048]{1,0:T(8,128)(2,1)}), bf16[704,2048]{1,0:T(8,128)(2,1)}) %all-gather.2.cloned.1.call-update) | async-done | bytes 2883600 | tf_op jit(solution)/shard_map/all_gather | solution.py:1364
  426.2 1.5 collective-permute-start.14
  427.7 1.5 collective-permute-start.15
  429.7 196.0 %finish.1 = (bf16[4,256,2816]{2,1,0:T(8,128)(2,1)}, bf16[256,2048]{1,0:T(8,128)(2,1)S(1)}, bf16[256,2560]{1,0:T(8,128)(2,1)S(1)}, bf16[16,512]{1,0:T(8,128)(2,1)S(1)}) custom-call(bf16[256,2816]{1,0:T(8,128)(2,1)S(1)} %get-tuple-element.116.refs_0_, bf16[256,2816]{1,0:T(8,128)(2,1)} %collective-permute-done.6.refs_1_, ...), custom_call_target="tpu_custom_call" | custom-call | flops 199999995904 | bytes 60000000 | tf_op jit(solution)/shard_map/finish/pallas_call | solution.py:1161
  625.7 1.6 convert_element_type.141
  627.3 1.6 slice.133
  628.9 1.0 copy-done.24
  629.9 3.3 convert_element_type.142
  633.2 8.1 %place_columns.1 = (f32[256,5632]{1,0:T(8,128)}, f32[256,5632]{1,0:T(8,128)}) custom-call(s32[4]{0:T(128)} %iota_xor_fusion.order, bf16[4,256,2816]{2,1,0:T(8,128)(2,1)} %get-tuple-element.131.both_ref), custom_call_target="tpu_custom_call" | custom-call | tf_op jit(solution)/shard_map/place_columns/pallas_call | solution.py:700
  641.8 0.8 fusion.45
  642.7 4.4 fusion.24
  (136 shorter events, 13.5 us)
Async XLA Ops:
  7.2 360.3 %reduce-scatter.2.cloned.1.call-start = ((), (), s32[]{:S(2)}) async-start(), calls=%async_computation.1 | async-start | bytes 3604480 | tf_op jit(solution)/shard_map/reduce_scatter | solution.py:1336
  9.2 115.3 %copy-start.19 = (bf16[1,256,2048]{2,1,0:T(8,128)(2,1)S(1)}, bf16[1,256,2048]{2,1,0:T(8,128)(2,1)}, u32[]{:S(2)}) copy-start(bf16[1,256,2048]{2,1,0:T(8,128)(2,1)} %param.13) | copy-start | bytes 3145732
  9.2 115.6 %copy-start.32 = (s32[1,256]{1,0:T(1,128)S(1)}, s32[1,256]{1,0:T(1,128)}, u32[]{:S(2)}) copy-start(s32[1,256]{1,0:T(1,128)} %param.24) | copy-start | bytes 3076
  124.5 3.4 copy-start.26
  131.4 14.0 %collective-permute-start = (bf16[256,512]{1,0:T(8,128)(2,1)}, bf16[256,512]{1,0:T(8,128)(2,1)}, u32[]{:S(2)}, u32[]{:S(2)}) collective-permute-start(bf16[256,512]{1,0:T(8,128)(2,1)} %own_keys.1), channel_id=1, source_target_pairs={{0,8},{8,0},{16,24},{24,16},{1,9},{9,1},{17,25},{25,17},{2,10},{10... | collective-permute-start | bytes 786440 | tf_op jit(solution)/shard_map/ppermute | solution.py:1196
  133.0 21.7 %collective-permute-start.1 = (bf16[256,512]{1,0:T(8,128)(2,1)}, bf16[256,512]{1,0:T(8,128)(2,1)}, u32[]{:S(2)}, u32[]{:S(2)}) collective-permute-start(bf16[256,512]{1,0:T(8,128)(2,1)} %own_keys.1), channel_id=1, source_target_pairs={{0,16},{8,24},{16,0},{24,8},{1,17},{9,25},{17,1},{25,9},{2,18},{10... | collective-permute-start | bytes 786440 | tf_op jit(solution)/shard_map/ppermute | solution.py:1196
  135.4 19.3 %collective-permute-start.2 = (bf16[256,512]{1,0:T(8,128)(2,1)}, bf16[256,512]{1,0:T(8,128)(2,1)}, u32[]{:S(2)}, u32[]{:S(2)}) collective-permute-start(bf16[256,512]{1,0:T(8,128)(2,1)} %own_keys.1), channel_id=1, source_target_pairs={{0,24},{8,16},{16,8},{24,0},{1,25},{9,17},{17,9},{25,1},{2,26},{10... | collective-permute-start | bytes 786440 | tf_op jit(solution)/shard_map/ppermute | solution.py:1196
  135.8 43.7 %collective-permute-start.3 = (bf16[256,2048]{1,0:T(8,128)(2,1)}, bf16[256,2048]{1,0:T(8,128)(2,1)}, u32[]{:S(2)}, u32[]{:S(2)}) collective-permute-start(bf16[256,2048]{1,0:T(8,128)(2,1)} %bitcast.8.refs_1_), channel_id=1, source_target_pairs={{0,2},{1,3},{2,0},{3,1},{4,6},{5,7},{6,4},{7,5},{8,10},{9,11},{10,... | collective-permute-start | bytes 3145736 | tf_op jit(solution)/shard_map/ppermute | solution.py:1186
  137.0 47.1 %collective-permute-start.4 = (bf16[256,2048]{1,0:T(8,128)(2,1)}, bf16[256,2048]{1,0:T(8,128)(2,1)}, u32[]{:S(2)}, u32[]{:S(2)}) collective-permute-start(bf16[256,2048]{1,0:T(8,128)(2,1)} %bitcast.8.refs_1_), channel_id=1, source_target_pairs={{0,4},{1,5},{2,6},{3,7},{4,0},{5,1},{6,2},{7,3},{8,12},{9,13},{10,... | collective-permute-start | bytes 3145736 | tf_op jit(solution)/shard_map/ppermute | solution.py:1186
  138.1 5.8 copy-start.31
  143.9 12.2 %copy-start = (f32[256,128]{1,0:T(8,128)S(1)}, f32[256,128]{1,0:T(8,128)}, u32[]{:S(2)}) copy-start(f32[256,128]{1,0:T(8,128)} %copy.49.sin_ref) | copy-start | bytes 393220
  143.9 12.2 %copy-start.1 = (f32[256,128]{1,0:T(8,128)S(1)}, f32[256,128]{1,0:T(8,128)}, u32[]{:S(2)}) copy-start(f32[256,128]{1,0:T(8,128)} %copy.48.cos_ref) | copy-start | bytes 393220
  145.5 38.7 %collective-permute-start.5 = (bf16[256,2048]{1,0:T(8,128)(2,1)}, bf16[256,2048]{1,0:T(8,128)(2,1)}, u32[]{:S(2)}, u32[]{:S(2)}) collective-permute-start(bf16[256,2048]{1,0:T(8,128)(2,1)} %bitcast.8.refs_1_), channel_id=1, source_target_pairs={{0,6},{1,7},{2,4},{3,5},{4,2},{5,3},{6,0},{7,1},{8,14},{9,15},{10,... | collective-permute-start | bytes 3145736 | tf_op jit(solution)/shard_map/ppermute | solution.py:1186
  154.7 20.9 %slice-start = ((s8[8388608]{0:T(1024)(128)(4,1)}), s8[4194304]{0:T(1024)(128)(4,1)S(1)}, s32[]{:S(2)}) async-start(s8[8388608]{0:T(1024)(128)(4,1)} %bitcast.127), calls=%async_computation.3 | async-start | bytes 8388608
  156.1 19.4 %copy-start.5 = (bf16[1024,512]{1,0:T(8,128)(2,1)}, bf16[1024,512]{1,0:T(8,128)(2,1)S(1)}, u32[]{:S(2)}) copy-start(bf16[1024,512]{1,0:T(8,128)(2,1)S(1)} %pad_maximum_fusion.k_pair.v_pair) | copy-start | bytes 3145732
  156.1 19.5 %slice-start.1 = ((s8[8388608]{0:T(1024)(128)(4,1)}), s8[4194304]{0:T(1024)(128)(4,1)S(1)}, s32[]{:S(2)}) async-start(s8[8388608]{0:T(1024)(128)(4,1)} %bitcast.127), calls=%async_computation.4 | async-start | bytes 8388608
  175.6 2.5 copy-start.3
  175.6 2.5 copy-start.10
  175.6 2.5 copy-start.12
  178.1 98.1 %copy-start.14 = (f32[256,2048]{1,0:T(8,128)}, f32[256,2048]{1,0:T(8,128)S(1)}, u32[]{:S(2)}) copy-start(f32[256,2048]{1,0:T(8,128)S(1)} %get-tuple-element.123) | copy-start | bytes 6291460
  281.9 144.3 %all-gather.2.cloned.1.call-start = ((), (), s32[]{:S(2)}) async-start(), calls=%async_computation.2 | async-start | bytes 3604480 | tf_op jit(solution)/shard_map/all_gather | solution.py:1364
  299.5 5.8 copy-start.15
  299.5 5.8 copy-start.17
  301.8 65.6 %collective-permute-start.6 = (bf16[256,2816]{1,0:T(8,128)(2,1)}, bf16[256,2816]{1,0:T(8,128)(2,1)}, u32[]{:S(2)}, u32[]{:S(2)}) collective-permute-start(bf16[256,2816]{1,0:T(8,128)(2,1)} %get-tuple-element.99), channel_id=1, source_target_pairs={{0,2},{1,3},{2,0},{3,1},{4,6},{5,7},{6,4},{7,5},{8,10},{9,11},{10,... | collective-permute-start | bytes 4325384 | tf_op jit(solution)/shard_map/ppermute | solution.py:1186
  303.1 64.3 %collective-permute-start.7 = (bf16[256,2816]{1,0:T(8,128)(2,1)}, bf16[256,2816]{1,0:T(8,128)(2,1)}, u32[]{:S(2)}, u32[]{:S(2)}) collective-permute-start(bf16[256,2816]{1,0:T(8,128)(2,1)} %get-tuple-element.100), channel_id=1, source_target_pairs={{0,4},{1,5},{2,6},{3,7},{4,0},{5,1},{6,2},{7,3},{8,12},{9,13},{10,... | collective-permute-start | bytes 4325384 | tf_op jit(solution)/shard_map/ppermute | solution.py:1186
  303.8 63.6 %collective-permute-start.8 = (bf16[256,2816]{1,0:T(8,128)(2,1)}, bf16[256,2816]{1,0:T(8,128)(2,1)}, u32[]{:S(2)}, u32[]{:S(2)}) collective-permute-start(bf16[256,2816]{1,0:T(8,128)(2,1)} %get-tuple-element.101), channel_id=1, source_target_pairs={{0,6},{1,7},{2,4},{3,5},{4,2},{5,3},{6,0},{7,1},{8,14},{9,15},{10,... | collective-permute-start | bytes 4325384 | tf_op jit(solution)/shard_map/ppermute | solution.py:1186
  307.9 6.2 copy-start.28
  307.9 6.2 copy-start.6
  307.9 6.2 copy-start.11
  307.9 6.2 copy-start.13
  338.9 26.2 %copy-start.22 = (bf16[256,2048]{1,0:T(8,128)(2,1)S(1)}, bf16[256,2048]{1,0:T(8,128)(2,1)}, u32[]{:S(2)}) copy-start(bf16[256,2048]{1,0:T(8,128)(2,1)} %copy-done.21) | copy-start | bytes 3145732
  366.3 28.3 %collective-permute-start.11 = (bf16[256,1024]{1,0:T(8,128)(2,1)}, bf16[256,1024]{1,0:T(8,128)(2,1)}, u32[]{:S(2)}, u32[]{:S(2)}) collective-permute-start(bf16[256,1024]{1,0:T(8,128)(2,1)} %get-tuple-element.150), channel_id=1, source_target_pairs={{0,1},{1,0},{2,3},{3,2},{4,5},{5,4},{6,7},{7,6},{8,9},{9,8},{10,11... | collective-permute-start | bytes 1572872 | tf_op jit(solution)/shard_map/ppermute | solution.py:1186
  367.5 4.5 copy-start.25
  367.5 4.5 copy-start.27
  373.6 9.5 %copy-start.4 = (bf16[256,2048]{1,0:T(8,128)(2,1)S(1)}, bf16[256,2048]{1,0:T(8,128)(2,1)}, u32[]{:S(2)}) copy-start(bf16[256,2048]{1,0:T(8,128)(2,1)} %copy-done.3) | copy-start | bytes 3145732
  381.8 8.2 %collective-permute-start.13 = (f32[2,4,256]{2,1,0:T(4,128)S(1)}, f32[2,4,256]{2,1,0:T(4,128)S(1)}, u32[]{:S(2)}, u32[]{:S(2)}) collective-permute-start(f32[2,4,256]{2,1,0:T(4,128)S(1)} %bitcast.119), channel_id=1, source_target_pairs={{0,1},{1,0},{2,3},{3,2},{4,5},{5,4},{6,7},{7,6},{8,9},{9,8},{10,11... | collective-permute-start | bytes 24584 | tf_op jit(solution)/shard_map/ppermute | solution.py:1186
  383.0 1.6 copy-start.16
  383.0 2.2 copy-start.18
  383.0 11.6 %collective-permute-start.12 = (bf16[256,2560]{1,0:T(8,128)(2,1)}, bf16[256,2560]{1,0:T(8,128)(2,1)S(1)}, u32[]{:S(2)}, u32[]{:S(2)}) collective-permute-start(bf16[256,2560]{1,0:T(8,128)(2,1)} %constant_dynamic-update-slice_fusion), channel_id=1, source_target_pairs={{0,1},{1,0},{2,3},{3,2},{4,5},{5,4},{6,7},{7,6},{8,9},{9,8},{10,11... | collective-permute-start | bytes 3932168 | tf_op jit(solution)/shard_map/ppermute | solution.py:1186
  383.4 6.7 %collective-permute-start.9 = (bf16[256,1024]{1,0:T(8,128)(2,1)S(1)}, bf16[256,1024]{1,0:T(8,128)(2,1)S(1)}, u32[]{:S(2)}, u32[]{:S(2)}) collective-permute-start(bf16[256,1024]{1,0:T(8,128)(2,1)S(1)} %get-tuple-element.160), channel_id=1, source_target_pairs={{0,1},{1,0},{2,3},{3,2},{4,5},{5,4},{6,7},{7,6},{8,9},{9,8},{10,11... | collective-permute-start | bytes 1572872 | tf_op jit(solution)/shard_map/ppermute | solution.py:1186
  383.9 6.2 collective-permute-start.10
  385.2 4.9 copy-start.29
  390.1 4.5 copy-start.30
  426.2 216.4 %collective-permute-start.14 = (bf16[256,2048]{1,0:T(8,128)(2,1)}, bf16[256,2048]{1,0:T(8,128)(2,1)}, u32[]{:S(2)}, u32[]{:S(2)}) collective-permute-start(bf16[256,2048]{1,0:T(8,128)(2,1)} %get-tuple-element.125), channel_id=1, source_target_pairs={{0,2},{1,3},{2,0},{3,1},{4,6},{5,7},{6,4},{7,5},{8,10},{9,11},{10,... | collective-permute-start | bytes 3145736 | tf_op jit(solution)/shard_map/ppermute | solution.py:1186
  427.7 215.0 %collective-permute-start.15 = (bf16[256,2048]{1,0:T(8,128)(2,1)}, bf16[256,2048]{1,0:T(8,128)(2,1)}, u32[]{:S(2)}, u32[]{:S(2)}) collective-permute-start(bf16[256,2048]{1,0:T(8,128)(2,1)} %get-tuple-element.126), channel_id=1, source_target_pairs={{0,4},{1,5},{2,6},{3,7},{4,0},{5,1},{6,2},{7,3},{8,12},{9,13},{10,... | collective-permute-start | bytes 3145736 | tf_op jit(solution)/shard_map/ppermute | solution.py:1186
  429.2 213.5 %collective-permute-start.16 = (bf16[256,2048]{1,0:T(8,128)(2,1)}, bf16[256,2048]{1,0:T(8,128)(2,1)}, u32[]{:S(2)}, u32[]{:S(2)}) collective-permute-start(bf16[256,2048]{1,0:T(8,128)(2,1)} %get-tuple-element.127), channel_id=1, source_target_pairs={{0,6},{1,7},{2,4},{3,5},{4,2},{5,3},{6,0},{7,1},{8,14},{9,15},{10,... | collective-permute-start | bytes 3145736 | tf_op jit(solution)/shard_map/ppermute | solution.py:1186
  627.3 2.6 copy-start.24
  633.2 9.5 %copy-start.23 = (bf16[256,2048]{1,0:T(8,128)(2,1)S(1)}, bf16[256,2048]{1,0:T(8,128)(2,1)}, u32[]{:S(2)}) copy-start(bf16[256,2048]{1,0:T(8,128)(2,1)} %get-tuple-element.124) | copy-start | bytes 3145732
  (6 other events, 7.0 us)
Sparse Core Ops, SparseCore 0:
  282.0 56.3 reduce-scatter.1
  367.6 58.5 all-gather.1

commit v4 on v3

--- a/solution.py
+++ b/solution.py
@@ -19,7 +19,6 @@
 THETA = 10000.0
 NEG = -1e30
 FLIGHT = 2
-USED = (0, 1, 2, 3)
 BF = jnp.bfloat16
 F32 = jnp.float32
 
@@ -318,33 +317,6 @@
     )(table, qr, grads, o, lse, kv, kv, cosine, sine)
 
 
-def own_keys_kernel(k_ref, v_ref, cos_ref, sin_ref, kv_ref):
-    width = k_ref.shape[1]
-    for p in range(width // LANES):
-        lanes = slice(p * LANES, (p + 1) * LANES)
-        z = k_ref[:, lanes]
-        kv_ref[:, lanes] = (z * cos_ref[...] + swap_halves(z) * sin_ref[...]).astype(BF)
-    kv_ref[:, width:] = v_ref[...].astype(BF)
-
-
-def own_keys(kv, cosine, sine):
-    rows, width = kv.shape[0], KV_HEADS * HEAD_DIM
-    whole = pl.BlockSpec((rows, LANES), lambda i: (0, 0))
-    return pl.pallas_call(
-        own_keys_kernel,
-        grid=(1,),
-        in_specs=[
-            pl.BlockSpec((rows, width), lambda i: (0, 0)),
-            pl.BlockSpec((rows, width), lambda i: (0, 1)),
-            whole,
-            whole,
-        ],
-        out_specs=pl.BlockSpec((rows, 2 * width), lambda i: (0, 0)),
-        out_shape=jax.ShapeDtypeStruct((rows, 2 * width), BF),
-        name="own_keys",
-    )(kv, kv, cosine, sine)
-
-
 def own_key_grads_kernel(nc, dkv_ref, cos_ref, sin_ref, out_ref, got, send_sem, recv_sem):
     rows, width = out_ref.shape[0], out_ref.shape[1] // 2
     here = lax.axis_index("ctx")
@@ -401,19 +373,20 @@
 
 
 def share_kernel(nf, nc, low, size, raw, *refs):
-    w_query, w_key, w_value, w_out, *halves, down, gains = refs[: 8 if raw else 7]
-    refs = refs[8 if raw else 7 :]
-    query, key_value, out, wide, downs, all_gains = refs[:6]
-    query_own, key_value_own, out_own, wide_own, down_own, gains_own = refs[6:12]
-    (local, plane_send, plane_recv, along_send, along_recv, core_send, core_recv) = refs[12:19]
-    (gain_send, gain_recv, down_sem, gather_send, gather_recv, gather_core) = refs[19:]
+    count = 2 if raw else 1
+    w_query, w_key, w_value, w_out, *halves, down, gains, tokens, cosine, sine = refs[: 9 + count]
+    refs = refs[9 + count :]
+    query, key_value, out, wide, downs, all_gains, kv_all = refs[:7]
+    query_own, key_value_own, out_own, wide_own, down_own, gains_own = refs[7:13]
+    (local, plane_send, plane_recv, along_send, along_recv, core_send, core_recv) = refs[13:20]
+    (gain_send, gain_recv, down_sem, gather_send, gather_recv, gather_core) = refs[20:26]
+    w_kv, gains_v, xn, kv, kv_load, kv_send, kv_recv = refs[26:]
     chips = nf // 2
     place, here = lax.axis_index("fsdp"), lax.axis_index("ctx")
     chip, core = place // 2, place % 2
     mesh_id = pl.DeviceIdType.MESH
     shard, columns = wide.shape[1:]
     part = columns // 2
-    count = len(halves)
     key_width = w_key.shape[1]
     gathered = [
         (w_query, query, query_own, pl.ds(0, w_query.shape[1])),
@@ -433,10 +406,11 @@
 
         @pl.when(here == pos)
         def _():
-            near = [i for i in (pos - 1, pos + 1) if 0 <= i < nc]
-            for i in near:
-                greet({"ctx": i})
-            pl.semaphore_wait(barrier, nf - 1 + len(near))
+            for i in range(nc):
+                if i != pos:
+                    greet({"ctx": i})
+
+    pl.semaphore_wait(barrier, nf - 1 + nc - 1)
 
     def remote(source, target, sends, recvs, where):
         return pltpu.make_async_remote_copy(
@@ -538,16 +512,16 @@
         gain_copy(j).start()
     for h in range(count):
         own_core_copy(h).start()
-    for u in USED:
+    for u in range(4):
         gather_core_copy(u, 0).start()
     down_copy().start()
-    own = [(source, stage.at[:, at], None) for source, _, stage, at in (gathered[u] for u in USED)]
+    own = [(source, stage.at[:, at], None) for source, _, stage, at in gathered]
     own += [(piece(0, h, pl.ds(0, shard)), wide_own.at[:, side(h)], None) for h in range(count)]
     own += [(down, down_own, downs.at[core]), (gains, gains_own, all_gains.at[place])]
-    back = [(query_own, query.at[place]), (key_value_own, key_value.at[place])]
-    if 3 in USED:
-        back.append((out_own, out.at[place]))
-    back += [
+    back = [
+        (query_own, query.at[place]),
+        (key_value_own, key_value.at[place]),
+        (out_own, out.at[place]),
         (wide_own, wide.at[place]),
         (down_own, downs.at[core]),
         (gains_own, all_gains.at[place]),
@@ -562,9 +536,52 @@
     for k in range(1, chips):
         for h in range(count):
             plane_copy(k, 1, h).wait_send()
-    for u in USED:
+    for u in (1, 2, 0, 3):
         for k in direct:
             gather_copy(u, k).start()
+
+    def kv_copy(k):
+        if k == 0:
+            return pltpu.make_async_copy(kv, kv_all.at[0], kv_recv.at[0])
+        return remote(kv, kv_all.at[k], kv_send.at[k], kv_recv.at[k], {"ctx": here ^ k})
+
+    def make_kv():
+        for i in (len(back) - 1, 1):
+            stage, target = back[i]
+            pltpu.make_async_copy(stage, target, local.at[1, i]).wait()
+        for j in range(1, nf):
+            gain_copy(j).wait_recv()
+        for u in (1, 2):
+            if relayed:
+                for k in direct:
+                    gather_copy(u, k, 1).wait_recv()
+                gather_core_copy(u, 3).start()
+            for k in range(chips):
+                gather_core_copy(u, k).wait_recv()
+        loads = [
+            pltpu.make_async_copy(key_value, w_kv, kv_load.at[0]),
+            pltpu.make_async_copy(all_gains, gains_v, kv_load.at[1]),
+        ]
+        for copy in loads:
+            copy.start()
+        for copy in loads:
+            copy.wait()
+        for i in range(0, xn.shape[0], 16):
+            x = tokens[i : i + 16, :].astype(F32)
+            unit = x * lax.rsqrt(jnp.mean(x * x, axis=1, keepdims=True) + EPS)
+            for f in range(nf):
+                lanes = slice(f * shard, (f + 1) * shard)
+                gain = gains_v[f, 0:1, :].astype(F32)
+                xn[i : i + 16, lanes] = (unit[:, lanes] * gain).astype(BF)
+        total = sum(
+            dot(xn[:, f * shard : (f + 1) * shard], w_kv[f], (1, 0)) for f in range(nf)
+        )
+        for p in range(0, key_width, LANES):
+            z = total[:, p : p + LANES]
+            kv[:, p : p + LANES] = (z * cosine[...] + swap_halves(z) * sine[...]).astype(BF)
+        kv[:, key_width:] = total[:, key_width:].astype(BF)
+        for k in reversed(range(nc)):
+            kv_copy(k).start()
 
     for pos in range(nc):
 
@@ -585,25 +602,31 @@
                 for k in range(1, chips):
                     for h in range(count):
                         plane_copy(k, 0, h).start()
-            for u in USED:
+            def gather_on(u):
                 for k in direct:
                     gather_copy(u, k).wait_recv()
                     if relayed:
                         gather_copy(u, 3 - k, 1).start()
                     gather_core_copy(u, k).start()
-            for d in range(1, nc):
+
+            groups = [(), (1, 2), (0, 3)]
+            for d in range(1, max(nc, len(groups))):
                 for share in (pos - d, pos + d):
                     if 0 <= share < nc:
                         for k in range(1, chips):
                             along_copy(k, share, 0, 0).wait_recv()
                             pass_on(k, share)
+                for u in groups[d] if d < len(groups) else ():
+                    if u == 3:
+                        make_kv()
+                    gather_on(u)
             if low:
                 for k in range(1, chips):
                     for h in range(count):
                         plane_copy(k, 0, h).wait_recv()
                     core_copy(k, nc).start()
             if relayed:
-                for u in USED:
+                for u in (0, 3):
                     for k in direct:
                         gather_copy(u, k, 1).wait_recv()
                     gather_core_copy(u, 3).start()
@@ -623,24 +646,44 @@
             for h in range(count):
                 plane_copy(k, 0, h).wait_send()
     for j in range(1, nf):
-        gain_copy(j).wait()
-    for u in USED:
+        gain_copy(j).wait_send()
+    for k in range(nc):
+        kv_copy(k).wait()
+    for u in range(4):
         for k in direct:
             gather_copy(u, k).wait_send()
             if relayed:
                 gather_copy(u, k, 1).wait_send()
         for k in range(chips):
-            gather_core_copy(u, k).wait()
+            gather_core_copy(u, k).wait_send()
+            if u in (0, 3):
+                gather_core_copy(u, k).wait_recv()
     down_copy().wait()
     for i, (stage, target) in enumerate(back):
-        pltpu.make_async_copy(stage, target, local.at[1, i]).wait()
-
-
-def share_weights(nf, nc, w_query, w_key, w_value, w_out, w_gate, w_up, order, down, gains):
+        if i not in (len(back) - 1, 1):
+            pltpu.make_async_copy(stage, target, local.at[1, i]).wait()
+
+
+def share_weights(
+    nf,
+    nc,
+    w_query,
+    w_key,
+    w_value,
+    w_out,
+    w_gate,
+    w_up,
+    order,
+    down,
+    gains,
+    tokens,
+    cosine,
+    sine,
+):
     chips = nf // 2
     shard, hidden = w_gate.shape
     part = hidden // chips
-    size = 16 * max(1, (shard * 3 // 4) // (16 * nc))
+    size = shard // nc
     low = shard - nc * size
     raw = part % 128 == 0
     halves = [w_gate, w_up]
@@ -649,15 +692,17 @@
         halves = [jnp.take(jnp.concatenate(both, axis=2), order, axis=0)]
     anywhere = pl.BlockSpec(memory_space=pl.ANY)
     dma = pltpu.SemaphoreType.DMA
+    kv_shape = (tokens.shape[0], 2 * w_key.shape[1])
     widths = [w_query.shape[1], 2 * w_key.shape[1], w_out.shape[1], 2 * part]
     return pl.pallas_call(
         functools.partial(share_kernel, nf, nc, low, size, raw),
-        in_specs=[anywhere] * (6 + len(halves)),
-        out_specs=[anywhere] * 6,
+        in_specs=[anywhere] * (6 + len(halves)) + [pl.BlockSpec(memory_space=pltpu.VMEM)] * 3,
+        out_specs=[anywhere] * 7,
         out_shape=[jax.ShapeDtypeStruct((nf, shard, width), BF) for width in widths]
         + [
             jax.ShapeDtypeStruct((2,) + down.shape, BF),
             jax.ShapeDtypeStruct((nf,) + gains.shape, BF),
+            jax.ShapeDtypeStruct((nc,) + kv_shape, BF),
         ],
         scratch_shapes=[pltpu.VMEM((shard, width), BF) for width in widths]
         + [
@@ -676,12 +721,19 @@
             dma((4, 2 * chips)),
             dma((4, 2 * chips)),
             dma((2, 4, chips)),
+            pltpu.VMEM((nf, shard, widths[1]), BF),
+            pltpu.VMEM((nf,) + gains.shape, BF),
+            pltpu.VMEM(tokens.shape, BF),
+            pltpu.VMEM(kv_shape, BF),
+            dma((2,)),
+            dma((nc,)),
+            dma((nc,)),
         ],
         compiler_params=pltpu.CompilerParams(
             collective_id=1, has_side_effects=True, vmem_limit_bytes=56 << 20
         ),
         name="share_weights",
-    )(w_query, w_key, w_value, w_out, *halves, down, gains)
+    )(w_query, w_key, w_value, w_out, *halves, down, gains, tokens, cosine, sine)
 
 
 def place_columns_kernel(order, both_ref, gate_ref, up_ref):
@@ -1236,9 +1288,26 @@
             return dot(left, right, (0, 0)).astype(BF).reshape(chips, shard, right.shape[1])
 
 
+        half = HEAD_DIM // 2
+        frequency = THETA ** (-jnp.arange(half, dtype=F32) * (2.0 / HEAD_DIM))
+        angle = positions[0].astype(F32)[:, None] * frequency[None, :]
+        cosine, sine = jnp.cos(angle), jnp.sin(angle)
+        cos_lanes = jnp.tile(cosine, (1, 4))
+        sin_lanes = jnp.tile(jnp.concatenate([-sine, sine], axis=1), (1, 2))
+        blocks = 2 * nc
+        stored = block_table.reshape(-1)
+        number = jnp.arange(blocks, dtype=jnp.int32)
+        where = jnp.sum(
+            jnp.where(stored[None, :] == number[:, None], number[None, :], 0), axis=1
+        )
+        here = lax.axis_index("ctx")
+        own = lax.dynamic_slice_in_dim(stored, 2 * here, 2)
+        where = 2 * ((where // 2) ^ here) + where % 2
+        table = jnp.concatenate([own, where]).astype(jnp.int32)
+
         order = chip ^ jnp.arange(chips, dtype=jnp.int32)
         both_gains = jnp.pad(jnp.stack([attn_gain, ffn_gain]), ((0, 14), (0, 0)))
-        w_q, w_kv, w_o, w_gu, w_d, gains = share_weights(
+        w_q, w_kv, w_o, w_gu, w_d, gains, kv = share_weights(
             nf,
             nc,
             w_query,
@@ -1250,43 +1319,24 @@
             order,
             w_down,
             both_gains,
+            tokens[0],
+            cos_lanes,
+            sin_lanes,
         )
         w_q = w_q.reshape(width, -1)
         w_kv = w_kv.reshape(width, -1)
         gb_sent, w_kv = lax.optimization_barrier((gb, w_kv))
-        if 3 in USED:
-            w_o = w_o.reshape(-1, width)
-        else:
-            w_out, w_kv = lax.optimization_barrier((w_out, w_kv))
-            w_o = lax.all_gather(w_out, "fsdp", axis=0, tiled=True)
+        w_o = w_o.reshape(-1, width)
         w_gu = w_gu.reshape(width, 2 * part)
         w_d = w_d.reshape(part, width)
         gains = gains[:, :2].astype(F32).transpose(1, 0, 2).reshape(2, width)
 
-        half = HEAD_DIM // 2
-        frequency = THETA ** (-jnp.arange(half, dtype=F32) * (2.0 / HEAD_DIM))
-        angle = positions[0].astype(F32)[:, None] * frequency[None, :]
-        cosine, sine = jnp.cos(angle), jnp.sin(angle)
-        cos_lanes = jnp.tile(cosine, (1, 4))
-        sin_lanes = jnp.tile(jnp.concatenate([-sine, sine], axis=1), (1, 2))
-        blocks = 2 * nc
-        stored = block_table.reshape(-1)
-        number = jnp.arange(blocks, dtype=jnp.int32)
-        where = jnp.sum(
-            jnp.where(stored[None, :] == number[:, None], number[None, :], 0), axis=1
-        )
-        here = lax.axis_index("ctx")
-        own = lax.dynamic_slice_in_dim(stored, 2 * here, 2)
-        where = 2 * ((where // 2) ^ here) + where % 2
-        table = jnp.concatenate([own, where]).astype(jnp.int32)
-
         inverse_one = lax.rsqrt(jnp.mean(x * x, axis=1, keepdims=True) + EPS)
         unit_one = x * inverse_one
         xn = (unit_one * gains[0][None, :]).astype(BF)
-        kv = own_keys(dot(xn, w_kv, (1, 0)), cos_lanes, sin_lanes)
         q_sum = dot(xn, w_q, (1, 0))
         gb_of = [gb] + [swap(gb_sent, 2 * k) for k in range(1, chips)]
-        kv = jnp.concatenate([cross(kv, k) if k else kv for k in range(nc)], axis=0)
+        kv = kv.reshape(nc * rows, 2 * key_width)
         qr, o, ob, lse = attention_forward(table, q_sum, cos_lanes, sin_lanes, kv)
         h1 = x + dot(ob, w_o, (1, 0))
         inverse_two = lax.rsqrt(jnp.mean(h1 * h1, axis=1, keepdims=True) + EPS)

time: 659 us -> 647 us (0.982)
    ppermute x3 -> x0, waiting for transfers between devices: 7.99 us -> none  [cross(): return lax.ppermute(x, 'ctx', [(i, i ^ k) for i in range(nc)])]
    dot_general x9 -> x8, matrix products: 52.5 us -> 51.3 us  [dot(): lax.dot_general(left, right, ((contract[:1], contract[1:]), ((), ())), pr...]
  transfers between devices with their start and end apart: 19 -> 16, of which waited for: 4 -> 3; matrix products, arithmetic and copies ran while one was open for 12% -> 13% of each run, Pallas kernels for 42% -> 42%
where the time goes in v4:
time: 647 us; the launch traced here: 641 us
  Pallas kernels  476 us (74%)
  matrix products  51.3 us (8%)
  waiting for transfers between devices  33.9 us (5%)
  other arithmetic  29 us (4%)
  local copies, waits for them, and re-layouts  23.7 us (4%)
  between operations  14.9 us (2%)
  starting transfers between devices  11.9 us (2%)
    pallas_call x1, Pallas kernels, finish(): pl.pallas_call(functools.partial(finish_kernel, nf, nc), in_specs=[anywhe...  196 us
    pallas_call x1, Pallas kernels, share_weights(): pl.pallas_call(functools.partial(share_kernel, nf, nc, low, size, raw), i...  113 us
    pallas_call x1, Pallas kernels, feed_forward(): pl.pallas_call(functools.partial(feed_forward_kernel, nf), in_specs=[anyw...  92 us
    dot_general x8, matrix products, dot(): lax.dot_general(left, right, ((contract[:1], contract[1:]), ((), ())), pr...  51.3 us
    pallas_call x1, Pallas kernels, own_key_grads(): pl.pallas_call(functools.partial(own_key_grads_kernel, nc), in_specs=[pl....  25.1 us
    all_gather x1, waiting for transfers between devices, shards(): down_sum = lax.all_gather(down_sum, 'ctx', axis=0, tiled=True)  24.4 us
    pallas_call x1, Pallas kernels, attention_backward(): pl.pallas_call(attention_backward_kernel, grid_spec=pltpu.PrefetchScalarG...  22.6 us
    pallas_call x1, Pallas kernels, attention_forward(): pl.pallas_call(attention_forward_kernel, grid_spec=pltpu.PrefetchScalarGr...  19.5 us
  transfers between devices with their start and end apart: 16, of which 3 were waited for; matrix products, arithmetic and copies ran while one was open for 13% of the time, Pallas kernels for 42%

profile of v4, /device:TPU:0, one launch (start us, length us, event | category | flops | bytes accessed | tf_op | source)
XLA Modules:
  0.0 640.7 jit_solution(1802665431400009191)
XLA Ops:
  8.2 0.8 copy.47.refs_10_.sin_ref
  8.9 0.8 copy.46.refs_9_.cos_ref
  11.6 112.7 %share_weights.1 = (bf16[8,256,2048]{2,1,0:T(8,128)(2,1)}, bf16[8,256,512]{2,1,0:T(8,128)(2,1)}, bf16[8,256,2048]{2,1,0:T(8,128)(2,1)}, bf16[8,256,2816]{2,1,0:T...) custom-call(bf16[256,2048]{1,0:T(8,128)(2,1)} %refs_0_.1, ...), custom_call_target="tpu_custom_call" | custom-call | tf_op jit(solution)/shard_map/share_weights/pallas_call | solution.py:697
  124.9 1.5 collective-permute-start.1
  126.4 1.4 collective-permute-start.2
  128.1 0.8 convert_bitcast_fusion
  129.4 5.9 fusion.20.q_ref
  135.4 19.5 %attention_forward.1 = (bf16[256,2048]{1,0:T(8,128)(2,1)S(1)}, f32[256,2048]{1,0:T(8,128)S(1)}, bf16[256,2048]{1,0:T(8,128)(2,1)S(1)}, f32[4,2,1024]{2,1,0:T(2,128)S(1)}) custom-call(s32[10]{0:T(128)S(1)} %pad_add_fusion.table, f32[256,2048]{1,0:T(8,128)S(1)} %fusion.20.q_ref, f32[256,128]{1,0:T(8,128)S(1)} %copy-done.1, f32[256,128]{1,0:T(8,128)S(1)} %copy-done, ...), custom_call_target="tpu_custom_call" | custom-call | flops 4294967296 | bytes 8388608 | tf_op jit(solution)/shard_map/attention_forward/pallas_call | solution.py:154
  154.9 1.3 copy-done.9
  156.2 1.0 copy-done.11
  157.1 1.0 copy-done.3
  158.1 3.7 multiply_reduce_fusion.2
  162.4 2.8 multiply_convert_fusion.refs_0_
  165.2 5.9 collective-permute-done.1.refs_3_
  171.1 92.0 %feed_forward.1 = (f32[256,2048]{1,0:T(8,128)}, bf16[2,4,256,1024]{3,2,1,0:T(8,128)(2,1)}, bf16[2,4,256,2816]{3,2,1,0:T(8,128)(2,1)}, bf16[2,704,2048]{2,1,0:T(8,128)(2,1)}, bf16[4,256,2048]{2,1,0:T(8,128)(2,1)}) custom-call(bf16[256,2048]{1,0:T(8,128)(2,1)} %multiply_convert_fusion.refs_0_, bf16[256,2048]{1,0:T(8,128)(2,1)} %bitcast.85, ...), custom_call_target="tpu_custom_call" | custom-call | flops 35433480192 | bytes 40000000 | tf_op jit(solution)/shard_map/feed_forward/pallas_call | solution.py:995
  263.1 5.7 fusion.4
  268.8 17.7 %convolution_convert_fusion.1 = bf16[1024,2816]{1,0:T(8,128)(2,1)S(1)} fusion(bf16[2048,1024]{1,0:T(8,128)(2,1)} %bitcast.113, bf16[2048,2816]{1,0:T(8,128)(2,1)} %bitcast.110), kind=kOutput, calls=%fused_computation.2 | convolution fusion | flops 11814043648 | bytes 21495808 | tf_op jit(solution)/shard_map/dot_general | solution.py:27
  286.6 2.3 dynamic-slice_bitcast_fusion
  289.5 1.4 collective-permute-start.4
  290.9 1.5 collective-permute-start.5
  293.8 6.2 convolution_convert_fusion.3.do_ref
  300.0 22.6 %attention_backward.1 = (bf16[256,2048]{1,0:T(8,128)(2,1)S(1)}, bf16[2,1024,256]{2,1,0:T(8,128)(2,1)S(1)}) custom-call(s32[10]{0:T(128)S(1)} %pad_add_fusion.table, bf16[256,2048]{1,0:T(8,128)(2,1)S(1)} %copy-done.12, bf16[256,2048]{1,0:T(8,128)(2,1)S(1)} %convolution_convert_fusion.3.do_ref, f32[256,2048]{1,0:T(8,128)S(1)} %copy-done.10, ...), custom_call_target="tpu_custom_call" | custom-call | flops 10737418240 | bytes 8388608 | tf_op jit(solution)/shard_map/attention_backward/pallas_call | solution.py:280
  322.6 1.0 copy-done.2
  323.6 1.0 copy-done.5
  324.6 25.1 %own_key_grads.1 = bf16[256,512]{1,0:T(8,128)(2,1)} custom-call(bf16[2,1024,256]{2,1,0:T(8,128)(2,1)} %copy-done.2, f32[256,128]{1,0:T(8,128)} %copy.46.refs_9_.cos_ref, f32[256,128]{1,0:T(8,128)} %copy.47.refs_10_.sin_ref), custom_call_target="tpu_custom_call" | custom-call | tf_op jit(solution)/shard_map/own_key_grads/pallas_call | solution.py:360
  349.6 4.5 slice_bitcast_fusion
  354.2 1.0 constant_dynamic-update-slice_fusion.1
  355.9 6.0 fusion.45
  361.9 2.8 fusion.10
  364.7 1.3 stack.21
  366.0 0.7 constant_dynamic-update-slice_fusion.3
  366.7 0.7 constant_dynamic-update-slice_fusion.2
  367.5 0.7 broadcast_multiply_fusion
  368.2 5.6 fusion.14
  375.8 3.5 collective-permute-done.6
  379.3 4.4 convolution_convert_fusion.2
  383.7 4.7 convolution_convert_fusion
  388.4 24.4 %all-gather.2.cloned.1.call-done = bf16[704,2048]{1,0:T(8,128)(2,1)} async-done(((bf16[176,2048]{1,0:T(8,128)(2,1)}), bf16[704,2048]{1,0:T(8,128)(2,1)}) %all-gather.2.cloned.1.call-update) | async-done | bytes 2883600 | tf_op jit(solution)/shard_map/all_gather | solution.py:1414
  412.8 1.5 collective-permute-start.11
  414.3 1.5 collective-permute-start.12
  416.3 196.0 %finish.1 = (bf16[4,256,2816]{2,1,0:T(8,128)(2,1)}, bf16[256,2048]{1,0:T(8,128)(2,1)S(1)}, bf16[256,2560]{1,0:T(8,128)(2,1)S(1)}, bf16[16,512]{1,0:T(8,128)(2,1)S(1)}) custom-call(bf16[256,2816]{1,0:T(8,128)(2,1)S(1)} %get-tuple-element.117.refs_0_, bf16[256,2816]{1,0:T(8,128)(2,1)} %collective-permute-done.3.refs_1_, ...), custom_call_target="tpu_custom_call" | custom-call | flops 199999995904 | bytes 60000000 | tf_op jit(solution)/shard_map/finish/pallas_call | solution.py:1213
  612.4 1.6 convert_element_type.137
  613.9 1.6 slice.133
  615.5 1.0 copy-done.21
  616.5 3.3 convert_element_type.138
  619.8 8.1 %place_columns.1 = (f32[256,5632]{1,0:T(8,128)}, f32[256,5632]{1,0:T(8,128)}) custom-call(s32[4]{0:T(128)} %iota_xor_fusion.order, bf16[4,256,2816]{2,1,0:T(8,128)(2,1)} %get-tuple-element.133.both_ref), custom_call_target="tpu_custom_call" | custom-call | tf_op jit(solution)/shard_map/place_columns/pallas_call | solution.py:752
  628.5 0.8 fusion.40
  629.3 4.3 fusion.22
  (125 shorter events, 10.6 us)
Async XLA Ops:
  7.2 347.0 %reduce-scatter.2.cloned.1.call-start = ((), (), s32[]{:S(2)}) async-start(), calls=%async_computation.1 | async-start | bytes 3604480 | tf_op jit(solution)/shard_map/reduce_scatter | solution.py:1386
  11.6 112.7 %copy-start.19 = (bf16[1,256,2048]{2,1,0:T(8,128)(2,1)S(1)}, bf16[1,256,2048]{2,1,0:T(8,128)(2,1)}, u32[]{:S(2)}) copy-start(bf16[1,256,2048]{2,1,0:T(8,128)(2,1)} %param.25) | copy-start | bytes 3145732
  11.6 116.3 %copy-start.16 = (bf16[1,256,2048]{2,1,0:T(8,128)(2,1)S(1)}, bf16[1,256,2048]{2,1,0:T(8,128)(2,1)}, u32[]{:S(2)}) copy-start(bf16[1,256,2048]{2,1,0:T(8,128)(2,1)} %param.13) | copy-start | bytes 3145732
  11.6 117.4 %copy-start.33 = (s32[4,2]{0,1:T(2,128)S(1)}, s32[4,2]{0,1:T(2,128)}, u32[]{:S(2)}) copy-start(s32[4,2]{0,1:T(2,128)} %param.23) | copy-start | bytes 100
  124.3 40.9 %collective-permute-start = (bf16[256,2048]{1,0:T(8,128)(2,1)S(1)}, bf16[256,2048]{1,0:T(8,128)(2,1)}, u32[]{:S(2)}, u32[]{:S(2)}) collective-permute-start(bf16[256,2048]{1,0:T(8,128)(2,1)S(1)} %bitcast.86), channel_id=1, source_target_pairs={{0,2},{1,3},{2,0},{3,1},{4,6},{5,7},{6,4},{7,5},{8,10},{9,11},{10,... | collective-permute-start | bytes 3145736 | tf_op jit(solution)/shard_map/ppermute | solution.py:1238
  124.9 46.2 %collective-permute-start.1 = (bf16[256,2048]{1,0:T(8,128)(2,1)S(1)}, bf16[256,2048]{1,0:T(8,128)(2,1)}, u32[]{:S(2)}, u32[]{:S(2)}) collective-permute-start(bf16[256,2048]{1,0:T(8,128)(2,1)S(1)} %bitcast.87), channel_id=1, source_target_pairs={{0,4},{1,5},{2,6},{3,7},{4,0},{5,1},{6,2},{7,3},{8,12},{9,13},{10,... | collective-permute-start | bytes 3145736 | tf_op jit(solution)/shard_map/ppermute | solution.py:1238
  126.4 44.7 %collective-permute-start.2 = (bf16[256,2048]{1,0:T(8,128)(2,1)S(1)}, bf16[256,2048]{1,0:T(8,128)(2,1)}, u32[]{:S(2)}, u32[]{:S(2)}) collective-permute-start(bf16[256,2048]{1,0:T(8,128)(2,1)S(1)} %bitcast.88), channel_id=1, source_target_pairs={{0,6},{1,7},{2,4},{3,5},{4,2},{5,3},{6,0},{7,1},{8,14},{9,15},{10,... | collective-permute-start | bytes 3145736 | tf_op jit(solution)/shard_map/ppermute | solution.py:1238
  128.9 6.4 copy-start.28
  129.0 6.4 copy-start.30
  129.4 5.9 copy-start
  129.4 5.9 copy-start.1
  129.4 5.9 copy-start.7
  135.4 22.7 %copy-start.34 = (bf16[8,256,2048]{2,1,0:T(8,128)(2,1)S(1)}, bf16[8,256,2048]{2,1,0:T(8,128)(2,1)}, u32[]{:S(2)}) copy-start(bf16[8,256,2048]{2,1,0:T(8,128)(2,1)} %get-tuple-element.78) | copy-start | bytes 25165828
  154.8 1.3 copy-start.9
  157.1 1.0 copy-start.3
  268.8 144.1 %all-gather.2.cloned.1.call-start = ((), (), s32[]{:S(2)}) async-start(), calls=%async_computation.2 | async-start | bytes 3604480 | tf_op jit(solution)/shard_map/all_gather | solution.py:1414
  286.6 5.8 copy-start.13
  286.6 5.8 copy-start.15
  288.9 4.1 copy-start.20
  288.9 65.2 %collective-permute-start.3 = (bf16[256,2816]{1,0:T(8,128)(2,1)}, bf16[256,2816]{1,0:T(8,128)(2,1)}, u32[]{:S(2)}, u32[]{:S(2)}) collective-permute-start(bf16[256,2816]{1,0:T(8,128)(2,1)} %get-tuple-element.100), channel_id=1, source_target_pairs={{0,2},{1,3},{2,0},{3,1},{4,6},{5,7},{6,4},{7,5},{8,10},{9,11},{10,... | collective-permute-start | bytes 4325384 | tf_op jit(solution)/shard_map/ppermute | solution.py:1238
  289.5 64.6 %collective-permute-start.4 = (bf16[256,2816]{1,0:T(8,128)(2,1)}, bf16[256,2816]{1,0:T(8,128)(2,1)}, u32[]{:S(2)}, u32[]{:S(2)}) collective-permute-start(bf16[256,2816]{1,0:T(8,128)(2,1)} %get-tuple-element.101), channel_id=1, source_target_pairs={{0,4},{1,5},{2,6},{3,7},{4,0},{5,1},{6,2},{7,3},{8,12},{9,13},{10,... | collective-permute-start | bytes 4325384 | tf_op jit(solution)/shard_map/ppermute | solution.py:1238
  290.9 63.2 %collective-permute-start.5 = (bf16[256,2816]{1,0:T(8,128)(2,1)}, bf16[256,2816]{1,0:T(8,128)(2,1)}, u32[]{:S(2)}, u32[]{:S(2)}) collective-permute-start(bf16[256,2816]{1,0:T(8,128)(2,1)} %get-tuple-element.102), channel_id=1, source_target_pairs={{0,6},{1,7},{2,4},{3,5},{4,2},{5,3},{6,0},{7,1},{8,14},{9,15},{10,... | collective-permute-start | bytes 4325384 | tf_op jit(solution)/shard_map/ppermute | solution.py:1238
  293.7 6.2 copy-start.25
  293.7 6.2 copy-start.8
  293.8 6.2 copy-start.10
  293.8 6.2 copy-start.12
  322.6 1.0 copy-start.2
  349.6 4.6 copy-start.6
  355.8 6.0 copy-start.17
  355.8 6.1 copy-start.22
  355.8 6.1 copy-start.24
  355.8 6.1 copy-start.29
  355.8 6.1 copy-start.31
  361.9 6.3 copy-start.14
  367.4 8.3 %collective-permute-start.10 = (f32[2,4,256]{2,1,0:T(4,128)S(1)}, f32[2,4,256]{2,1,0:T(4,128)S(1)}, u32[]{:S(2)}, u32[]{:S(2)}) collective-permute-start(f32[2,4,256]{2,1,0:T(4,128)S(1)} %bitcast.100), channel_id=1, source_target_pairs={{0,1},{1,0},{2,3},{3,2},{4,5},{5,4},{6,7},{7,6},{8,9},{9,8},{10,11... | collective-permute-start | bytes 24584 | tf_op jit(solution)/shard_map/ppermute | solution.py:1238
  368.2 5.7 copy-start.26
  368.2 6.2 copy-start.23
  368.2 6.2 copy-start.27
  368.2 6.3 copy-start.4
  373.9 5.4 collective-permute-start.7
  374.4 9.3 %collective-permute-start.9 = (bf16[256,2560]{1,0:T(8,128)(2,1)S(1)}, bf16[256,2560]{1,0:T(8,128)(2,1)S(1)}, u32[]{:S(2)}, u32[]{:S(2)}) collective-permute-start(bf16[256,2560]{1,0:T(8,128)(2,1)S(1)} %constant_dynamic-update-slice_fusion), channel_id=1, source_target_pairs={{0,1},{1,0},{2,3},{3,2},{4,5},{5,4},{6,7},{7,6},{8,9},{9,8},{10,11... | collective-permute-start | bytes 3932168 | tf_op jit(solution)/shard_map/ppermute | solution.py:1238
  374.8 4.5 collective-permute-start.6
  375.6 8.1 %collective-permute-start.8 = (bf16[256,1024]{1,0:T(8,128)(2,1)S(1)}, bf16[256,1024]{1,0:T(8,128)(2,1)S(1)}, u32[]{:S(2)}, u32[]{:S(2)}) collective-permute-start(bf16[256,1024]{1,0:T(8,128)(2,1)S(1)} %get-tuple-element.154), channel_id=1, source_target_pairs={{0,1},{1,0},{2,3},{3,2},{4,5},{5,4},{6,7},{7,6},{8,9},{9,8},{10,11... | collective-permute-start | bytes 1572872 | tf_op jit(solution)/shard_map/ppermute | solution.py:1238
  412.8 216.5 %collective-permute-start.11 = (bf16[256,2048]{1,0:T(8,128)(2,1)}, bf16[256,2048]{1,0:T(8,128)(2,1)}, u32[]{:S(2)}, u32[]{:S(2)}) collective-permute-start(bf16[256,2048]{1,0:T(8,128)(2,1)} %get-tuple-element.127), channel_id=1, source_target_pairs={{0,2},{1,3},{2,0},{3,1},{4,6},{5,7},{6,4},{7,5},{8,10},{9,11},{10,... | collective-permute-start | bytes 3145736 | tf_op jit(solution)/shard_map/ppermute | solution.py:1238
  414.3 215.0 %collective-permute-start.12 = (bf16[256,2048]{1,0:T(8,128)(2,1)}, bf16[256,2048]{1,0:T(8,128)(2,1)}, u32[]{:S(2)}, u32[]{:S(2)}) collective-permute-start(bf16[256,2048]{1,0:T(8,128)(2,1)} %get-tuple-element.128), channel_id=1, source_target_pairs={{0,4},{1,5},{2,6},{3,7},{4,0},{5,1},{6,2},{7,3},{8,12},{9,13},{10,... | collective-permute-start | bytes 3145736 | tf_op jit(solution)/shard_map/ppermute | solution.py:1238
  415.8 213.5 %collective-permute-start.13 = (bf16[256,2048]{1,0:T(8,128)(2,1)}, bf16[256,2048]{1,0:T(8,128)(2,1)}, u32[]{:S(2)}, u32[]{:S(2)}) collective-permute-start(bf16[256,2048]{1,0:T(8,128)(2,1)} %get-tuple-element.129), channel_id=1, source_target_pairs={{0,6},{1,7},{2,4},{3,5},{4,2},{5,3},{6,0},{7,1},{8,14},{9,15},{10,... | collective-permute-start | bytes 3145736 | tf_op jit(solution)/shard_map/ppermute | solution.py:1238
  613.9 2.6 copy-start.21
  619.8 9.5 %copy-start.18 = (bf16[256,2048]{1,0:T(8,128)(2,1)S(1)}, bf16[256,2048]{1,0:T(8,128)(2,1)}, u32[]{:S(2)}) copy-start(bf16[256,2048]{1,0:T(8,128)(2,1)} %get-tuple-element.126) | copy-start | bytes 3145732
  (3 other events, 2.6 us)
Sparse Core Ops, SparseCore 0:
  268.9 55.6 reduce-scatter.1
  354.3 58.4 all-gather.1

commit v5 on v4

--- a/solution.py
+++ b/solution.py
@@ -766,7 +766,7 @@
     chips = nf // 2
     hn, *gbs, w_gu, w_d, grad, left, right, downs, outs = refs[: chips + 8]
     w_gu_v, w_d_v, hn_v, gb_v, dact_v, act_v, dgu_v, sent, got, outs_v = refs[chips + 8 : chips + 18]
-    tiles, *sems = refs[chips + 18 :]
+    tiles, halves, half_sem, *sems = refs[chips + 18 :]
     load, load_gb, hn_send, hn_recv, dhn_send, dhn_recv, store = sems[:7]
     left_local, left_send, left_recv, right_local, right_send, right_recv = sems[7:13]
     down_local, down_send, down_recv = sems[13:]
@@ -808,6 +808,12 @@
 
     def dhn_copy(k):
         return remote(sent.at[k - 1], got.at[k - 1], dhn_send.at[k], dhn_recv.at[k], 2 * k)
+
+    def half_copy(k):
+        lines = pl.ds((k - 1) * half, half)
+        return remote(
+            sent.at[2, lines], halves.at[k - 1], half_sem.at[0, k], half_sem.at[1, k], 2 * k
+        )
 
     def left_copy(k, j, other):
         number = 1 - core if other else core
@@ -888,9 +894,6 @@
             else:
                 grad[:, lines] = dhn
 
-        if k:
-            dhn_copy(k).start()
-
     for copy in loads[1:]:
         copy.wait()
     forward(0)
@@ -898,12 +901,33 @@
         hn_copy(k).wait_recv()
         if relayed:
             hn_copy(3 - k, 1).start()
-    for k in range(1, chips):
-        if relayed and k == 3:
-            for i in direct:
-                hn_copy(i, 1).wait_recv()
-        forward(k)
-        backward(k)
+    if relayed:
+        forward(1)
+        forward(2)
+        for i in direct:
+            hn_copy(i, 1).wait_recv()
+        forward(3)
+        backward(3)
+        for k in direct:
+            half_copy(k).start()
+        backward(1)
+        backward(2)
+        for k in direct:
+            half_copy(k).wait_recv()
+
+            @pl.loop(0, half // 16)
+            def _(i):
+                lines = pl.ds(pl.multiple_of(i * 16, 16), 16)
+                into = pl.ds(pl.multiple_of((k - 1) * half + i * 16, 16), 16)
+                total = sent[2 - k, into, :].astype(F32) + halves[k - 1, lines, :].astype(F32)
+                sent[2 - k, into, :] = total.astype(BF)
+
+            dhn_copy(3 - k).start()
+    else:
+        for k in range(1, chips):
+            forward(k)
+            backward(k)
+            dhn_copy(k).start()
     backward(0)
 
     @pl.loop(0, width // 256)
@@ -962,13 +986,13 @@
         def _():
             send().wait_recv()
 
-    for k in range(1, chips):
+    for k in direct:
         dhn_copy(k).wait_recv()
 
     @pl.loop(0, rows // 16)
     def _(i):
         lines = pl.ds(pl.multiple_of(i * 16, 16), 16)
-        grad[lines, :] += sum(got[k, lines, :].astype(F32) for k in range(chips - 1))
+        grad[lines, :] += sum(got[k - 1, lines, :].astype(F32) for k in direct)
 
     store_outs.wait()
     for k in range(chips):
@@ -977,11 +1001,11 @@
             left_copy(k, j, 1).wait()
         right_copy(k, 0).wait()
         right_copy(k, 1).wait()
-        if k:
-            dhn_copy(k).wait_send()
     for k in direct:
+        dhn_copy(k).wait_send()
         hn_copy(k).wait_send()
         if relayed:
+            half_copy(k).wait_send()
             hn_copy(k, 1).wait_send()
 
 
@@ -1015,6 +1039,8 @@
             pltpu.VMEM((chips - 1, rows, width), BF),
             pltpu.VMEM((chips, rows, width), BF),
             pltpu.VMEM((2, 128, width), BF),
+            pltpu.VMEM((2, rows // 2, width), BF),
+            dma((2, chips)),
             dma((3,)),
             dma((chips,)),
             dma((2 * chips,)),
@@ -1045,7 +1071,7 @@
 
 
 def chunk_rows(rows):
-    return max(r for r in range(16, 65, 16) if rows % r == 0)
+    return max(r for r in range(16, 33, 16) if rows % r == 0)
 
 
 def finish_kernel(nf, nc, *refs):
@@ -1182,7 +1208,7 @@
 
         @pl.when(depth == level)
         def _():
-            lag = 1 + 2 * (top - level)
+            lag = 1 + 4 * (top - level)
             for t in range(count + lag):
                 if t < count:
                     inward(t, level)

time: 647 us -> 641 us (level)
  transfers between devices with their start and end apart: 16 -> 16, of which waited for: 3 -> 3; matrix products, arithmetic and copies ran while one was open for 13% -> 13% of each run, Pallas kernels for 42% -> 43%
where the time goes in v5:
time: 641 us; the launch traced here: 634 us
  Pallas kernels  470 us (73%)
  matrix products  51.1 us (8%)
  waiting for transfers between devices  33.9 us (5%)
  other arithmetic  29 us (5%)
  local copies, waits for them, and re-layouts  23.7 us (4%)
  between operations  15.1 us (2%)
  starting transfers between devices  11.9 us (2%)
    pallas_call x1, Pallas kernels, finish(): pl.pallas_call(functools.partial(finish_kernel, nf, nc), in_specs=[anywhe...  193 us
    pallas_call x1, Pallas kernels, share_weights(): pl.pallas_call(functools.partial(share_kernel, nf, nc, low, size, raw), i...  113 us
    pallas_call x1, Pallas kernels, feed_forward(): pl.pallas_call(functools.partial(feed_forward_kernel, nf), in_specs=[anyw...  86.1 us
    dot_general x8, matrix products, dot(): lax.dot_general(left, right, ((contract[:1], contract[1:]), ((), ())), pr...  51.1 us
    pallas_call x1, Pallas kernels, own_key_grads(): pl.pallas_call(functools.partial(own_key_grads_kernel, nc), in_specs=[pl....  28.4 us
    all_gather x1, waiting for transfers between devices, shards(): down_sum = lax.all_gather(down_sum, 'ctx', axis=0, tiled=True)  24.1 us
    pallas_call x1, Pallas kernels, attention_backward(): pl.pallas_call(attention_backward_kernel, grid_spec=pltpu.PrefetchScalarG...  22.6 us
    pallas_call x1, Pallas kernels, attention_forward(): pl.pallas_call(attention_forward_kernel, grid_spec=pltpu.PrefetchScalarGr...  19.2 us
  transfers between devices with their start and end apart: 16, of which 3 were waited for; matrix products, arithmetic and copies ran while one was open for 13% of the time, Pallas kernels for 43%

profile of v5, /device:TPU:0, one launch (start us, length us, event | category | flops | bytes accessed | tf_op | source)
XLA Modules:
  0.0 634.5 jit_solution(8338711867942719124)
XLA Ops:
  8.2 0.8 copy.47.refs_10_.sin_ref
  8.9 0.8 copy.46.refs_9_.cos_ref
  11.6 112.7 %share_weights.1 = (bf16[8,256,2048]{2,1,0:T(8,128)(2,1)}, bf16[8,256,512]{2,1,0:T(8,128)(2,1)}, bf16[8,256,2048]{2,1,0:T(8,128)(2,1)}, bf16[8,256,2816]{2,1,0:T...) custom-call(bf16[256,2048]{1,0:T(8,128)(2,1)} %refs_0_.1, ...), custom_call_target="tpu_custom_call" | custom-call | tf_op jit(solution)/shard_map/share_weights/pallas_call | solution.py:697
  124.9 1.5 collective-permute-start.1
  126.4 1.4 collective-permute-start.2
  128.1 0.8 convert_bitcast_fusion
  129.4 5.9 fusion.20.q_ref
  135.4 19.2 %attention_forward.1 = (bf16[256,2048]{1,0:T(8,128)(2,1)S(1)}, f32[256,2048]{1,0:T(8,128)S(1)}, bf16[256,2048]{1,0:T(8,128)(2,1)S(1)}, f32[4,2,1024]{2,1,0:T(2,128)S(1)}) custom-call(s32[10]{0:T(128)S(1)} %pad_add_fusion.table, f32[256,2048]{1,0:T(8,128)S(1)} %fusion.20.q_ref, f32[256,128]{1,0:T(8,128)S(1)} %copy-done.1, f32[256,128]{1,0:T(8,128)S(1)} %copy-done, ...), custom_call_target="tpu_custom_call" | custom-call | flops 4294967296 | bytes 8388608 | tf_op jit(solution)/shard_map/attention_forward/pallas_call | solution.py:154
  154.6 1.3 copy-done.9
  155.9 1.0 copy-done.11
  156.8 1.0 copy-done.3
  157.8 3.7 multiply_reduce_fusion.2
  162.1 2.8 multiply_convert_fusion.refs_0_
  164.9 6.2 collective-permute-done.1.refs_3_
  171.1 86.1 %feed_forward.1 = (f32[256,2048]{1,0:T(8,128)}, bf16[2,4,256,1024]{3,2,1,0:T(8,128)(2,1)}, bf16[2,4,256,2816]{3,2,1,0:T(8,128)(2,1)}, bf16[2,704,2048]{2,1,0:T(8,128)(2,1)}, bf16[4,256,2048]{2,1,0:T(8,128)(2,1)}) custom-call(bf16[256,2048]{1,0:T(8,128)(2,1)} %multiply_convert_fusion.refs_0_, bf16[256,2048]{1,0:T(8,128)(2,1)} %bitcast.85, ...), custom_call_target="tpu_custom_call" | custom-call | flops 35433480192 | bytes 40000000 | tf_op jit(solution)/shard_map/feed_forward/pallas_call | solution.py:1019
  257.2 5.7 fusion.4
  263.0 17.5 %convolution_convert_fusion.1 = bf16[1024,2816]{1,0:T(8,128)(2,1)S(1)} fusion(bf16[2048,1024]{1,0:T(8,128)(2,1)} %bitcast.113, bf16[2048,2816]{1,0:T(8,128)(2,1)} %bitcast.110), kind=kOutput, calls=%fused_computation.2 | convolution fusion | flops 11814043648 | bytes 21495808 | tf_op jit(solution)/shard_map/dot_general | solution.py:27
  280.5 2.3 dynamic-slice_bitcast_fusion
  282.8 0.8 collective-permute-start.3
  283.7 1.4 collective-permute-start.4
  285.0 1.3 collective-permute-start.5
  287.7 6.2 convolution_convert_fusion.3.do_ref
  294.0 22.6 %attention_backward.1 = (bf16[256,2048]{1,0:T(8,128)(2,1)S(1)}, bf16[2,1024,256]{2,1,0:T(8,128)(2,1)S(1)}) custom-call(s32[10]{0:T(128)S(1)} %pad_add_fusion.table, bf16[256,2048]{1,0:T(8,128)(2,1)S(1)} %copy-done.12, bf16[256,2048]{1,0:T(8,128)(2,1)S(1)} %convolution_convert_fusion.3.do_ref, f32[256,2048]{1,0:T(8,128)S(1)} %copy-done.10, ...), custom_call_target="tpu_custom_call" | custom-call | flops 10737418240 | bytes 8388608 | tf_op jit(solution)/shard_map/attention_backward/pallas_call | solution.py:280
  316.6 1.0 copy-done.2
  317.6 1.0 copy-done.5
  318.6 28.4 %own_key_grads.1 = bf16[256,512]{1,0:T(8,128)(2,1)} custom-call(bf16[2,1024,256]{2,1,0:T(8,128)(2,1)} %copy-done.2, f32[256,128]{1,0:T(8,128)} %copy.46.refs_9_.cos_ref, f32[256,128]{1,0:T(8,128)} %copy.47.refs_10_.sin_ref), custom_call_target="tpu_custom_call" | custom-call | tf_op jit(solution)/shard_map/own_key_grads/pallas_call | solution.py:360
  347.0 4.5 slice_bitcast_fusion
  351.5 1.0 constant_dynamic-update-slice_fusion.1
  353.2 6.0 fusion.45
  359.3 2.8 fusion.10
  362.0 1.3 stack.21
  363.3 0.7 constant_dynamic-update-slice_fusion.3
  364.0 0.7 constant_dynamic-update-slice_fusion.2
  365.6 5.7 fusion.14
  373.1 3.5 collective-permute-done.6
  376.7 4.4 convolution_convert_fusion.2
  381.1 4.7 convolution_convert_fusion
  385.7 24.1 %all-gather.2.cloned.1.call-done = bf16[704,2048]{1,0:T(8,128)(2,1)} async-done(((bf16[176,2048]{1,0:T(8,128)(2,1)}), bf16[704,2048]{1,0:T(8,128)(2,1)}) %all-gather.2.cloned.1.call-update) | async-done | bytes 2883600 | tf_op jit(solution)/shard_map/all_gather | solution.py:1440
  409.9 1.5 collective-permute-start.11
  411.3 1.5 collective-permute-start.12
  413.3 192.6 %finish.1 = (bf16[4,256,2816]{2,1,0:T(8,128)(2,1)}, bf16[256,2048]{1,0:T(8,128)(2,1)S(1)}, bf16[256,2560]{1,0:T(8,128)(2,1)S(1)}, bf16[16,512]{1,0:T(8,128)(2,1)S(1)}) custom-call(bf16[256,2816]{1,0:T(8,128)(2,1)S(1)} %get-tuple-element.117.refs_0_, bf16[256,2816]{1,0:T(8,128)(2,1)} %collective-permute-done.3.refs_1_, ...), custom_call_target="tpu_custom_call" | custom-call | flops 199999995904 | bytes 60000000 | tf_op jit(solution)/shard_map/finish/pallas_call | solution.py:1239
  605.9 1.6 convert_element_type.137
  607.5 1.6 slice.133
  609.0 1.0 copy-done.21
  610.0 3.3 convert_element_type.138
  613.4 8.1 %place_columns.1 = (f32[256,5632]{1,0:T(8,128)}, f32[256,5632]{1,0:T(8,128)}) custom-call(s32[4]{0:T(128)} %iota_xor_fusion.order, bf16[4,256,2816]{2,1,0:T(8,128)(2,1)} %get-tuple-element.133.both_ref), custom_call_target="tpu_custom_call" | custom-call | tf_op jit(solution)/shard_map/place_columns/pallas_call | solution.py:752
  622.0 0.8 fusion.40
  622.9 4.3 fusion.22
  (125 shorter events, 10.7 us)
Async XLA Ops:
  7.2 344.3 %reduce-scatter.2.cloned.1.call-start = ((), (), s32[]{:S(2)}) async-start(), calls=%async_computation.1 | async-start | bytes 3604480 | tf_op jit(solution)/shard_map/reduce_scatter | solution.py:1412
  11.6 112.7 %copy-start.19 = (bf16[1,256,2048]{2,1,0:T(8,128)(2,1)S(1)}, bf16[1,256,2048]{2,1,0:T(8,128)(2,1)}, u32[]{:S(2)}) copy-start(bf16[1,256,2048]{2,1,0:T(8,128)(2,1)} %param.25) | copy-start | bytes 3145732
  11.6 116.3 %copy-start.16 = (bf16[1,256,2048]{2,1,0:T(8,128)(2,1)S(1)}, bf16[1,256,2048]{2,1,0:T(8,128)(2,1)}, u32[]{:S(2)}) copy-start(bf16[1,256,2048]{2,1,0:T(8,128)(2,1)} %param.13) | copy-start | bytes 3145732
  11.6 117.4 %copy-start.33 = (s32[4,2]{0,1:T(2,128)S(1)}, s32[4,2]{0,1:T(2,128)}, u32[]{:S(2)}) copy-start(s32[4,2]{0,1:T(2,128)} %param.23) | copy-start | bytes 100
  124.3 40.6 %collective-permute-start = (bf16[256,2048]{1,0:T(8,128)(2,1)S(1)}, bf16[256,2048]{1,0:T(8,128)(2,1)}, u32[]{:S(2)}, u32[]{:S(2)}) collective-permute-start(bf16[256,2048]{1,0:T(8,128)(2,1)S(1)} %bitcast.86), channel_id=1, source_target_pairs={{0,2},{1,3},{2,0},{3,1},{4,6},{5,7},{6,4},{7,5},{8,10},{9,11},{10,... | collective-permute-start | bytes 3145736 | tf_op jit(solution)/shard_map/ppermute | solution.py:1264
  124.9 46.2 %collective-permute-start.1 = (bf16[256,2048]{1,0:T(8,128)(2,1)S(1)}, bf16[256,2048]{1,0:T(8,128)(2,1)}, u32[]{:S(2)}, u32[]{:S(2)}) collective-permute-start(bf16[256,2048]{1,0:T(8,128)(2,1)S(1)} %bitcast.87), channel_id=1, source_target_pairs={{0,4},{1,5},{2,6},{3,7},{4,0},{5,1},{6,2},{7,3},{8,12},{9,13},{10,... | collective-permute-start | bytes 3145736 | tf_op jit(solution)/shard_map/ppermute | solution.py:1264
  126.4 44.7 %collective-permute-start.2 = (bf16[256,2048]{1,0:T(8,128)(2,1)S(1)}, bf16[256,2048]{1,0:T(8,128)(2,1)}, u32[]{:S(2)}, u32[]{:S(2)}) collective-permute-start(bf16[256,2048]{1,0:T(8,128)(2,1)S(1)} %bitcast.88), channel_id=1, source_target_pairs={{0,6},{1,7},{2,4},{3,5},{4,2},{5,3},{6,0},{7,1},{8,14},{9,15},{10,... | collective-permute-start | bytes 3145736 | tf_op jit(solution)/shard_map/ppermute | solution.py:1264
  128.9 6.4 %copy-start.28 = (f32[1,8,256]{2,0,1:T(1,128)}, f32[1,8,256]{2,0,1:T(1,128)S(1)}, u32[]{:S(2)}) copy-start(f32[1,8,256]{2,0,1:T(1,128)S(1)} %get-tuple-element.176) | copy-start | bytes 24580
  129.0 6.4 %copy-start.30 = (f32[256]{0:T(256)}, f32[256]{0:T(256)S(1)}, u32[]{:S(2)}) copy-start(f32[256]{0:T(256)S(1)} %add_rsqrt_fusion.1) | copy-start | bytes 3076
  129.4 5.9 copy-start
  129.4 5.9 copy-start.1
  129.4 5.9 copy-start.7
  135.4 22.4 %copy-start.34 = (bf16[8,256,2048]{2,1,0:T(8,128)(2,1)S(1)}, bf16[8,256,2048]{2,1,0:T(8,128)(2,1)}, u32[]{:S(2)}) copy-start(bf16[8,256,2048]{2,1,0:T(8,128)(2,1)} %get-tuple-element.78) | copy-start | bytes 25165828
  154.5 1.3 copy-start.9
  156.8 1.0 copy-start.3
  262.9 146.9 %all-gather.2.cloned.1.call-start = ((), (), s32[]{:S(2)}) async-start(), calls=%async_computation.2 | async-start | bytes 3604480 | tf_op jit(solution)/shard_map/all_gather | solution.py:1440
  280.5 5.8 copy-start.13
  280.5 5.8 copy-start.15
  282.8 4.2 copy-start.20
  282.8 68.6 %collective-permute-start.3 = (bf16[256,2816]{1,0:T(8,128)(2,1)}, bf16[256,2816]{1,0:T(8,128)(2,1)}, u32[]{:S(2)}, u32[]{:S(2)}) collective-permute-start(bf16[256,2816]{1,0:T(8,128)(2,1)} %get-tuple-element.100), channel_id=1, source_target_pairs={{0,2},{1,3},{2,0},{3,1},{4,6},{5,7},{6,4},{7,5},{8,10},{9,11},{10,... | collective-permute-start | bytes 4325384 | tf_op jit(solution)/shard_map/ppermute | solution.py:1264
  283.7 67.8 %collective-permute-start.4 = (bf16[256,2816]{1,0:T(8,128)(2,1)}, bf16[256,2816]{1,0:T(8,128)(2,1)}, u32[]{:S(2)}, u32[]{:S(2)}) collective-permute-start(bf16[256,2816]{1,0:T(8,128)(2,1)} %get-tuple-element.101), channel_id=1, source_target_pairs={{0,4},{1,5},{2,6},{3,7},{4,0},{5,1},{6,2},{7,3},{8,12},{9,13},{10,... | collective-permute-start | bytes 4325384 | tf_op jit(solution)/shard_map/ppermute | solution.py:1264
  285.0 66.4 %collective-permute-start.5 = (bf16[256,2816]{1,0:T(8,128)(2,1)}, bf16[256,2816]{1,0:T(8,128)(2,1)}, u32[]{:S(2)}, u32[]{:S(2)}) collective-permute-start(bf16[256,2816]{1,0:T(8,128)(2,1)} %get-tuple-element.102), channel_id=1, source_target_pairs={{0,6},{1,7},{2,4},{3,5},{4,2},{5,3},{6,0},{7,1},{8,14},{9,15},{10,... | collective-permute-start | bytes 4325384 | tf_op jit(solution)/shard_map/ppermute | solution.py:1264
  287.7 6.3 copy-start.25
  287.7 6.3 copy-start.8
  287.7 6.3 copy-start.10
  287.7 6.3 copy-start.12
  316.6 1.0 copy-start.2
  347.0 4.6 copy-start.6
  353.2 6.0 copy-start.17
  353.2 6.1 copy-start.22
  353.2 6.1 copy-start.24
  353.2 6.1 copy-start.29
  353.2 6.1 copy-start.31
  359.3 6.3 copy-start.14
  364.8 8.3 %collective-permute-start.10 = (f32[2,4,256]{2,1,0:T(4,128)S(1)}, f32[2,4,256]{2,1,0:T(4,128)S(1)}, u32[]{:S(2)}, u32[]{:S(2)}) collective-permute-start(f32[2,4,256]{2,1,0:T(4,128)S(1)} %bitcast.100), channel_id=1, source_target_pairs={{0,1},{1,0},{2,3},{3,2},{4,5},{5,4},{6,7},{7,6},{8,9},{9,8},{10,11... | collective-permute-start | bytes 24584 | tf_op jit(solution)/shard_map/ppermute | solution.py:1264
  365.5 5.7 copy-start.26
  365.5 6.2 copy-start.23
  365.5 6.2 copy-start.27
  365.6 6.3 copy-start.4
  371.2 5.4 collective-permute-start.7
  371.8 9.3 %collective-permute-start.9 = (bf16[256,2560]{1,0:T(8,128)(2,1)S(1)}, bf16[256,2560]{1,0:T(8,128)(2,1)S(1)}, u32[]{:S(2)}, u32[]{:S(2)}) collective-permute-start(bf16[256,2560]{1,0:T(8,128)(2,1)S(1)} %constant_dynamic-update-slice_fusion), channel_id=1, source_target_pairs={{0,1},{1,0},{2,3},{3,2},{4,5},{5,4},{6,7},{7,6},{8,9},{9,8},{10,11... | collective-permute-start | bytes 3932168 | tf_op jit(solution)/shard_map/ppermute | solution.py:1264
  372.2 4.5 collective-permute-start.6
  373.0 8.1 %collective-permute-start.8 = (bf16[256,1024]{1,0:T(8,128)(2,1)S(1)}, bf16[256,1024]{1,0:T(8,128)(2,1)S(1)}, u32[]{:S(2)}, u32[]{:S(2)}) collective-permute-start(bf16[256,1024]{1,0:T(8,128)(2,1)S(1)} %get-tuple-element.154), channel_id=1, source_target_pairs={{0,1},{1,0},{2,3},{3,2},{4,5},{5,4},{6,7},{7,6},{8,9},{9,8},{10,11... | collective-permute-start | bytes 1572872 | tf_op jit(solution)/shard_map/ppermute | solution.py:1264
  409.9 213.0 %collective-permute-start.11 = (bf16[256,2048]{1,0:T(8,128)(2,1)}, bf16[256,2048]{1,0:T(8,128)(2,1)}, u32[]{:S(2)}, u32[]{:S(2)}) collective-permute-start(bf16[256,2048]{1,0:T(8,128)(2,1)} %get-tuple-element.127), channel_id=1, source_target_pairs={{0,2},{1,3},{2,0},{3,1},{4,6},{5,7},{6,4},{7,5},{8,10},{9,11},{10,... | collective-permute-start | bytes 3145736 | tf_op jit(solution)/shard_map/ppermute | solution.py:1264
  411.3 211.5 %collective-permute-start.12 = (bf16[256,2048]{1,0:T(8,128)(2,1)}, bf16[256,2048]{1,0:T(8,128)(2,1)}, u32[]{:S(2)}, u32[]{:S(2)}) collective-permute-start(bf16[256,2048]{1,0:T(8,128)(2,1)} %get-tuple-element.128), channel_id=1, source_target_pairs={{0,4},{1,5},{2,6},{3,7},{4,0},{5,1},{6,2},{7,3},{8,12},{9,13},{10,... | collective-permute-start | bytes 3145736 | tf_op jit(solution)/shard_map/ppermute | solution.py:1264
  412.8 210.1 %collective-permute-start.13 = (bf16[256,2048]{1,0:T(8,128)(2,1)}, bf16[256,2048]{1,0:T(8,128)(2,1)}, u32[]{:S(2)}, u32[]{:S(2)}) collective-permute-start(bf16[256,2048]{1,0:T(8,128)(2,1)} %get-tuple-element.129), channel_id=1, source_target_pairs={{0,6},{1,7},{2,4},{3,5},{4,2},{5,3},{6,0},{7,1},{8,14},{9,15},{10,... | collective-permute-start | bytes 3145736 | tf_op jit(solution)/shard_map/ppermute | solution.py:1264
  607.5 2.6 copy-start.21
  613.4 9.5 %copy-start.18 = (bf16[256,2048]{1,0:T(8,128)(2,1)S(1)}, bf16[256,2048]{1,0:T(8,128)(2,1)}, u32[]{:S(2)}) copy-start(bf16[256,2048]{1,0:T(8,128)(2,1)} %get-tuple-element.126) | copy-start | bytes 3145732
  (3 other events, 2.6 us)
Sparse Core Ops, SparseCore 0:
  263.1 55.9 reduce-scatter.1
  351.6 58.1 all-gather.1

commit v6 on v5

--- a/solution.py
+++ b/solution.py
@@ -764,9 +764,10 @@
 
 def feed_forward_kernel(nf, *refs):
     chips = nf // 2
-    hn, *gbs, w_gu, w_d, grad, left, right, downs, outs = refs[: chips + 8]
-    w_gu_v, w_d_v, hn_v, gb_v, dact_v, act_v, dgu_v, sent, got, outs_v = refs[chips + 8 : chips + 18]
-    tiles, halves, half_sem, *sems = refs[chips + 18 :]
+    hn, *gbs, w_gu, w_d, grad, left, right, down_kept, down_got = refs[: chips + 8]
+    outs, refs = refs[chips + 8 : 2 * chips + 8], refs[2 * chips + 8 :]
+    w_gu_v, w_d_v, hn_v, gb_v, dact_v, act_v, dgu_v, sent, got, outs_v = refs[:10]
+    tiles, halves, half_sem, *sems = refs[10:]
     load, load_gb, hn_send, hn_recv, dhn_send, dhn_recv, store = sems[:7]
     left_local, left_send, left_recv, right_local, right_send, right_recv = sems[7:13]
     down_local, down_send, down_recv = sems[13:]
@@ -837,7 +838,9 @@
     gb_loads = [
         pltpu.make_async_copy(gb, gb_v.at[k], load_gb.at[k]) for k, gb in enumerate(gbs)
     ]
-    store_outs = pltpu.make_async_copy(outs_v, outs, store.at[0])
+    store_outs = [
+        pltpu.make_async_copy(outs_v.at[k], out, store.at[k]) for k, out in enumerate(outs)
+    ]
     for k in direct:
         hn_copy(k).start()
     for copy in loads[:1] + gb_loads + loads[1:]:
@@ -936,7 +939,8 @@
         for k in range(chips):
             outs_v[k, :, columns] = dot(act_v[k], w_d_v[:, columns], (1, 0)).astype(BF)
 
-    store_outs.start()
+    for copy in store_outs:
+        copy.start()
 
     lower = part // 2
     spans = []
@@ -951,10 +955,10 @@
         at = pl.ds(a - number * lower, b - a)
 
         def keep():
-            return pltpu.make_async_copy(source, downs.at[0, at], down_local.at[n])
+            return pltpu.make_async_copy(source, down_kept.at[at], down_local.at[n])
 
         def send():
-            return remote(source, downs.at[1, at], down_send.at[n], down_recv.at[n], 1)
+            return remote(source, down_got.at[at], down_send.at[n], down_recv.at[n], 1)
 
         return number, keep, send
 
@@ -994,7 +998,8 @@
         lines = pl.ds(pl.multiple_of(i * 16, 16), 16)
         grad[lines, :] += sum(got[k - 1, lines, :].astype(F32) for k in direct)
 
-    store_outs.wait()
+    for copy in store_outs:
+        copy.wait()
     for k in range(chips):
         for j in range(chips):
             left_copy(k, j, 0).wait()
@@ -1019,14 +1024,15 @@
     return pl.pallas_call(
         functools.partial(feed_forward_kernel, nf),
         in_specs=[anywhere] * (chips + 3),
-        out_specs=[pl.BlockSpec(memory_space=pltpu.VMEM)] + [anywhere] * 4,
+        out_specs=[pl.BlockSpec(memory_space=pltpu.VMEM)] + [anywhere] * (chips + 4),
         out_shape=[
             shape((rows, width), F32),
             shape((2, chips, rows, width // 2), BF),
             shape((2, chips, rows, 2 * part), BF),
-            shape((2, part // 2, width), BF),
-            shape((chips, rows, width), BF),
-        ],
+            shape((part // 2, width), BF),
+            shape((part // 2, width), BF),
+        ]
+        + [shape((rows, width), BF)] * chips,
         scratch_shapes=[
             pltpu.VMEM((width, 2 * part), BF),
             pltpu.VMEM((part, width), BF),
@@ -1047,7 +1053,7 @@
             dma((2 * chips,)),
             dma((chips,)),
             dma((chips,)),
-            dma((1,)),
+            dma((chips,)),
             dma((chips, chips)),
             dma((chips, chips)),
             dma((chips, chips)),
@@ -1373,7 +1379,8 @@
 
         fused = part % 128 == 0
         if fused:
-            grad_hn, left, right, downs, outs = feed_forward(nf, hn, gb_of, w_gu, w_d)
+            grad_hn, left, right, *downs = feed_forward(nf, hn, gb_of, w_gu, w_d)
+            outs = downs[2:]
             left = left.reshape(2 * chips * rows, width // 2)
             right = right.reshape(2 * chips * rows, 2 * part)
             down_sum = (downs[0].astype(F32) + downs[1].astype(F32)).astype(BF)
@@ -1429,9 +1436,7 @@
         dob = dot(dab, w_o, (1, 1)).astype(BF)
         dq, dkv = attention_backward(table, qr, dob, o, lse, kv, cos_lanes, sin_lanes)
         xn, ob, dab, _ = lax.optimization_barrier((xn, ob, dab, dq))
-        if fused:
-            outs = [outs[k] for k in range(chips)]
-        else:
+        if not fused:
             act_of, _ = lax.optimization_barrier((act_of, dq))
             outs = [dot(act, w_d, (1, 0)).astype(BF) for act in act_of]
         sent = outs[1:]

time: 641 us -> 639 us (level)
  waiting for transfers between devices: 33.9 us -> 41.2 us
    ppermute x14, waiting for transfers between devices: 9.74 us -> 16.4 us  [swap(): return lax.ppermute(x, 'fsdp', [(i, i ^ k) for i in range(nf)])]
  transfers between devices with their start and end apart: 16 -> 16, of which waited for: 3 -> 4; matrix products, arithmetic and copies ran while one was open for 13% -> 12% of each run, Pallas kernels for 43% -> 43%
where the time goes in v6:
time: 639 us; the launch traced here: 633 us
  Pallas kernels  470 us (74%)
  matrix products  49.8 us (8%)
  waiting for transfers between devices  41.2 us (6%)
  other arithmetic  27.5 us (4%)
  local copies, waits for them, and re-layouts  17.3 us (3%)
  between operations  15.2 us (2%)
  starting transfers between devices  11.9 us (2%)
    pallas_call x1, Pallas kernels, finish(): pl.pallas_call(functools.partial(finish_kernel, nf, nc), in_specs=[anywhe...  193 us
    pallas_call x1, Pallas kernels, share_weights(): pl.pallas_call(functools.partial(share_kernel, nf, nc, low, size, raw), i...  113 us
    pallas_call x1, Pallas kernels, feed_forward(): pl.pallas_call(functools.partial(feed_forward_kernel, nf), in_specs=[anyw...  86.1 us
    dot_general x8, matrix products, dot(): lax.dot_general(left, right, ((contract[:1], contract[1:]), ((), ())), pr...  49.8 us
    pallas_call x1, Pallas kernels, own_key_grads(): pl.pallas_call(functools.partial(own_key_grads_kernel, nc), in_specs=[pl....  28.5 us
    all_gather x1, waiting for transfers between devices, shards(): down_sum = lax.all_gather(down_sum, 'ctx', axis=0, tiled=True)  24.8 us
    pallas_call x1, Pallas kernels, attention_backward(): pl.pallas_call(attention_backward_kernel, grid_spec=pltpu.PrefetchScalarG...  22.6 us
    pallas_call x1, Pallas kernels, attention_forward(): pl.pallas_call(attention_forward_kernel, grid_spec=pltpu.PrefetchScalarGr...  19.1 us
  transfers between devices with their start and end apart: 16, of which 4 were waited for; matrix products, arithmetic and copies ran while one was open for 12% of the time, Pallas kernels for 43%

profile of v6, /device:TPU:0, one launch (start us, length us, event | category | flops | bytes accessed | tf_op | source)
XLA Modules:
  0.0 632.7 jit_solution(10361303351590097392)
XLA Ops:
  7.2 0.7 convert_element_type.106
  8.2 0.8 copy.47.refs_10_.sin_ref
  8.9 0.8 copy.46.refs_9_.cos_ref
  11.6 112.7 %share_weights.1 = (bf16[8,256,2048]{2,1,0:T(8,128)(2,1)}, bf16[8,256,512]{2,1,0:T(8,128)(2,1)}, bf16[8,256,2048]{2,1,0:T(8,128)(2,1)}, bf16[8,256,2816]{2,1,0:T...) custom-call(bf16[256,2048]{1,0:T(8,128)(2,1)} %refs_0_.1, ...), custom_call_target="tpu_custom_call" | custom-call | tf_op jit(solution)/shard_map/share_weights/pallas_call | solution.py:697
  124.9 1.5 collective-permute-start.1
  126.4 1.4 collective-permute-start.2
  128.1 0.8 convert_bitcast_fusion
  129.4 5.9 fusion.19.q_ref
  135.4 19.1 %attention_forward.1 = (bf16[256,2048]{1,0:T(8,128)(2,1)S(1)}, f32[256,2048]{1,0:T(8,128)S(1)}, bf16[256,2048]{1,0:T(8,128)(2,1)S(1)}, f32[4,2,1024]{2,1,0:T(2,128)S(1)}) custom-call(s32[10]{0:T(128)S(1)} %pad_add_fusion.table, f32[256,2048]{1,0:T(8,128)S(1)} %fusion.19.q_ref, f32[256,128]{1,0:T(8,128)S(1)} %copy-done.1, f32[256,128]{1,0:T(8,128)S(1)} %copy-done, ...), custom_call_target="tpu_custom_call" | custom-call | flops 4294967296 | bytes 8388608 | tf_op jit(solution)/shard_map/attention_forward/pallas_call | solution.py:154
  154.6 2.5 multiply_reduce_fusion.2
  157.1 1.3 copy-done.13
  158.4 1.2 multiply_convert_fusion.refs_0_
  159.6 11.5 %collective-permute-done.1.refs_3_ = bf16[256,2048]{1,0:T(8,128)(2,1)} collective-permute-done((bf16[256,2048]{1,0:T(8,128)(2,1)S(1)}, bf16[256,2048]{1,0:T(8,128)(2,1)}, u32[]{:S(2)}, u32[]{:S(2)}) %collective-permute-start.1) | collective-permute-done | bytes 1048608 | tf_op jit(solution)/shard_map/ppermute | solution.py:1270
  171.1 86.1 %feed_forward.1 = (f32[256,2048]{1,0:T(8,128)}, bf16[2,4,256,1024]{3,2,1,0:T(8,128)(2,1)}, bf16[2,4,256,2816]{3,2,1,0:T(8,128)(2,1)}, bf16[704,2048]{1,0:T(8,128...) custom-call(bf16[256,2048]{1,0:T(8,128)(2,1)} %multiply_convert_fusi, ...), custom_call_target="tpu_custom_call" | custom-call | flops 35433480192 | bytes 40000000 | tf_op jit(solution)/shard_map/feed_forward/pallas_call | solution.py:1024
  257.2 5.7 add_convert_fusion
  263.6 17.5 %convolution_convert_fusion.1 = bf16[1024,2816]{1,0:T(8,128)(2,1)S(1)} fusion(bf16[2048,1024]{1,0:T(8,128)(2,1)} %bitcast.102, bf16[2048,2816]{1,0:T(8,128)(2,1)} %bitcast.100), kind=kOutput, calls=%fused_computation.2 | convolution fusion | flops 11814043648 | bytes 21495808 | tf_op jit(solution)/shard_map/dot_general | solution.py:27
  281.1 2.3 dynamic-slice_bitcast_fusion
  283.5 0.8 collective-permute-start.3
  284.3 1.4 collective-permute-start.4
  285.6 1.3 collective-permute-start.5
  288.3 6.2 convolution_convert_fusion.3.do_ref
  294.6 22.6 %attention_backward.1 = (bf16[256,2048]{1,0:T(8,128)(2,1)S(1)}, bf16[2,1024,256]{2,1,0:T(8,128)(2,1)S(1)}) custom-call(s32[10]{0:T(128)S(1)} %pad_add_fusion.table, bf16[256,2048]{1,0:T(8,128)(2,1)S(1)} %copy-done.12, bf16[256,2048]{1,0:T(8,128)(2,1)S(1)} %convolution_convert_fusion.3.do_ref, f32[256,2048]{1,0:T(8,128)S(1)} %copy-done.10, ...), custom_call_target="tpu_custom_call" | custom-call | flops 10737418240 | bytes 8388608 | tf_op jit(solution)/shard_map/attention_backward/pallas_call | solution.py:280
  317.2 1.0 copy-done.2
  318.2 1.0 copy-done.5
  319.2 28.5 %own_key_grads.1 = bf16[256,512]{1,0:T(8,128)(2,1)} custom-call(bf16[2,1024,256]{2,1,0:T(8,128)(2,1)} %copy-done.2, f32[256,128]{1,0:T(8,128)} %copy.46.refs_9_.cos_ref, f32[256,128]{1,0:T(8,128)} %copy.47.refs_10_.sin_ref), custom_call_target="tpu_custom_call" | custom-call | tf_op jit(solution)/shard_map/own_key_grads/pallas_call | solution.py:360
  347.7 1.4 collective-permute-done.4.refs_2_
  349.1 1.0 constant_dynamic-update-slice_fusion.1
  350.8 6.0 fusion.44
  356.9 2.8 fusion.9
  359.6 1.3 stack.21
  360.9 0.7 constant_dynamic-update-slice_fusion.3
  361.6 0.7 constant_dynamic-update-slice_fusion.2
  362.4 0.7 broadcast_multiply_fusion
  363.1 5.7 fusion.13
  370.7 3.5 collective-permute-done.6
  374.2 4.4 convolution_convert_fusion.2
  378.6 4.7 convolution_convert_fusion
  383.3 24.8 %all-gather.2.cloned.1.call-done = bf16[704,2048]{1,0:T(8,128)(2,1)} async-done(((bf16[176,2048]{1,0:T(8,128)(2,1)}), bf16[704,2048]{1,0:T(8,128)(2,1)}) %all-gather.2.cloned.1.call-update) | async-done | bytes 2883600 | tf_op jit(solution)/shard_map/all_gather | solution.py:1445
  408.1 1.5 collective-permute-start.11
  409.5 1.5 collective-permute-start.12
  411.6 192.6 %finish.1 = (bf16[4,256,2816]{2,1,0:T(8,128)(2,1)}, bf16[256,2048]{1,0:T(8,128)(2,1)S(1)}, bf16[256,2560]{1,0:T(8,128)(2,1)S(1)}, bf16[16,512]{1,0:T(8,128)(2,1)S(1)}) custom-call(bf16[256,2816]{1,0:T(8,128)(2,1)S(1)} %get-tuple-element.125.refs_0_, bf16[256,2816]{1,0:T(8,128)(2,1)} %collective-permute-done.3.refs_1_, ...), custom_call_target="tpu_custom_call" | custom-call | flops 199999995904 | bytes 60000000 | tf_op jit(solution)/shard_map/finish/pallas_call | solution.py:1245
  604.1 1.6 convert_element_type.131
  605.7 1.6 slice.109
  607.3 1.0 copy-done.21
  608.3 3.3 convert_element_type.132
  611.6 8.1 %place_columns.1 = (f32[256,5632]{1,0:T(8,128)}, f32[256,5632]{1,0:T(8,128)}) custom-call(s32[4]{0:T(128)} %iota_xor_fusion.order, bf16[4,256,2816]{2,1,0:T(8,128)(2,1)} %get-tuple-element.141.both_ref), custom_call_target="tpu_custom_call" | custom-call | tf_op jit(solution)/shard_map/place_columns/pallas_call | solution.py:752
  620.2 0.8 fusion.39
  621.1 4.3 fusion.21
  (126 shorter events, 9.4 us)
Async XLA Ops:
  7.2 341.9 %reduce-scatter.2.cloned.1.call-start = ((), (), s32[]{:S(2)}) async-start(), calls=%async_computation.1 | async-start | bytes 3604480 | tf_op jit(solution)/shard_map/reduce_scatter | solution.py:1419
  11.6 112.7 %copy-start.19 = (bf16[1,256,2048]{2,1,0:T(8,128)(2,1)S(1)}, bf16[1,256,2048]{2,1,0:T(8,128)(2,1)}, u32[]{:S(2)}) copy-start(bf16[1,256,2048]{2,1,0:T(8,128)(2,1)} %param.25) | copy-start | bytes 3145732
  11.6 116.3 %copy-start.17 = (bf16[1,256,2048]{2,1,0:T(8,128)(2,1)S(1)}, bf16[1,256,2048]{2,1,0:T(8,128)(2,1)}, u32[]{:S(2)}) copy-start(bf16[1,256,2048]{2,1,0:T(8,128)(2,1)} %param.13) | copy-start | bytes 3145732
  11.6 117.4 %copy-start.34 = (s32[4,2]{0,1:T(2,128)S(1)}, s32[4,2]{0,1:T(2,128)}, u32[]{:S(2)}) copy-start(s32[4,2]{0,1:T(2,128)} %param.23) | copy-start | bytes 100
  124.3 35.3 %collective-permute-start = (bf16[256,2048]{1,0:T(8,128)(2,1)S(1)}, bf16[256,2048]{1,0:T(8,128)(2,1)}, u32[]{:S(2)}, u32[]{:S(2)}) collective-permute-start(bf16[256,2048]{1,0:T(8,128)(2,1)S(1)} %bitcast.76), channel_id=1, source_target_pairs={{0,2},{1,3},{2,0},{3,1},{4,6},{5,7},{6,4},{7,5},{8,10},{9,11},{10,... | collective-permute-start | bytes 3145736 | tf_op jit(solution)/shard_map/ppermute | solution.py:1270
  124.9 46.2 %collective-permute-start.1 = (bf16[256,2048]{1,0:T(8,128)(2,1)S(1)}, bf16[256,2048]{1,0:T(8,128)(2,1)}, u32[]{:S(2)}, u32[]{:S(2)}) collective-permute-start(bf16[256,2048]{1,0:T(8,128)(2,1)S(1)} %bitcast.77), channel_id=1, source_target_pairs={{0,4},{1,5},{2,6},{3,7},{4,0},{5,1},{6,2},{7,3},{8,12},{9,13},{10,... | collective-permute-start | bytes 3145736 | tf_op jit(solution)/shard_map/ppermute | solution.py:1270
  126.4 44.7 %collective-permute-start.2 = (bf16[256,2048]{1,0:T(8,128)(2,1)S(1)}, bf16[256,2048]{1,0:T(8,128)(2,1)}, u32[]{:S(2)}, u32[]{:S(2)}) collective-permute-start(bf16[256,2048]{1,0:T(8,128)(2,1)S(1)} %bitcast.78), channel_id=1, source_target_pairs={{0,6},{1,7},{2,4},{3,5},{4,2},{5,3},{6,0},{7,1},{8,14},{9,15},{10,... | collective-permute-start | bytes 3145736 | tf_op jit(solution)/shard_map/ppermute | solution.py:1270
  128.9 6.4 %copy-start.29 = (f32[1,8,256]{2,0,1:T(1,128)}, f32[1,8,256]{2,0,1:T(1,128)S(1)}, u32[]{:S(2)}) copy-start(f32[1,8,256]{2,0,1:T(1,128)S(1)} %get-tuple-element.180) | copy-start | bytes 24580
  129.0 6.4 %copy-start.31 = (f32[256]{0:T(256)}, f32[256]{0:T(256)S(1)}, u32[]{:S(2)}) copy-start(f32[256]{0:T(256)S(1)} %add_rsqrt_fusion.1) | copy-start | bytes 3076
  129.4 5.9 copy-start
  129.4 5.9 copy-start.1
  129.4 5.9 copy-start.7
  135.4 19.2 %copy-start.35 = (bf16[8,256,2048]{2,1,0:T(8,128)(2,1)S(1)}, bf16[8,256,2048]{2,1,0:T(8,128)(2,1)}, u32[]{:S(2)}) copy-start(bf16[8,256,2048]{2,1,0:T(8,128)(2,1)} %get-tuple-element.82) | copy-start | bytes 25165828
  154.5 2.5 copy-start.3
  154.5 2.5 copy-start.9
  154.6 2.5 copy-start.11
  262.9 145.1 %all-gather.2.cloned.1.call-start = ((), (), s32[]{:S(2)}) async-start(), calls=%async_computation.2 | async-start | bytes 3604480 | tf_op jit(solution)/shard_map/all_gather | solution.py:1445
  281.1 5.8 copy-start.14
  281.1 5.8 copy-start.16
  283.5 4.2 copy-start.20
  283.5 64.3 %collective-permute-start.3 = (bf16[256,2816]{1,0:T(8,128)(2,1)}, bf16[256,2816]{1,0:T(8,128)(2,1)}, u32[]{:S(2)}, u32[]{:S(2)}) collective-permute-start(bf16[256,2816]{1,0:T(8,128)(2,1)} %get-tuple-element.105), channel_id=1, source_target_pairs={{0,2},{1,3},{2,0},{3,1},{4,6},{5,7},{6,4},{7,5},{8,10},{9,11},{10,... | collective-permute-start | bytes 4325384 | tf_op jit(solution)/shard_map/ppermute | solution.py:1270
  284.3 64.8 %collective-permute-start.4 = (bf16[256,2816]{1,0:T(8,128)(2,1)}, bf16[256,2816]{1,0:T(8,128)(2,1)}, u32[]{:S(2)}, u32[]{:S(2)}) collective-permute-start(bf16[256,2816]{1,0:T(8,128)(2,1)} %get-tuple-element.106), channel_id=1, source_target_pairs={{0,4},{1,5},{2,6},{3,7},{4,0},{5,1},{6,2},{7,3},{8,12},{9,13},{10,... | collective-permute-start | bytes 4325384 | tf_op jit(solution)/shard_map/ppermute | solution.py:1270
  285.6 63.4 %collective-permute-start.5 = (bf16[256,2816]{1,0:T(8,128)(2,1)}, bf16[256,2816]{1,0:T(8,128)(2,1)}, u32[]{:S(2)}, u32[]{:S(2)}) collective-permute-start(bf16[256,2816]{1,0:T(8,128)(2,1)} %get-tuple-element.107), channel_id=1, source_target_pairs={{0,6},{1,7},{2,4},{3,5},{4,2},{5,3},{6,0},{7,1},{8,14},{9,15},{10,... | collective-permute-start | bytes 4325384 | tf_op jit(solution)/shard_map/ppermute | solution.py:1270
  288.3 6.2 copy-start.26
  288.3 6.2 copy-start.8
  288.3 6.2 copy-start.10
  288.3 6.2 copy-start.12
  319.2 29.9 %copy-start.6 = (bf16[256,2048]{1,0:T(8,128)(2,1)S(1)}, bf16[256,2048]{1,0:T(8,128)(2,1)}, u32[]{:S(2)}) copy-start(bf16[256,2048]{1,0:T(8,128)(2,1)} %copy-done.5) | copy-start | bytes 3145732
  350.8 6.0 copy-start.18
  350.8 6.1 copy-start.22
  350.8 6.1 copy-start.24
  350.8 6.1 copy-start.30
  350.8 6.1 copy-start.32
  356.9 6.3 copy-start.15
  362.4 8.3 %collective-permute-start.10 = (f32[2,4,256]{2,1,0:T(4,128)S(1)}, f32[2,4,256]{2,1,0:T(4,128)S(1)}, u32[]{:S(2)}, u32[]{:S(2)}) collective-permute-start(f32[2,4,256]{2,1,0:T(4,128)S(1)} %bitcast.90), channel_id=1, source_target_pairs={{0,1},{1,0},{2,3},{3,2},{4,5},{5,4},{6,7},{7,6},{8,9},{9,8},{10,11... | collective-permute-start | bytes 24584 | tf_op jit(solution)/shard_map/ppermute | solution.py:1270
  363.1 5.7 copy-start.27
  363.1 6.2 copy-start.23
  363.1 6.2 copy-start.28
  363.1 6.3 copy-start.4
  368.8 5.4 collective-permute-start.7
  369.3 9.3 %collective-permute-start.9 = (bf16[256,2560]{1,0:T(8,128)(2,1)S(1)}, bf16[256,2560]{1,0:T(8,128)(2,1)S(1)}, u32[]{:S(2)}, u32[]{:S(2)}) collective-permute-start(bf16[256,2560]{1,0:T(8,128)(2,1)S(1)} %constant_dynamic-update-slice_fusion), channel_id=1, source_target_pairs={{0,1},{1,0},{2,3},{3,2},{4,5},{5,4},{6,7},{7,6},{8,9},{9,8},{10,11... | collective-permute-start | bytes 3932168 | tf_op jit(solution)/shard_map/ppermute | solution.py:1270
  369.7 4.5 collective-permute-start.6
  370.6 8.1 %collective-permute-start.8 = (bf16[256,1024]{1,0:T(8,128)(2,1)S(1)}, bf16[256,1024]{1,0:T(8,128)(2,1)S(1)}, u32[]{:S(2)}, u32[]{:S(2)}) collective-permute-start(bf16[256,1024]{1,0:T(8,128)(2,1)S(1)} %get-tuple-element.158), channel_id=1, source_target_pairs={{0,1},{1,0},{2,3},{3,2},{4,5},{5,4},{6,7},{7,6},{8,9},{9,8},{10,11... | collective-permute-start | bytes 1572872 | tf_op jit(solution)/shard_map/ppermute | solution.py:1270
  408.1 213.0 %collective-permute-start.11 = (bf16[256,2048]{1,0:T(8,128)(2,1)}, bf16[256,2048]{1,0:T(8,128)(2,1)}, u32[]{:S(2)}, u32[]{:S(2)}) collective-permute-start(bf16[256,2048]{1,0:T(8,128)(2,1)} %get-tuple-element.135), channel_id=1, source_target_pairs={{0,2},{1,3},{2,0},{3,1},{4,6},{5,7},{6,4},{7,5},{8,10},{9,11},{10,... | collective-permute-start | bytes 3145736 | tf_op jit(solution)/shard_map/ppermute | solution.py:1270
  409.5 211.5 %collective-permute-start.12 = (bf16[256,2048]{1,0:T(8,128)(2,1)}, bf16[256,2048]{1,0:T(8,128)(2,1)}, u32[]{:S(2)}, u32[]{:S(2)}) collective-permute-start(bf16[256,2048]{1,0:T(8,128)(2,1)} %get-tuple-element.136), channel_id=1, source_target_pairs={{0,4},{1,5},{2,6},{3,7},{4,0},{5,1},{6,2},{7,3},{8,12},{9,13},{10,... | collective-permute-start | bytes 3145736 | tf_op jit(solution)/shard_map/ppermute | solution.py:1270
  411.0 210.1 %collective-permute-start.13 = (bf16[256,2048]{1,0:T(8,128)(2,1)}, bf16[256,2048]{1,0:T(8,128)(2,1)}, u32[]{:S(2)}, u32[]{:S(2)}) collective-permute-start(bf16[256,2048]{1,0:T(8,128)(2,1)} %get-tuple-element.137), channel_id=1, source_target_pairs={{0,6},{1,7},{2,4},{3,5},{4,2},{5,3},{6,0},{7,1},{8,14},{9,15},{10,... | collective-permute-start | bytes 3145736 | tf_op jit(solution)/shard_map/ppermute | solution.py:1270
  605.7 2.6 copy-start.21
  611.6 9.5 %copy-start.25 = (bf16[256,2048]{1,0:T(8,128)(2,1)S(1)}, bf16[256,2048]{1,0:T(8,128)(2,1)}, u32[]{:S(2)}) copy-start(bf16[256,2048]{1,0:T(8,128)(2,1)} %get-tuple-element.134) | copy-start | bytes 3145732
  (4 other events, 3.9 us)
Sparse Core Ops, SparseCore 0:
  263.1 55.9 reduce-scatter.1
  349.2 58.8 all-gather.1

commit v7 on v6

--- a/solution.py
+++ b/solution.py
@@ -1459,8 +1459,12 @@
         mine = lax.dynamic_index_in_dim(gains_of, core, 2, keepdims=False)
         gains_of = (mine + swap(other, 1)).transpose(1, 0, 2).reshape(chips, 1, 2 * shard)
         gains_of = jnp.pad(gains_of.astype(BF), ((0, 0), (0, 15), (0, 0)))
-        wide, down_sum, out_term, qkv_term, outs[0], sent = lax.optimization_barrier(
-            (wide, down_sum, out_term, qkv_term, outs[0], sent)
+        out_term, qkv_term, outs[0], sent = lax.optimization_barrier(
+            (out_term, qkv_term, outs[0], sent)
+        )
+        terms = [swap(sent[k - 1], 2 * k) for k in range(1, chips)]
+        wide, down_sum, out_term, qkv_term = lax.optimization_barrier(
+            (wide, down_sum, out_term, qkv_term)
         )
         gu_sum, out_sum, qkv_sum, gain_sum = finish(
             nf, nc, wide, [out_term, qkv_term, gains_of]
@@ -1468,7 +1472,7 @@
         h1, gain_sum = lax.optimization_barrier((h1, gain_sum))
         branch = h1 + outs[0].astype(F32)
         for k in range(1, chips):
-            branch = branch + swap(sent[k - 1], 2 * k).astype(F32)
+            branch = branch + terms[k - 1].astype(F32)
         layer_out = branch.astype(BF)
         qkv_sum = qkv_sum.astype(F32)
         gain_sum = gain_sum[0].reshape(2, shard).astype(F32)

time: 639 us -> 635 us (level)
  no operation moved by 1% of the time
where the time goes in v7:
time: 635 us; the launch traced here: 629 us
  Pallas kernels  469 us (74%)
  matrix products  49.8 us (8%)
  waiting for transfers between devices  37.7 us (6%)
  other arithmetic  27.5 us (4%)
  local copies, waits for them, and re-layouts  17.3 us (3%)
  between operations  15.2 us (2%)
  starting transfers between devices  11.9 us (2%)
    pallas_call x1, Pallas kernels, finish(): pl.pallas_call(functools.partial(finish_kernel, nf, nc), in_specs=[anywhe...  192 us
    pallas_call x1, Pallas kernels, share_weights(): pl.pallas_call(functools.partial(share_kernel, nf, nc, low, size, raw), i...  113 us
    pallas_call x1, Pallas kernels, feed_forward(): pl.pallas_call(functools.partial(feed_forward_kernel, nf), in_specs=[anyw...  86.1 us
    dot_general x8, matrix products, dot(): lax.dot_general(left, right, ((contract[:1], contract[1:]), ((), ())), pr...  49.8 us
    pallas_call x1, Pallas kernels, own_key_grads(): pl.pallas_call(functools.partial(own_key_grads_kernel, nc), in_specs=[pl....  28.5 us
    pallas_call x1, Pallas kernels, attention_backward(): pl.pallas_call(attention_backward_kernel, grid_spec=pltpu.PrefetchScalarG...  22.6 us
    all_gather x1, waiting for transfers between devices, shards(): down_sum = lax.all_gather(down_sum, 'ctx', axis=0, tiled=True)  21.3 us
    pallas_call x1, Pallas kernels, attention_forward(): pl.pallas_call(attention_forward_kernel, grid_spec=pltpu.PrefetchScalarGr...  19.1 us
  transfers between devices with their start and end apart: 16, of which 4 were waited for; matrix products, arithmetic and copies ran while one was open for 12% of the time, Pallas kernels for 43%

profile of v7, /device:TPU:0, one launch (start us, length us, event | category | flops | bytes accessed | tf_op | source)
XLA Modules:
  0.0 628.8 jit_solution(12767875627275455589)
XLA Ops:
  7.2 0.7 convert_element_type.106
  8.2 0.8 copy.47.refs_10_.sin_ref
  8.9 0.8 copy.46.refs_9_.cos_ref
  11.6 112.7 %share_weights.1 = (bf16[8,256,2048]{2,1,0:T(8,128)(2,1)}, bf16[8,256,512]{2,1,0:T(8,128)(2,1)}, bf16[8,256,2048]{2,1,0:T(8,128)(2,1)}, bf16[8,256,2816]{2,1,0:T...) custom-call(bf16[256,2048]{1,0:T(8,128)(2,1)} %refs_0_.1, ...), custom_call_target="tpu_custom_call" | custom-call | tf_op jit(solution)/shard_map/share_weights/pallas_call | solution.py:697
  124.9 1.5 collective-permute-start.1
  126.4 1.4 collective-permute-start.2
  128.1 0.8 convert_bitcast_fusion
  129.4 5.9 fusion.19.q_ref
  135.4 19.1 %attention_forward.1 = (bf16[256,2048]{1,0:T(8,128)(2,1)S(1)}, f32[256,2048]{1,0:T(8,128)S(1)}, bf16[256,2048]{1,0:T(8,128)(2,1)S(1)}, f32[4,2,1024]{2,1,0:T(2,128)S(1)}) custom-call(s32[10]{0:T(128)S(1)} %pad_add_fusion.table, f32[256,2048]{1,0:T(8,128)S(1)} %fusion.19.q_ref, f32[256,128]{1,0:T(8,128)S(1)} %copy-done.1, f32[256,128]{1,0:T(8,128)S(1)} %copy-done, ...), custom_call_target="tpu_custom_call" | custom-call | flops 4294967296 | bytes 8388608 | tf_op jit(solution)/shard_map/attention_forward/pallas_call | solution.py:154
  154.6 2.5 multiply_reduce_fusion.2
  157.1 1.3 copy-done.13
  158.4 1.2 multiply_convert_fusion.refs_0_
  159.6 11.5 %collective-permute-done.1.refs_3_ = bf16[256,2048]{1,0:T(8,128)(2,1)} collective-permute-done((bf16[256,2048]{1,0:T(8,128)(2,1)S(1)}, bf16[256,2048]{1,0:T(8,128)(2,1)}, u32[]{:S(2)}, u32[]{:S(2)}) %collective-permute-start.1) | collective-permute-done | bytes 1048608 | tf_op jit(solution)/shard_map/ppermute | solution.py:1270
  171.1 86.1 %feed_forward.1 = (f32[256,2048]{1,0:T(8,128)}, bf16[2,4,256,1024]{3,2,1,0:T(8,128)(2,1)}, bf16[2,4,256,2816]{3,2,1,0:T(8,128)(2,1)}, bf16[704,2048]{1,0:T(8,128...) custom-call(bf16[256,2048]{1,0:T(8,128)(2,1)} %multiply_convert_fusi, ...), custom_call_target="tpu_custom_call" | custom-call | flops 35433480192 | bytes 40000000 | tf_op jit(solution)/shard_map/feed_forward/pallas_call | solution.py:1024
  257.2 5.7 add_convert_fusion
  263.6 17.5 %convolution_convert_fusion.1 = bf16[1024,2816]{1,0:T(8,128)(2,1)S(1)} fusion(bf16[2048,1024]{1,0:T(8,128)(2,1)} %bitcast.102, bf16[2048,2816]{1,0:T(8,128)(2,1)} %bitcast.100), kind=kOutput, calls=%fused_computation.2 | convolution fusion | flops 11814043648 | bytes 21495808 | tf_op jit(solution)/shard_map/dot_general | solution.py:27
  281.1 2.3 dynamic-slice_bitcast_fusion
  283.5 0.8 collective-permute-start.3
  284.3 1.4 collective-permute-start.4
  285.6 1.3 collective-permute-start.5
  288.3 6.2 convolution_convert_fusion.3.do_ref
  294.6 22.6 %attention_backward.1 = (bf16[256,2048]{1,0:T(8,128)(2,1)S(1)}, bf16[2,1024,256]{2,1,0:T(8,128)(2,1)S(1)}) custom-call(s32[10]{0:T(128)S(1)} %pad_add_fusion.table, bf16[256,2048]{1,0:T(8,128)(2,1)S(1)} %copy-done.12, bf16[256,2048]{1,0:T(8,128)(2,1)S(1)} %convolution_convert_fusion.3.do_ref, f32[256,2048]{1,0:T(8,128)S(1)} %copy-done.10, ...), custom_call_target="tpu_custom_call" | custom-call | flops 10737418240 | bytes 8388608 | tf_op jit(solution)/shard_map/attention_backward/pallas_call | solution.py:280
  317.2 1.0 copy-done.2
  318.2 1.0 copy-done.5
  319.2 28.5 %own_key_grads.1 = bf16[256,512]{1,0:T(8,128)(2,1)} custom-call(bf16[2,1024,256]{2,1,0:T(8,128)(2,1)} %copy-done.2, f32[256,128]{1,0:T(8,128)} %copy.46.refs_9_.cos_ref, f32[256,128]{1,0:T(8,128)} %copy.47.refs_10_.sin_ref), custom_call_target="tpu_custom_call" | custom-call | tf_op jit(solution)/shard_map/own_key_grads/pallas_call | solution.py:360
  347.7 1.4 collective-permute-done.4.refs_2_
  349.1 1.0 constant_dynamic-update-slice_fusion.1
  350.8 6.0 fusion.44
  356.9 2.8 fusion.9
  359.6 1.3 stack.21
  360.9 0.7 constant_dynamic-update-slice_fusion.3
  361.6 0.7 constant_dynamic-update-slice_fusion.2
  363.1 5.7 fusion.13
  370.7 3.5 collective-permute-done.6
  374.2 4.4 convolution_convert_fusion.2
  378.6 4.7 convolution_convert_fusion
  383.3 1.2 collective-permute-start.11
  384.5 0.8 collective-permute-start.12
  385.3 1.5 collective-permute-start.13
  386.8 21.3 %all-gather.2.cloned.1.call-done = bf16[704,2048]{1,0:T(8,128)(2,1)} async-done(((bf16[176,2048]{1,0:T(8,128)(2,1)}), bf16[704,2048]{1,0:T(8,128)(2,1)}) %all-gather.2.cloned.1.call-update) | async-done | bytes 2883600 | tf_op jit(solution)/shard_map/all_gather | solution.py:1445
  408.1 192.1 %finish.1 = (bf16[4,256,2816]{2,1,0:T(8,128)(2,1)}, bf16[256,2048]{1,0:T(8,128)(2,1)S(1)}, bf16[256,2560]{1,0:T(8,128)(2,1)S(1)}, bf16[16,512]{1,0:T(8,128)(2,1)S(1)}) custom-call(bf16[256,2816]{1,0:T(8,128)(2,1)S(1)} %get-tuple-element.129.refs_0_, bf16[256,2816]{1,0:T(8,128)(2,1)} %collective-permute-done.3.refs_1_, ...), custom_call_target="tpu_custom_call" | custom-call | flops 199999995904 | bytes 60000000 | tf_op jit(solution)/shard_map/finish/pallas_call | solution.py:1245
  600.2 1.6 convert_element_type.131
  601.8 1.6 slice.109
  603.3 1.0 copy-done.21
  604.3 3.3 convert_element_type.132
  607.7 8.1 %place_columns.1 = (f32[256,5632]{1,0:T(8,128)}, f32[256,5632]{1,0:T(8,128)}) custom-call(s32[4]{0:T(128)} %iota_xor_fusion.order, bf16[4,256,2816]{2,1,0:T(8,128)(2,1)} %get-tuple-element.145.both_ref), custom_call_target="tpu_custom_call" | custom-call | tf_op jit(solution)/shard_map/place_columns/pallas_call | solution.py:752
  616.3 0.8 fusion.39
  617.2 4.3 fusion.21
  (126 shorter events, 9.5 us)
Async XLA Ops:
  7.2 341.9 %reduce-scatter.2.cloned.1.call-start = ((), (), s32[]{:S(2)}) async-start(), calls=%async_computation.1 | async-start | bytes 3604480 | tf_op jit(solution)/shard_map/reduce_scatter | solution.py:1419
  11.6 112.7 %copy-start.19 = (bf16[1,256,2048]{2,1,0:T(8,128)(2,1)S(1)}, bf16[1,256,2048]{2,1,0:T(8,128)(2,1)}, u32[]{:S(2)}) copy-start(bf16[1,256,2048]{2,1,0:T(8,128)(2,1)} %param.25) | copy-start | bytes 3145732
  11.6 116.3 %copy-start.17 = (bf16[1,256,2048]{2,1,0:T(8,128)(2,1)S(1)}, bf16[1,256,2048]{2,1,0:T(8,128)(2,1)}, u32[]{:S(2)}) copy-start(bf16[1,256,2048]{2,1,0:T(8,128)(2,1)} %param.13) | copy-start | bytes 3145732
  11.6 117.4 %copy-start.34 = (s32[4,2]{0,1:T(2,128)S(1)}, s32[4,2]{0,1:T(2,128)}, u32[]{:S(2)}) copy-start(s32[4,2]{0,1:T(2,128)} %param.23) | copy-start | bytes 100
  124.3 35.3 %collective-permute-start = (bf16[256,2048]{1,0:T(8,128)(2,1)S(1)}, bf16[256,2048]{1,0:T(8,128)(2,1)}, u32[]{:S(2)}, u32[]{:S(2)}) collective-permute-start(bf16[256,2048]{1,0:T(8,128)(2,1)S(1)} %bitcast.76), channel_id=1, source_target_pairs={{0,2},{1,3},{2,0},{3,1},{4,6},{5,7},{6,4},{7,5},{8,10},{9,11},{10,... | collective-permute-start | bytes 3145736 | tf_op jit(solution)/shard_map/ppermute | solution.py:1270
  124.9 46.2 %collective-permute-start.1 = (bf16[256,2048]{1,0:T(8,128)(2,1)S(1)}, bf16[256,2048]{1,0:T(8,128)(2,1)}, u32[]{:S(2)}, u32[]{:S(2)}) collective-permute-start(bf16[256,2048]{1,0:T(8,128)(2,1)S(1)} %bitcast.77), channel_id=1, source_target_pairs={{0,4},{1,5},{2,6},{3,7},{4,0},{5,1},{6,2},{7,3},{8,12},{9,13},{10,... | collective-permute-start | bytes 3145736 | tf_op jit(solution)/shard_map/ppermute | solution.py:1270
  126.4 44.7 %collective-permute-start.2 = (bf16[256,2048]{1,0:T(8,128)(2,1)S(1)}, bf16[256,2048]{1,0:T(8,128)(2,1)}, u32[]{:S(2)}, u32[]{:S(2)}) collective-permute-start(bf16[256,2048]{1,0:T(8,128)(2,1)S(1)} %bitcast.78), channel_id=1, source_target_pairs={{0,6},{1,7},{2,4},{3,5},{4,2},{5,3},{6,0},{7,1},{8,14},{9,15},{10,... | collective-permute-start | bytes 3145736 | tf_op jit(solution)/shard_map/ppermute | solution.py:1270
  128.9 6.4 %copy-start.29 = (f32[1,8,256]{2,0,1:T(1,128)}, f32[1,8,256]{2,0,1:T(1,128)S(1)}, u32[]{:S(2)}) copy-start(f32[1,8,256]{2,0,1:T(1,128)S(1)} %get-tuple-element.184) | copy-start | bytes 24580
  129.0 6.4 %copy-start.31 = (f32[256]{0:T(256)}, f32[256]{0:T(256)S(1)}, u32[]{:S(2)}) copy-start(f32[256]{0:T(256)S(1)} %add_rsqrt_fusion.1) | copy-start | bytes 3076
  129.4 5.9 copy-start
  129.4 5.9 copy-start.1
  129.4 5.9 copy-start.7
  135.4 19.2 %copy-start.35 = (bf16[8,256,2048]{2,1,0:T(8,128)(2,1)S(1)}, bf16[8,256,2048]{2,1,0:T(8,128)(2,1)}, u32[]{:S(2)}) copy-start(bf16[8,256,2048]{2,1,0:T(8,128)(2,1)} %get-tuple-element.84) | copy-start | bytes 25165828
  154.5 2.5 copy-start.3
  154.5 2.5 copy-start.9
  154.6 2.5 copy-start.11
  262.9 145.1 %all-gather.2.cloned.1.call-start = ((), (), s32[]{:S(2)}) async-start(), calls=%async_computation.2 | async-start | bytes 3604480 | tf_op jit(solution)/shard_map/all_gather | solution.py:1445
  281.1 5.8 copy-start.14
  281.1 5.8 copy-start.16
  283.5 4.2 copy-start.20
  283.5 64.3 %collective-permute-start.3 = (bf16[256,2816]{1,0:T(8,128)(2,1)}, bf16[256,2816]{1,0:T(8,128)(2,1)}, u32[]{:S(2)}, u32[]{:S(2)}) collective-permute-start(bf16[256,2816]{1,0:T(8,128)(2,1)} %get-tuple-element.107), channel_id=1, source_target_pairs={{0,2},{1,3},{2,0},{3,1},{4,6},{5,7},{6,4},{7,5},{8,10},{9,11},{10,... | collective-permute-start | bytes 4325384 | tf_op jit(solution)/shard_map/ppermute | solution.py:1270
  284.3 64.8 %collective-permute-start.4 = (bf16[256,2816]{1,0:T(8,128)(2,1)}, bf16[256,2816]{1,0:T(8,128)(2,1)}, u32[]{:S(2)}, u32[]{:S(2)}) collective-permute-start(bf16[256,2816]{1,0:T(8,128)(2,1)} %get-tuple-element.108), channel_id=1, source_target_pairs={{0,4},{1,5},{2,6},{3,7},{4,0},{5,1},{6,2},{7,3},{8,12},{9,13},{10,... | collective-permute-start | bytes 4325384 | tf_op jit(solution)/shard_map/ppermute | solution.py:1270
  285.6 63.4 %collective-permute-start.5 = (bf16[256,2816]{1,0:T(8,128)(2,1)}, bf16[256,2816]{1,0:T(8,128)(2,1)}, u32[]{:S(2)}, u32[]{:S(2)}) collective-permute-start(bf16[256,2816]{1,0:T(8,128)(2,1)} %get-tuple-element.109), channel_id=1, source_target_pairs={{0,6},{1,7},{2,4},{3,5},{4,2},{5,3},{6,0},{7,1},{8,14},{9,15},{10,... | collective-permute-start | bytes 4325384 | tf_op jit(solution)/shard_map/ppermute | solution.py:1270
  288.3 6.2 copy-start.26
  288.3 6.2 copy-start.8
  288.3 6.2 copy-start.10
  288.3 6.2 copy-start.12
  319.2 29.9 %copy-start.6 = (bf16[256,2048]{1,0:T(8,128)(2,1)S(1)}, bf16[256,2048]{1,0:T(8,128)(2,1)}, u32[]{:S(2)}) copy-start(bf16[256,2048]{1,0:T(8,128)(2,1)} %copy-done.5) | copy-start | bytes 3145732
  350.8 6.0 copy-start.18
  350.8 6.1 copy-start.22
  350.8 6.1 copy-start.24
  350.8 6.1 copy-start.30
  350.8 6.1 copy-start.32
  356.9 6.3 copy-start.15
  362.4 8.3 %collective-permute-start.10 = (f32[2,4,256]{2,1,0:T(4,128)S(1)}, f32[2,4,256]{2,1,0:T(4,128)S(1)}, u32[]{:S(2)}, u32[]{:S(2)}) collective-permute-start(f32[2,4,256]{2,1,0:T(4,128)S(1)} %bitcast.90), channel_id=1, source_target_pairs={{0,1},{1,0},{2,3},{3,2},{4,5},{5,4},{6,7},{7,6},{8,9},{9,8},{10,11... | collective-permute-start | bytes 24584 | tf_op jit(solution)/shard_map/ppermute | solution.py:1270
  363.1 5.7 copy-start.27
  363.1 6.2 copy-start.23
  363.1 6.2 copy-start.28
  363.1 6.3 %copy-start.4 = (bf16[256,2048]{1,0:T(8,128)(2,1)S(1)}, bf16[256,2048]{1,0:T(8,128)(2,1)}, u32[]{:S(2)}) copy-start(bf16[256,2048]{1,0:T(8,128)(2,1)} %copy-done.3) | copy-start | bytes 3145732
  368.8 5.4 collective-permute-start.7
  369.3 9.3 %collective-permute-start.9 = (bf16[256,2560]{1,0:T(8,128)(2,1)S(1)}, bf16[256,2560]{1,0:T(8,128)(2,1)S(1)}, u32[]{:S(2)}, u32[]{:S(2)}) collective-permute-start(bf16[256,2560]{1,0:T(8,128)(2,1)S(1)} %constant_dynamic-update-slice_fusion), channel_id=1, source_target_pairs={{0,1},{1,0},{2,3},{3,2},{4,5},{5,4},{6,7},{7,6},{8,9},{9,8},{10,11... | collective-permute-start | bytes 3932168 | tf_op jit(solution)/shard_map/ppermute | solution.py:1270
  369.7 4.5 collective-permute-start.6
  370.6 8.1 %collective-permute-start.8 = (bf16[256,1024]{1,0:T(8,128)(2,1)S(1)}, bf16[256,1024]{1,0:T(8,128)(2,1)S(1)}, u32[]{:S(2)}, u32[]{:S(2)}) collective-permute-start(bf16[256,1024]{1,0:T(8,128)(2,1)S(1)} %get-tuple-element.162), channel_id=1, source_target_pairs={{0,1},{1,0},{2,3},{3,2},{4,5},{5,4},{6,7},{7,6},{8,9},{9,8},{10,11... | collective-permute-start | bytes 1572872 | tf_op jit(solution)/shard_map/ppermute | solution.py:1270
  383.3 233.9 %collective-permute-start.11 = (bf16[256,2048]{1,0:T(8,128)(2,1)}, bf16[256,2048]{1,0:T(8,128)(2,1)}, u32[]{:S(2)}, u32[]{:S(2)}) collective-permute-start(bf16[256,2048]{1,0:T(8,128)(2,1)} %get-tuple-element.139), channel_id=1, source_target_pairs={{0,2},{1,3},{2,0},{3,1},{4,6},{5,7},{6,4},{7,5},{8,10},{9,11},{10,... | collective-permute-start | bytes 3145736 | tf_op jit(solution)/shard_map/ppermute | solution.py:1270
  384.5 232.6 %collective-permute-start.12 = (bf16[256,2048]{1,0:T(8,128)(2,1)}, bf16[256,2048]{1,0:T(8,128)(2,1)}, u32[]{:S(2)}, u32[]{:S(2)}) collective-permute-start(bf16[256,2048]{1,0:T(8,128)(2,1)} %get-tuple-element.140), channel_id=1, source_target_pairs={{0,4},{1,5},{2,6},{3,7},{4,0},{5,1},{6,2},{7,3},{8,12},{9,13},{10,... | collective-permute-start | bytes 3145736 | tf_op jit(solution)/shard_map/ppermute | solution.py:1270
  385.3 231.8 %collective-permute-start.13 = (bf16[256,2048]{1,0:T(8,128)(2,1)}, bf16[256,2048]{1,0:T(8,128)(2,1)}, u32[]{:S(2)}, u32[]{:S(2)}) collective-permute-start(bf16[256,2048]{1,0:T(8,128)(2,1)} %get-tuple-element.141), channel_id=1, source_target_pairs={{0,6},{1,7},{2,4},{3,5},{4,2},{5,3},{6,0},{7,1},{8,14},{9,15},{10,... | collective-permute-start | bytes 3145736 | tf_op jit(solution)/shard_map/ppermute | solution.py:1270
  601.8 2.6 copy-start.21
  607.7 9.5 %copy-start.25 = (bf16[256,2048]{1,0:T(8,128)(2,1)S(1)}, bf16[256,2048]{1,0:T(8,128)(2,1)}, u32[]{:S(2)}) copy-start(bf16[256,2048]{1,0:T(8,128)(2,1)} %get-tuple-element.138) | copy-start | bytes 3145732
  (4 other events, 3.9 us)
Sparse Core Ops, SparseCore 0:
  263.1 55.9 reduce-scatter.1
  349.2 58.8 all-gather.1

commit v8 on v7

--- a/solution.py
+++ b/solution.py
@@ -1077,7 +1077,7 @@
 
 
 def chunk_rows(rows):
-    return max(r for r in range(16, 33, 16) if rows % r == 0)
+    return max(r for r in range(16, 17, 16) if rows % r == 0)
 
 
 def finish_kernel(nf, nc, *refs):
@@ -1214,7 +1214,7 @@
 
         @pl.when(depth == level)
         def _():
-            lag = 1 + 4 * (top - level)
+            lag = 3 + 6 * (top - level)
             for t in range(count + lag):
                 if t < count:
                     inward(t, level)

time: 635 us -> 637 us (level)
  no operation moved by 1% of the time
where the time goes in v8:
time: 637 us; the launch traced here: 630 us
  Pallas kernels  471 us (74%)
  matrix products  49.8 us (8%)
  waiting for transfers between devices  37.7 us (6%)
  other arithmetic  27.5 us (4%)
  local copies, waits for them, and re-layouts  17.3 us (3%)
  between operations  15.2 us (2%)
  starting transfers between devices  11.9 us (2%)
    pallas_call x1, Pallas kernels, finish(): pl.pallas_call(functools.partial(finish_kernel, nf, nc), in_specs=[anywhe...  194 us
    pallas_call x1, Pallas kernels, share_weights(): pl.pallas_call(functools.partial(share_kernel, nf, nc, low, size, raw), i...  113 us
    pallas_call x1, Pallas kernels, feed_forward(): pl.pallas_call(functools.partial(feed_forward_kernel, nf), in_specs=[anyw...  86.1 us
    dot_general x8, matrix products, dot(): lax.dot_general(left, right, ((contract[:1], contract[1:]), ((), ())), pr...  49.8 us
    pallas_call x1, Pallas kernels, own_key_grads(): pl.pallas_call(functools.partial(own_key_grads_kernel, nc), in_specs=[pl....  28.5 us
    pallas_call x1, Pallas kernels, attention_backward(): pl.pallas_call(attention_backward_kernel, grid_spec=pltpu.PrefetchScalarG...  22.6 us
    all_gather x1, waiting for transfers between devices, shards(): down_sum = lax.all_gather(down_sum, 'ctx', axis=0, tiled=True)  21.3 us
    pallas_call x1, Pallas kernels, attention_forward(): pl.pallas_call(attention_forward_kernel, grid_spec=pltpu.PrefetchScalarGr...  19.2 us
  transfers between devices with their start and end apart: 16, of which 4 were waited for; matrix products, arithmetic and copies ran while one was open for 12% of the time, Pallas kernels for 43%

profile of v8, /device:TPU:0, one launch (start us, length us, event | category | flops | bytes accessed | tf_op | source)
XLA Modules:
  0.0 630.3 jit_solution(3415501520241140676)
XLA Ops:
  7.2 0.7 convert_element_type.106
  8.2 0.8 copy.47.refs_10_.sin_ref
  8.9 0.8 copy.46.refs_9_.cos_ref
  11.6 112.7 %share_weights.1 = (bf16[8,256,2048]{2,1,0:T(8,128)(2,1)}, bf16[8,256,512]{2,1,0:T(8,128)(2,1)}, bf16[8,256,2048]{2,1,0:T(8,128)(2,1)}, bf16[8,256,2816]{2,1,0:T...) custom-call(bf16[256,2048]{1,0:T(8,128)(2,1)} %refs_0_.1, ...), custom_call_target="tpu_custom_call" | custom-call | tf_op jit(solution)/shard_map/share_weights/pallas_call | solution.py:697
  124.9 1.5 collective-permute-start.1
  126.4 1.4 collective-permute-start.2
  128.1 0.8 convert_bitcast_fusion
  129.4 5.9 fusion.19.q_ref
  135.4 19.2 %attention_forward.1 = (bf16[256,2048]{1,0:T(8,128)(2,1)S(1)}, f32[256,2048]{1,0:T(8,128)S(1)}, bf16[256,2048]{1,0:T(8,128)(2,1)S(1)}, f32[4,2,1024]{2,1,0:T(2,128)S(1)}) custom-call(s32[10]{0:T(128)S(1)} %pad_add_fusion.table, f32[256,2048]{1,0:T(8,128)S(1)} %fusion.19.q_ref, f32[256,128]{1,0:T(8,128)S(1)} %copy-done.1, f32[256,128]{1,0:T(8,128)S(1)} %copy-done, ...), custom_call_target="tpu_custom_call" | custom-call | flops 4294967296 | bytes 8388608 | tf_op jit(solution)/shard_map/attention_forward/pallas_call | solution.py:154
  154.6 2.5 multiply_reduce_fusion.2
  157.1 1.3 copy-done.13
  158.4 1.2 multiply_convert_fusion.refs_0_
  159.6 11.5 %collective-permute-done.1.refs_3_ = bf16[256,2048]{1,0:T(8,128)(2,1)} collective-permute-done((bf16[256,2048]{1,0:T(8,128)(2,1)S(1)}, bf16[256,2048]{1,0:T(8,128)(2,1)}, u32[]{:S(2)}, u32[]{:S(2)}) %collective-permute-start.1) | collective-permute-done | bytes 1048608 | tf_op jit(solution)/shard_map/ppermute | solution.py:1270
  171.1 86.1 %feed_forward.1 = (f32[256,2048]{1,0:T(8,128)}, bf16[2,4,256,1024]{3,2,1,0:T(8,128)(2,1)}, bf16[2,4,256,2816]{3,2,1,0:T(8,128)(2,1)}, bf16[704,2048]{1,0:T(8,128...) custom-call(bf16[256,2048]{1,0:T(8,128)(2,1)} %multiply_convert_fusi, ...), custom_call_target="tpu_custom_call" | custom-call | flops 35433480192 | bytes 40000000 | tf_op jit(solution)/shard_map/feed_forward/pallas_call | solution.py:1024
  257.2 5.7 add_convert_fusion
  263.6 17.5 %convolution_convert_fusion.1 = bf16[1024,2816]{1,0:T(8,128)(2,1)S(1)} fusion(bf16[2048,1024]{1,0:T(8,128)(2,1)} %bitcast.102, bf16[2048,2816]{1,0:T(8,128)(2,1)} %bitcast.100), kind=kOutput, calls=%fused_computation.2 | convolution fusion | flops 11814043648 | bytes 21495808 | tf_op jit(solution)/shard_map/dot_general | solution.py:27
  281.1 2.3 dynamic-slice_bitcast_fusion
  283.5 0.8 collective-permute-start.3
  284.3 1.4 collective-permute-start.4
  285.6 1.3 collective-permute-start.5
  288.3 6.2 convolution_convert_fusion.3.do_ref
  294.6 22.6 %attention_backward.1 = (bf16[256,2048]{1,0:T(8,128)(2,1)S(1)}, bf16[2,1024,256]{2,1,0:T(8,128)(2,1)S(1)}) custom-call(s32[10]{0:T(128)S(1)} %pad_add_fusion.table, bf16[256,2048]{1,0:T(8,128)(2,1)S(1)} %copy-done.12, bf16[256,2048]{1,0:T(8,128)(2,1)S(1)} %convolution_convert_fusion.3.do_ref, f32[256,2048]{1,0:T(8,128)S(1)} %copy-done.10, ...), custom_call_target="tpu_custom_call" | custom-call | flops 10737418240 | bytes 8388608 | tf_op jit(solution)/shard_map/attention_backward/pallas_call | solution.py:280
  317.2 1.0 copy-done.2
  318.2 1.0 copy-done.5
  319.2 28.5 %own_key_grads.1 = bf16[256,512]{1,0:T(8,128)(2,1)} custom-call(bf16[2,1024,256]{2,1,0:T(8,128)(2,1)} %copy-done.2, f32[256,128]{1,0:T(8,128)} %copy.46.refs_9_.cos_ref, f32[256,128]{1,0:T(8,128)} %copy.47.refs_10_.sin_ref), custom_call_target="tpu_custom_call" | custom-call | tf_op jit(solution)/shard_map/own_key_grads/pallas_call | solution.py:360
  347.7 1.4 collective-permute-done.4.refs_2_
  349.1 1.0 constant_dynamic-update-slice_fusion.1
  350.8 6.0 fusion.44
  356.9 2.8 fusion.9
  359.6 1.3 stack.21
  360.9 0.7 constant_dynamic-update-slice_fusion.3
  361.6 0.7 constant_dynamic-update-slice_fusion.2
  363.1 5.7 fusion.13
  370.7 3.5 collective-permute-done.6
  374.2 4.4 convolution_convert_fusion.2
  378.6 4.7 convolution_convert_fusion
  383.3 1.2 collective-permute-start.11
  384.5 0.8 collective-permute-start.12
  385.3 1.5 collective-permute-start.13
  386.8 21.3 %all-gather.2.cloned.1.call-done = bf16[704,2048]{1,0:T(8,128)(2,1)} async-done(((bf16[176,2048]{1,0:T(8,128)(2,1)}), bf16[704,2048]{1,0:T(8,128)(2,1)}) %all-gather.2.cloned.1.call-update) | async-done | bytes 2883600 | tf_op jit(solution)/shard_map/all_gather | solution.py:1445
  408.1 193.6 %finish.1 = (bf16[4,256,2816]{2,1,0:T(8,128)(2,1)}, bf16[256,2048]{1,0:T(8,128)(2,1)S(1)}, bf16[256,2560]{1,0:T(8,128)(2,1)S(1)}, bf16[16,512]{1,0:T(8,128)(2,1)S(1)}) custom-call(bf16[256,2816]{1,0:T(8,128)(2,1)S(1)} %get-tuple-element.129.refs_0_, bf16[256,2816]{1,0:T(8,128)(2,1)} %collective-permute-done.3.refs_1_, ...), custom_call_target="tpu_custom_call" | custom-call | flops 199999995904 | bytes 60000000 | tf_op jit(solution)/shard_map/finish/pallas_call | solution.py:1245
  601.7 1.6 convert_element_type.131
  603.3 1.6 slice.109
  604.8 1.0 copy-done.21
  605.8 3.3 convert_element_type.132
  609.2 8.1 %place_columns.1 = (f32[256,5632]{1,0:T(8,128)}, f32[256,5632]{1,0:T(8,128)}) custom-call(s32[4]{0:T(128)} %iota_xor_fusion.order, bf16[4,256,2816]{2,1,0:T(8,128)(2,1)} %get-tuple-element.145.both_ref), custom_call_target="tpu_custom_call" | custom-call | tf_op jit(solution)/shard_map/place_columns/pallas_call | solution.py:752
  617.8 0.8 fusion.39
  618.7 4.3 fusion.21
  (126 shorter events, 9.5 us)
Async XLA Ops:
  7.2 341.9 %reduce-scatter.2.cloned.1.call-start = ((), (), s32[]{:S(2)}) async-start(), calls=%async_computation.1 | async-start | bytes 3604480 | tf_op jit(solution)/shard_map/reduce_scatter | solution.py:1419
  11.6 112.7 %copy-start.19 = (bf16[1,256,2048]{2,1,0:T(8,128)(2,1)S(1)}, bf16[1,256,2048]{2,1,0:T(8,128)(2,1)}, u32[]{:S(2)}) copy-start(bf16[1,256,2048]{2,1,0:T(8,128)(2,1)} %param.25) | copy-start | bytes 3145732
  11.6 116.3 %copy-start.17 = (bf16[1,256,2048]{2,1,0:T(8,128)(2,1)S(1)}, bf16[1,256,2048]{2,1,0:T(8,128)(2,1)}, u32[]{:S(2)}) copy-start(bf16[1,256,2048]{2,1,0:T(8,128)(2,1)} %param.13) | copy-start | bytes 3145732
  11.6 117.4 %copy-start.34 = (s32[4,2]{0,1:T(2,128)S(1)}, s32[4,2]{0,1:T(2,128)}, u32[]{:S(2)}) copy-start(s32[4,2]{0,1:T(2,128)} %param.23) | copy-start | bytes 100
  124.3 35.3 %collective-permute-start = (bf16[256,2048]{1,0:T(8,128)(2,1)S(1)}, bf16[256,2048]{1,0:T(8,128)(2,1)}, u32[]{:S(2)}, u32[]{:S(2)}) collective-permute-start(bf16[256,2048]{1,0:T(8,128)(2,1)S(1)} %bitcast.76), channel_id=1, source_target_pairs={{0,2},{1,3},{2,0},{3,1},{4,6},{5,7},{6,4},{7,5},{8,10},{9,11},{10,... | collective-permute-start | bytes 3145736 | tf_op jit(solution)/shard_map/ppermute | solution.py:1270
  124.9 46.2 %collective-permute-start.1 = (bf16[256,2048]{1,0:T(8,128)(2,1)S(1)}, bf16[256,2048]{1,0:T(8,128)(2,1)}, u32[]{:S(2)}, u32[]{:S(2)}) collective-permute-start(bf16[256,2048]{1,0:T(8,128)(2,1)S(1)} %bitcast.77), channel_id=1, source_target_pairs={{0,4},{1,5},{2,6},{3,7},{4,0},{5,1},{6,2},{7,3},{8,12},{9,13},{10,... | collective-permute-start | bytes 3145736 | tf_op jit(solution)/shard_map/ppermute | solution.py:1270
  126.4 44.7 %collective-permute-start.2 = (bf16[256,2048]{1,0:T(8,128)(2,1)S(1)}, bf16[256,2048]{1,0:T(8,128)(2,1)}, u32[]{:S(2)}, u32[]{:S(2)}) collective-permute-start(bf16[256,2048]{1,0:T(8,128)(2,1)S(1)} %bitcast.78), channel_id=1, source_target_pairs={{0,6},{1,7},{2,4},{3,5},{4,2},{5,3},{6,0},{7,1},{8,14},{9,15},{10,... | collective-permute-start | bytes 3145736 | tf_op jit(solution)/shard_map/ppermute | solution.py:1270
  128.9 6.4 %copy-start.29 = (f32[1,8,256]{2,0,1:T(1,128)}, f32[1,8,256]{2,0,1:T(1,128)S(1)}, u32[]{:S(2)}) copy-start(f32[1,8,256]{2,0,1:T(1,128)S(1)} %get-tuple-element.184) | copy-start | bytes 24580
  129.0 6.4 %copy-start.31 = (f32[256]{0:T(256)}, f32[256]{0:T(256)S(1)}, u32[]{:S(2)}) copy-start(f32[256]{0:T(256)S(1)} %add_rsqrt_fusion.1) | copy-start | bytes 3076
  129.4 5.9 copy-start
  129.4 5.9 copy-start.1
  129.4 5.9 copy-start.7
  135.4 19.2 %copy-start.35 = (bf16[8,256,2048]{2,1,0:T(8,128)(2,1)S(1)}, bf16[8,256,2048]{2,1,0:T(8,128)(2,1)}, u32[]{:S(2)}) copy-start(bf16[8,256,2048]{2,1,0:T(8,128)(2,1)} %get-tuple-element.84) | copy-start | bytes 25165828
  154.5 2.5 copy-start.3
  154.5 2.5 copy-start.9
  154.6 2.5 copy-start.11
  262.9 145.1 %all-gather.2.cloned.1.call-start = ((), (), s32[]{:S(2)}) async-start(), calls=%async_computation.2 | async-start | bytes 3604480 | tf_op jit(solution)/shard_map/all_gather | solution.py:1445
  281.1 5.8 copy-start.14
  281.1 5.8 copy-start.16
  283.5 4.2 copy-start.20
  283.5 64.3 %collective-permute-start.3 = (bf16[256,2816]{1,0:T(8,128)(2,1)}, bf16[256,2816]{1,0:T(8,128)(2,1)}, u32[]{:S(2)}, u32[]{:S(2)}) collective-permute-start(bf16[256,2816]{1,0:T(8,128)(2,1)} %get-tuple-element.107), channel_id=1, source_target_pairs={{0,2},{1,3},{2,0},{3,1},{4,6},{5,7},{6,4},{7,5},{8,10},{9,11},{10,... | collective-permute-start | bytes 4325384 | tf_op jit(solution)/shard_map/ppermute | solution.py:1270
  284.3 64.8 %collective-permute-start.4 = (bf16[256,2816]{1,0:T(8,128)(2,1)}, bf16[256,2816]{1,0:T(8,128)(2,1)}, u32[]{:S(2)}, u32[]{:S(2)}) collective-permute-start(bf16[256,2816]{1,0:T(8,128)(2,1)} %get-tuple-element.108), channel_id=1, source_target_pairs={{0,4},{1,5},{2,6},{3,7},{4,0},{5,1},{6,2},{7,3},{8,12},{9,13},{10,... | collective-permute-start | bytes 4325384 | tf_op jit(solution)/shard_map/ppermute | solution.py:1270
  285.6 63.4 %collective-permute-start.5 = (bf16[256,2816]{1,0:T(8,128)(2,1)}, bf16[256,2816]{1,0:T(8,128)(2,1)}, u32[]{:S(2)}, u32[]{:S(2)}) collective-permute-start(bf16[256,2816]{1,0:T(8,128)(2,1)} %get-tuple-element.109), channel_id=1, source_target_pairs={{0,6},{1,7},{2,4},{3,5},{4,2},{5,3},{6,0},{7,1},{8,14},{9,15},{10,... | collective-permute-start | bytes 4325384 | tf_op jit(solution)/shard_map/ppermute | solution.py:1270
  288.3 6.2 copy-start.26
  288.3 6.2 copy-start.8
  288.3 6.2 copy-start.10
  288.3 6.2 copy-start.12
  319.2 29.9 %copy-start.6 = (bf16[256,2048]{1,0:T(8,128)(2,1)S(1)}, bf16[256,2048]{1,0:T(8,128)(2,1)}, u32[]{:S(2)}) copy-start(bf16[256,2048]{1,0:T(8,128)(2,1)} %copy-done.5) | copy-start | bytes 3145732
  350.8 6.0 copy-start.18
  350.8 6.1 copy-start.22
  350.8 6.1 copy-start.24
  350.8 6.1 copy-start.30
  350.8 6.1 copy-start.32
  356.9 6.3 copy-start.15
  362.4 8.3 %collective-permute-start.10 = (f32[2,4,256]{2,1,0:T(4,128)S(1)}, f32[2,4,256]{2,1,0:T(4,128)S(1)}, u32[]{:S(2)}, u32[]{:S(2)}) collective-permute-start(f32[2,4,256]{2,1,0:T(4,128)S(1)} %bitcast.90), channel_id=1, source_target_pairs={{0,1},{1,0},{2,3},{3,2},{4,5},{5,4},{6,7},{7,6},{8,9},{9,8},{10,11... | collective-permute-start | bytes 24584 | tf_op jit(solution)/shard_map/ppermute | solution.py:1270
  363.1 5.7 copy-start.27
  363.1 6.2 copy-start.23
  363.1 6.2 copy-start.28
  363.1 6.3 copy-start.4
  368.8 5.4 collective-permute-start.7
  369.3 9.3 %collective-permute-start.9 = (bf16[256,2560]{1,0:T(8,128)(2,1)S(1)}, bf16[256,2560]{1,0:T(8,128)(2,1)S(1)}, u32[]{:S(2)}, u32[]{:S(2)}) collective-permute-start(bf16[256,2560]{1,0:T(8,128)(2,1)S(1)} %constant_dynamic-update-slice_fusion), channel_id=1, source_target_pairs={{0,1},{1,0},{2,3},{3,2},{4,5},{5,4},{6,7},{7,6},{8,9},{9,8},{10,11... | collective-permute-start | bytes 3932168 | tf_op jit(solution)/shard_map/ppermute | solution.py:1270
  369.7 4.5 collective-permute-start.6
  370.6 8.1 %collective-permute-start.8 = (bf16[256,1024]{1,0:T(8,128)(2,1)S(1)}, bf16[256,1024]{1,0:T(8,128)(2,1)S(1)}, u32[]{:S(2)}, u32[]{:S(2)}) collective-permute-start(bf16[256,1024]{1,0:T(8,128)(2,1)S(1)} %get-tuple-element.162), channel_id=1, source_target_pairs={{0,1},{1,0},{2,3},{3,2},{4,5},{5,4},{6,7},{7,6},{8,9},{9,8},{10,11... | collective-permute-start | bytes 1572872 | tf_op jit(solution)/shard_map/ppermute | solution.py:1270
  383.3 235.4 %collective-permute-start.11 = (bf16[256,2048]{1,0:T(8,128)(2,1)}, bf16[256,2048]{1,0:T(8,128)(2,1)}, u32[]{:S(2)}, u32[]{:S(2)}) collective-permute-start(bf16[256,2048]{1,0:T(8,128)(2,1)} %get-tuple-element.139), channel_id=1, source_target_pairs={{0,2},{1,3},{2,0},{3,1},{4,6},{5,7},{6,4},{7,5},{8,10},{9,11},{10,... | collective-permute-start | bytes 3145736 | tf_op jit(solution)/shard_map/ppermute | solution.py:1270
  384.5 234.1 %collective-permute-start.12 = (bf16[256,2048]{1,0:T(8,128)(2,1)}, bf16[256,2048]{1,0:T(8,128)(2,1)}, u32[]{:S(2)}, u32[]{:S(2)}) collective-permute-start(bf16[256,2048]{1,0:T(8,128)(2,1)} %get-tuple-element.140), channel_id=1, source_target_pairs={{0,4},{1,5},{2,6},{3,7},{4,0},{5,1},{6,2},{7,3},{8,12},{9,13},{10,... | collective-permute-start | bytes 3145736 | tf_op jit(solution)/shard_map/ppermute | solution.py:1270
  385.3 233.3 %collective-permute-start.13 = (bf16[256,2048]{1,0:T(8,128)(2,1)}, bf16[256,2048]{1,0:T(8,128)(2,1)}, u32[]{:S(2)}, u32[]{:S(2)}) collective-permute-start(bf16[256,2048]{1,0:T(8,128)(2,1)} %get-tuple-element.141), channel_id=1, source_target_pairs={{0,6},{1,7},{2,4},{3,5},{4,2},{5,3},{6,0},{7,1},{8,14},{9,15},{10,... | collective-permute-start | bytes 3145736 | tf_op jit(solution)/shard_map/ppermute | solution.py:1270
  603.3 2.6 copy-start.21
  609.2 9.5 %copy-start.25 = (bf16[256,2048]{1,0:T(8,128)(2,1)S(1)}, bf16[256,2048]{1,0:T(8,128)(2,1)}, u32[]{:S(2)}) copy-start(bf16[256,2048]{1,0:T(8,128)(2,1)} %get-tuple-element.138) | copy-start | bytes 3145732
  (4 other events, 3.9 us)
Sparse Core Ops, SparseCore 0:
  263.1 55.9 reduce-scatter.1
  349.2 58.8 all-gather.1
